TPU v7x, 32 devices: a whole 2x2x4 slice. The times are simulated.
32 devices in a mesh: dp: 4 (over x, core), seq: 2 (over y), mp: 4 (over z).
Axes of the slice: x: 2, y: 2, z: 4, core: 2. Of those that a mesh axis runs over, the one named last changes fastest.
Arguments:
- inputs: float32 [4, 1024, 1024], P('dp', 'seq'), may hold values from -6 to 6
- receptance_key_value_weight: bfloat16 [3, 1024, 1024], P(None, ('dp', 'seq'), 'mp'), may hold values from -0.1875 to 0.1875
- output_weight: bfloat16 [1024, 1024], P('mp', ('dp', 'seq')), may hold values from -0.375 to 0.375
- lowrank_first_factors: bfloat16 [2, 1024, 64], P(None, ('dp', 'seq')), may hold values from -0.1875 to 0.1875
- lowrank_second_factors: bfloat16 [2, 64, 1024], P(None, ('dp', 'seq'), 'mp'), may hold values from -0.75 to 0.75
- gate_first_factor: bfloat16 [1024, 128], P(('dp', 'seq')), may hold values from -0.1875 to 0.1875
- gate_second_factor: bfloat16 [128, 1024], P(('dp', 'seq'), 'mp'), may hold values from -0.5 to 0.5
- channel_key_weight: bfloat16 [1024, 4096], P(('dp', 'seq'), 'mp'), may hold values from -0.1875 to 0.1875
- channel_value_weight: bfloat16 [4096, 1024], P('mp', ('dp', 'seq')), may hold values from -0.09375 to 0.09375
- head_table: bfloat16 [7, 16, 64], P(None, 'mp', ('dp', 'seq')), may hold values from -8.5 to 1.5, as said below
- feature_table: bfloat16 [11, 1024], P(None, ('dp', 'seq')), may hold values from -0.5 to 1.5, as said below
- cotangent: float32 [4, 1024, 1024], P('dp', 'seq'), may hold values from -6 to 6
Outputs:
- block_out: float32 [4, 1024, 1024], P('dp', ('seq', 'mp'))
- input_grad: float32 [4, 1024, 1024], P('dp', ('seq', 'mp'))
- receptance_key_value_gradient: float32 [3, 1024, 1024], P(None, ('dp', 'seq'), 'mp')
- output_weight_gradient: float32 [1024, 1024], P('mp', ('dp', 'seq'))
- lowrank_first_gradient: float32 [2, 1024, 64], P(None, ('dp', 'seq'))
- lowrank_second_gradient: float32 [2, 64, 1024], P(None, ('dp', 'seq'), 'mp')
- gate_first_gradient: float32 [1024, 128], P(('dp', 'seq'))
- gate_second_gradient: float32 [128, 1024], P(('dp', 'seq'), 'mp')
- ffn_key_grad: float32 [1024, 4096], P(('dp', 'seq'), 'mp')
- ffn_value_grad: float32 [4096, 1024], P('mp', ('dp', 'seq'))
- head_table_gradient: float32 [7, 16, 64], P(None, 'mp', ('dp', 'seq'))
- feature_table_gradient: float32 [11, 1024], P(None, ('dp', 'seq'))
Inputs may be any that keep to these rules, and one draw needn't show every extreme that they name: `head_table`: Rows: decay base, rate base, key normalization scale, key rate scale, bonus, group norm gain, group norm bias; the decay base lies in -8.5 to -1. `feature_table`: rows 0 and 2 are gains of 0.5 to 1.5, rows 1 and 3 biases of -0.5 to 0.5, rows 4 to 10 token-shift weights of 0.05 to 0.95.
All inputs are finite; a program needn't handle non-finite values.
Results may differ from a plain program's by a relative error of at most 0.02.
Values may be sent and summed in bfloat16 or wider, within the bound.
No kernel may reach another device: no remote copies, remote signals or barrier semaphores. Data moves between devices by JAX's collectives and lax.ppermute only.
A program may use at most 128 MiB of HBM per device.

v0:
```python
import jax
import jax.numpy as jnp
from jax import lax
from jax.sharding import PartitionSpec as P

ATTENTION_SPAN = 64
BLOCK = 64


precise = lax.Precision.HIGHEST


def from_behind(x, axis, by):
    devices = lax.axis_size(axis)
    pairs = [(i, i + by) for i in range(devices) if 0 <= i + by < devices]
    return lax.ppermute(x, axis, pairs)


def matrix_product(former, latter):
    return jnp.dot(former, latter, preferred_element_type=jnp.float32)


def matrix_product_transposed_right(former, latter):
    return lax.dot_general(
        former, latter, (((1,), (1,)), ((), ())), preferred_element_type=jnp.float32
    )


def matrix_product_transposed_left(former, latter):
    return lax.dot_general(
        former, latter, (((0,), (0,)), ((), ())), preferred_element_type=jnp.float32
    )


def norm_rows(values, multiplier_entries, offset):
    center = values - jnp.mean(values, axis=-1, keepdims=True)
    spread = jnp.mean(center * center, axis=-1, keepdims=True)
    return center * lax.rsqrt(spread + 1e-05) * multiplier_entries + offset


def token_edge(row_here, offset_by):
    return from_behind(row_here, ("seq", "mp"), offset_by)


def shift_later(values, offset_by):
    return jnp.concatenate([token_edge(values[-1:], offset_by), values[:-1]], axis=0)


def shift_earlier(values, offset_by):
    return jnp.concatenate([values[1:], token_edge(values[:1], -offset_by)], axis=0)


def prepare(acceptor_lines, key_proj, payload_mapped, decay_input, rate_input, head_rows):
    overall_line_count = key_proj.shape[0]
    log_decay = -jnp.exp(-jax.nn.softplus(-(head_rows[0] + decay_input)) - 0.5)
    context_rate = jax.nn.sigmoid(head_rows[1] + rate_input)
    scaled = (key_proj * head_rows[2]).reshape(overall_line_count, -1, ATTENTION_SPAN)
    unit_key = (
        scaled * lax.rsqrt(jnp.sum(scaled * scaled, axis=-1, keepdims=True) + 1e-06)
    ).reshape(overall_line_count, -1)
    corrected_lookup = key_proj * (1.0 + (context_rate - 1.0) * head_rows[3])
    removal = unit_key * context_rate
    return (acceptor_lines, log_decay, corrected_lookup, payload_mapped, unit_key, removal)


def finish(
    read_out, acceptor_lines, corrected_lookup, payload_mapped, valve_sigmoided, standardized_lines
):
    overall_line_count = read_out.shape[0]
    grouped = read_out.reshape(overall_line_count, -1, ATTENTION_SPAN)
    center = grouped - jnp.mean(grouped, axis=-1, keepdims=True)
    spread = jnp.mean(center * center, axis=-1, keepdims=True)
    standardized_source = (center * lax.rsqrt(spread + 0.00064)).reshape(
        overall_line_count, -1
    ) * standardized_lines[1] + standardized_lines[2]
    extra_term_sum = jnp.sum(
        (acceptor_lines * corrected_lookup * standardized_lines[0]).reshape(
            overall_line_count, -1, ATTENTION_SPAN
        ),
        axis=-1,
        keepdims=True,
    )
    extra_term_share = (
        extra_term_sum * payload_mapped.reshape(overall_line_count, -1, ATTENTION_SPAN)
    ).reshape(overall_line_count, -1)
    return (standardized_source + extra_term_share) * valve_sigmoided


def to_blocks(values, heads_here):
    overall_line_count = values.shape[0]
    return values.reshape(overall_line_count // BLOCK, BLOCK, heads_here, ATTENTION_SPAN).transpose(
        0, 2, 1, 3
    )


def from_blocks(blocked):
    return blocked.transpose(0, 2, 1, 3).reshape(blocked.shape[0] * blocked.shape[2], -1)


def pair_product(former, latter):
    return jnp.einsum("htj,hsj->hts", former, latter, precision=precise)


def block_parts(acceptor_lines, log_decay, corrected_lookup, payload_mapped, unit_key, removal):
    length_here = acceptor_lines.shape[1]
    width_here = acceptor_lines.shape[2]
    inclusive = jnp.cumsum(log_decay, axis=1)
    exclusive = jnp.concatenate([jnp.zeros_like(inclusive[:, :1]), inclusive[:, :-1]], axis=1)
    growth = jnp.exp(-inclusive)
    key_scaled = corrected_lookup * growth
    removal_scaled = removal * growth
    query_unit = unit_key * jnp.exp(exclusive)
    query_read = acceptor_lines * jnp.exp(inclusive)
    positions = jnp.arange(length_here)
    strict = (positions[:, None] > positions[None, :]).astype(inclusive.dtype)
    inclusive_mask = (positions[:, None] >= positions[None, :]).astype(inclusive.dtype)
    key_mix = pair_product(query_unit, key_scaled) * strict
    removal_mix = pair_product(query_unit, removal_scaled) * strict
    read_key = pair_product(query_read, key_scaled) * inclusive_mask
    read_removal = pair_product(query_read, removal_scaled) * inclusive_mask
    system = removal_mix + jnp.eye(length_here, dtype=inclusive.dtype)
    start_map = lax.linalg.triangular_solve(
        system, query_unit, left_side=True, lower=True, unit_diagonal=True
    )
    pushed = jnp.einsum("hts,hsi->hti", key_mix, payload_mapped, precision=precise)
    local_push = lax.linalg.triangular_solve(
        system, pushed, left_side=True, lower=True, unit_diagonal=True
    )
    local_out = jnp.einsum(
        "hts,hsi->hti", read_key, payload_mapped, precision=precise
    ) - jnp.einsum("hts,hsi->hti", read_removal, local_push, precision=precise)
    state_read = query_read - jnp.einsum("hts,hsj->htj", read_removal, start_map, precision=precise)
    tail_decay = jnp.exp(inclusive[:, -1:, :] - inclusive)
    key_tail = corrected_lookup * tail_decay
    removal_tail = removal * tail_decay
    eye_here = jnp.eye(width_here, dtype=inclusive.dtype)
    carry_map = jnp.exp(inclusive[:, -1, :])[:, :, None] * eye_here - jnp.einsum(
        "htj,htl->hjl", start_map, removal_tail, precision=precise
    )
    carry_add = jnp.einsum(
        "hti,htj->hij", payload_mapped, key_tail, precision=precise
    ) - jnp.einsum("hti,htj->hij", local_push, removal_tail, precision=precise)
    return (local_out, state_read, carry_map, carry_add)


def block_step(state_now, inputs_here):
    local_out, state_read, carry_map, carry_add = block_parts(*inputs_here)
    read_out = local_out + jnp.einsum("htj,hij->hti", state_read, state_now, precision=precise)
    next_state = jnp.einsum("hij,hjl->hil", state_now, carry_map, precision=precise) + carry_add
    return (read_out, next_state)


def compose(earlier, later):
    return (
        jnp.einsum("hjk,hkl->hjl", earlier[0], later[0], precision=precise),
        jnp.einsum("hik,hkl->hil", earlier[1], later[0], precision=precise) + later[1],
    )


def identity_map(like_state):
    heads_here = like_state.shape[0]
    width_here = like_state.shape[2]
    eye_here = jnp.broadcast_to(
        jnp.eye(width_here, dtype=jnp.float32), (heads_here, width_here, width_here)
    )
    return (eye_here, jnp.zeros_like(like_state))


def carry_chain(affine, reverse):
    direction = -1 if reverse else 1

    def advance(counter, state_now):
        passed = jnp.einsum("hik,hkl->hil", state_now, affine[0], precision=precise) + affine[1]
        return from_behind(passed.astype(jnp.bfloat16), "seq", direction).astype(passed.dtype)

    return lax.fori_loop(0, lax.axis_size("seq") - 1, advance, jnp.zeros_like(affine[1]))


def core_forward(blocked):
    local_out, state_read, carry_map, carry_add = lax.map(
        lambda members: block_parts(*members), blocked
    )

    def gather_prefix(carried, affine_here):
        return (compose(carried, affine_here), carried)

    device_map, before = lax.scan(gather_prefix, identity_map(carry_add[0]), (carry_map, carry_add))
    incoming = carry_chain(device_map, False)
    states = jnp.einsum("hij,bhjl->bhil", incoming, before[0], precision=precise) + before[1]
    read_blocks = local_out + jnp.einsum("bhtj,bhij->bhti", state_read, states, precision=precise)
    return (read_blocks, states, state_read, carry_map)


def core_backward(blocked, d_read, states, state_read, carry_map):
    read_terms = jnp.einsum("bhti,bhtj->bhij", d_read, state_read, precision=precise)
    flipped = jnp.swapaxes(carry_map, -1, -2)

    def gather_suffix(carried, affine_here):
        return (compose(carried, affine_here), carried)

    device_map, after_maps = lax.scan(
        gather_suffix, identity_map(read_terms[0]), (flipped, read_terms), reverse=True
    )
    outgoing = carry_chain(device_map, True)
    next_grads = (
        jnp.einsum("hij,bhjl->bhil", outgoing, after_maps[0], precision=precise) + after_maps[1]
    )

    def block_grad(members):
        state_here, grad_here, cot_here, inputs_here = members
        result_pair, pull_back = jax.vjp(block_step, state_here, inputs_here)
        return pull_back((cot_here, grad_here))[1]

    return lax.map(block_grad, (states, next_grads, d_read, blocked))


def body(
    inputs,
    receptance_key_value_weight,
    output_weight,
    lowrank_first_factors,
    lowrank_second_factors,
    gate_first_factor,
    gate_second_factor,
    channel_key_weight,
    channel_value_weight,
    head_table,
    feature_table,
    cotangent,
):
    (
        rkv_full,
        out_full,
        down_full,
        up_full,
        gate_down_full,
        gate_up_full,
        key_full,
        value_full,
        head_full,
        norm_full,
    ) = (
        lax.all_gather(receptance_key_value_weight, ("dp", "seq"), axis=1, tiled=True),
        lax.all_gather(output_weight, ("dp", "seq"), axis=1, tiled=True),
        lax.all_gather(lowrank_first_factors, ("dp", "seq"), axis=1, tiled=True),
        lax.all_gather(lowrank_second_factors, ("dp", "seq"), axis=1, tiled=True),
        lax.all_gather(gate_first_factor, ("dp", "seq"), axis=0, tiled=True),
        lax.all_gather(gate_second_factor, ("dp", "seq"), axis=0, tiled=True),
        lax.all_gather(channel_key_weight, ("dp", "seq"), axis=0, tiled=True),
        lax.all_gather(channel_value_weight, ("dp", "seq"), axis=1, tiled=True),
        lax.all_gather(head_table, ("dp", "seq"), axis=2, tiled=True),
        lax.all_gather(feature_table, ("dp", "seq"), axis=1, tiled=True),
    )
    residual_stream = inputs[0]
    cotangent_whole = cotangent[0]
    heads_here = head_full.shape[1]
    mp_count = lax.axis_size("mp")
    share_rows = residual_stream.shape[0] // mp_count
    share_start = lax.axis_index("mp") * share_rows
    norms = norm_full.astype(jnp.float32)
    head_rows = head_full.astype(jnp.float32).reshape(head_full.shape[0], -1)
    first_norm, first_pull = jax.vjp(norm_rows, residual_stream, norms[0], norms[1])
    first_diff = shift_later(first_norm, mp_count) - first_norm
    mixed_inputs = [
        (first_norm + first_diff * norms[4 + slot_index]).astype(jnp.bfloat16)
        for slot_index in range(6)
    ]
    acceptor_lines = matrix_product(mixed_inputs[0], rkv_full[0])
    key_proj = matrix_product(mixed_inputs[2], rkv_full[1])
    payload_mapped = matrix_product(mixed_inputs[3], rkv_full[2])
    decay_latent = jnp.tanh(matrix_product(mixed_inputs[1], down_full[0]))
    decay_lowrank = decay_latent.astype(jnp.bfloat16)
    decay_input = matrix_product(decay_lowrank, up_full[0])
    rate_lowrank = matrix_product(mixed_inputs[4], down_full[1]).astype(jnp.bfloat16)
    rate_input = matrix_product(rate_lowrank, up_full[1])
    gate_lat = jax.nn.sigmoid(matrix_product(mixed_inputs[5], gate_down_full))
    gate_low = gate_lat.astype(jnp.bfloat16)
    valve_sigmoided = matrix_product(gate_low, gate_up_full)
    prepared, prep_pull = jax.vjp(
        prepare, acceptor_lines, key_proj, payload_mapped, decay_input, rate_input, head_rows[:4]
    )
    blocked = tuple((to_blocks(member, heads_here) for member in prepared))
    read_blocks, states, state_read, carry_map = core_forward(blocked)
    read_out = from_blocks(read_blocks)
    gated, post_pull = jax.vjp(
        finish, read_out, prepared[0], prepared[2], prepared[3], valve_sigmoided, head_rows[4:]
    )
    gated_low = gated.astype(jnp.bfloat16)
    middle = lax.dynamic_slice_in_dim(
        residual_stream, share_start, share_rows, 0
    ) + lax.psum_scatter(
        matrix_product(gated_low, out_full).astype(jnp.bfloat16),
        "mp",
        scatter_dimension=0,
        tiled=True,
    ).astype(
        jnp.float32
    )
    second_norm, second_pull = jax.vjp(norm_rows, middle, norms[2], norms[3])
    second_diff = shift_later(second_norm, 1) - second_norm
    ffn_share_in = (second_norm + second_diff * norms[10]).astype(jnp.bfloat16)
    ffn_in = lax.all_gather(ffn_share_in, "mp", axis=0, tiled=True)
    pre_act = matrix_product(ffn_in, key_full)
    hidden = jnp.square(jnp.maximum(pre_act, 0.0)).astype(jnp.bfloat16)
    block_out = middle + lax.psum_scatter(
        matrix_product(hidden, value_full).astype(jnp.bfloat16),
        "mp",
        scatter_dimension=0,
        tiled=True,
    ).astype(jnp.float32)
    cot_low = cotangent_whole.astype(jnp.bfloat16)
    d_pre = (
        matrix_product_transposed_right(cot_low, value_full) * 2.0 * jnp.maximum(pre_act, 0.0)
    ).astype(jnp.bfloat16)
    value_gradient = matrix_product_transposed_left(hidden, cot_low)
    key_gradient = matrix_product_transposed_left(ffn_in, d_pre)
    d_ffn_in = lax.psum_scatter(
        matrix_product_transposed_right(d_pre, key_full).astype(jnp.bfloat16),
        "mp",
        scatter_dimension=0,
        tiled=True,
    ).astype(jnp.float32)
    d_second = d_ffn_in * (1.0 - norms[10]) + shift_earlier(d_ffn_in * norms[10], 1)
    mu_ffn_part = jnp.sum(d_ffn_in * second_diff, axis=0)
    d_middle_ln, gain_two_part, bias_two_part = second_pull(d_second)
    d_middle = lax.dynamic_slice_in_dim(cotangent_whole, share_start, share_rows, 0) + d_middle_ln
    d_mid_low = lax.all_gather(d_middle.astype(jnp.bfloat16), "mp", axis=0, tiled=True)
    output_weight_gradient = matrix_product_transposed_left(gated_low, d_mid_low)
    d_gated = matrix_product_transposed_right(d_mid_low, out_full)
    d_read, d_recept_post, d_newkey_post, d_value_post, d_gate, post_grad = post_pull(d_gated)
    core_grads = core_backward(
        blocked, to_blocks(d_read, heads_here), states, state_read, carry_map
    )
    core_flat = [from_blocks(member) for member in core_grads]
    d_prepared = (
        core_flat[0] + d_recept_post,
        core_flat[1],
        core_flat[2] + d_newkey_post,
        core_flat[3] + d_value_post,
        core_flat[4],
        core_flat[5],
    )
    d_recept, d_key, d_value, d_decay, d_rate, pre_grad = prep_pull(d_prepared)
    receptance_lowrank_gradient = d_recept.astype(jnp.bfloat16)
    key_lowrank_gradient = d_key.astype(jnp.bfloat16)
    value_lowrank_gradient = d_value.astype(jnp.bfloat16)
    decay_lowrank_gradient = d_decay.astype(jnp.bfloat16)
    rate_lowrank_gradient = d_rate.astype(jnp.bfloat16)
    d_gate_low = d_gate.astype(jnp.bfloat16)
    receptance_key_value_gradient = jnp.stack(
        [
            matrix_product_transposed_left(mixed_inputs[0], receptance_lowrank_gradient),
            matrix_product_transposed_left(mixed_inputs[2], key_lowrank_gradient),
            matrix_product_transposed_left(mixed_inputs[3], value_lowrank_gradient),
        ]
    )
    lowrank_second_gradient = jnp.stack(
        [
            matrix_product_transposed_left(decay_lowrank, decay_lowrank_gradient),
            matrix_product_transposed_left(rate_lowrank, rate_lowrank_gradient),
        ]
    )
    gate_second_gradient = matrix_product_transposed_left(gate_low, d_gate_low)
    second_rows_part = jnp.stack([gain_two_part, bias_two_part, mu_ffn_part])
    decay_latent_gradient, rate_latent_gradient, d_gate_lat, second_rows = (
        lax.psum(
            matrix_product_transposed_right(decay_lowrank_gradient, up_full[0]).astype(
                jnp.bfloat16
            ),
            "mp",
        ).astype(jnp.float32),
        lax.psum(
            matrix_product_transposed_right(rate_lowrank_gradient, up_full[1]).astype(jnp.bfloat16),
            "mp",
        ).astype(jnp.float32),
        lax.psum(
            matrix_product_transposed_right(d_gate_low, gate_up_full).astype(jnp.bfloat16), "mp"
        ).astype(jnp.float32),
        lax.psum(second_rows_part.astype(jnp.bfloat16), "mp").astype(jnp.float32),
    )
    decay_preactivation = (decay_latent_gradient * (1.0 - decay_latent * decay_latent)).astype(
        jnp.bfloat16
    )
    rate_preactivation = rate_latent_gradient.astype(jnp.bfloat16)
    gate_preactivation = (d_gate_lat * gate_lat * (1.0 - gate_lat)).astype(jnp.bfloat16)
    lowrank_first_gradient = jnp.stack(
        [
            matrix_product_transposed_left(mixed_inputs[1], decay_preactivation),
            matrix_product_transposed_left(mixed_inputs[4], rate_preactivation),
        ]
    )
    gate_first_gradient = matrix_product_transposed_left(mixed_inputs[5], gate_preactivation)
    keep_share = (lax.axis_index("mp") == 0).astype(jnp.float32)
    mixed_inputs_gradient = [
        matrix_product_transposed_right(receptance_lowrank_gradient, rkv_full[0]),
        matrix_product_transposed_right(decay_preactivation, down_full[0]) * keep_share,
        matrix_product_transposed_right(key_lowrank_gradient, rkv_full[1]),
        matrix_product_transposed_right(value_lowrank_gradient, rkv_full[2]),
        matrix_product_transposed_right(rate_preactivation, down_full[1]) * keep_share,
        matrix_product_transposed_right(gate_preactivation, gate_down_full) * keep_share,
    ]
    shifted_sum = sum(
        (mixed_inputs_gradient[slot_index] * norms[4 + slot_index] for slot_index in range(6))
    )
    direct_sum = sum(
        (
            mixed_inputs_gradient[slot_index] * (1.0 - norms[4 + slot_index])
            for slot_index in range(6)
        )
    )
    first_part = direct_sum + shift_earlier(shifted_sum, mp_count)
    mu_part = jnp.stack(
        [jnp.sum(mixed_inputs_gradient[slot_index] * first_diff, axis=0) for slot_index in range(6)]
    )
    d_first, mu_grads = (
        lax.psum(first_part.astype(jnp.bfloat16), "mp").astype(jnp.float32),
        lax.psum(mu_part.astype(jnp.bfloat16), "mp").astype(jnp.float32),
    )
    d_input_ln, gain_one_grad, bias_one_grad = first_pull(d_first)
    input_grad = d_middle + lax.dynamic_slice_in_dim(d_input_ln, share_start, share_rows, 0)
    feature_table_gradient = jnp.concatenate(
        [
            jnp.stack([gain_one_grad, bias_one_grad, second_rows[0], second_rows[1]]),
            mu_grads,
            second_rows[2:3],
        ],
        axis=0,
    )
    head_table_gradient = jnp.concatenate([pre_grad, post_grad], axis=0).reshape(head_full.shape)
    (
        rkv_out,
        out_out,
        down_out,
        up_out,
        gate_down_out,
        gate_up_out,
        key_out,
        value_out,
        head_out,
        norm_out,
    ) = (
        lax.psum_scatter(
            receptance_key_value_gradient.astype(jnp.bfloat16),
            ("dp", "seq"),
            scatter_dimension=1,
            tiled=True,
        ).astype(jnp.float32),
        lax.psum_scatter(
            output_weight_gradient.astype(jnp.bfloat16),
            ("dp", "seq"),
            scatter_dimension=1,
            tiled=True,
        ).astype(jnp.float32),
        lax.psum_scatter(
            lowrank_first_gradient.astype(jnp.bfloat16),
            ("dp", "seq"),
            scatter_dimension=1,
            tiled=True,
        ).astype(jnp.float32),
        lax.psum_scatter(
            lowrank_second_gradient.astype(jnp.bfloat16),
            ("dp", "seq"),
            scatter_dimension=1,
            tiled=True,
        ).astype(jnp.float32),
        lax.psum_scatter(
            gate_first_gradient.astype(jnp.bfloat16), ("dp", "seq"), scatter_dimension=0, tiled=True
        ).astype(jnp.float32),
        lax.psum_scatter(
            gate_second_gradient.astype(jnp.bfloat16),
            ("dp", "seq"),
            scatter_dimension=0,
            tiled=True,
        ).astype(jnp.float32),
        lax.psum_scatter(
            key_gradient.astype(jnp.bfloat16), ("dp", "seq"), scatter_dimension=0, tiled=True
        ).astype(jnp.float32),
        lax.psum_scatter(
            value_gradient.astype(jnp.bfloat16), ("dp", "seq"), scatter_dimension=1, tiled=True
        ).astype(jnp.float32),
        lax.psum_scatter(
            head_table_gradient.astype(jnp.bfloat16), ("dp", "seq"), scatter_dimension=2, tiled=True
        ).astype(jnp.float32),
        lax.psum_scatter(
            feature_table_gradient.astype(jnp.bfloat16),
            ("dp", "seq"),
            scatter_dimension=1,
            tiled=True,
        ).astype(jnp.float32),
    )
    return (
        block_out[None],
        input_grad[None],
        rkv_out,
        out_out,
        down_out,
        up_out,
        gate_down_out,
        gate_up_out,
        key_out,
        value_out,
        head_out,
        norm_out,
    )


def solution(mesh):
    return jax.shard_map(
        body,
        mesh=mesh,
        in_specs=(
            P("dp", "seq", None),
            P(None, ("dp", "seq"), "mp"),
            P("mp", ("dp", "seq")),
            P(None, ("dp", "seq"), None),
            P(None, ("dp", "seq"), "mp"),
            P(("dp", "seq"), None),
            P(("dp", "seq"), "mp"),
            P(("dp", "seq"), "mp"),
            P("mp", ("dp", "seq")),
            P(None, "mp", ("dp", "seq")),
            P(None, ("dp", "seq")),
            P("dp", "seq", None),
        ),
        out_specs=(
            P("dp", ("seq", "mp"), None),
            P("dp", ("seq", "mp"), None),
            P(None, ("dp", "seq"), "mp"),
            P("mp", ("dp", "seq")),
            P(None, ("dp", "seq"), None),
            P(None, ("dp", "seq"), "mp"),
            P(("dp", "seq"), None),
            P(("dp", "seq"), "mp"),
            P(("dp", "seq"), "mp"),
            P("mp", ("dp", "seq")),
            P(None, "mp", ("dp", "seq")),
            P(None, ("dp", "seq")),
        ),
        check_vma=False,
    )
```

profile of v0, /device:TPU:0, one launch (start us, length us, event | category | flops | bytes accessed | tf_op | source)
XLA Modules:
  0.0 1820.9 jit_solution(5440025024486159983)
XLA Ops:
  8.0 17.5 all_gather.36
  35.6 15.5 all_gather.38
  51.1 14.3 all_gather.40
  65.3 16.6 all_gather.39
  81.9 16.2 all_gather.41
  98.8 19.1 %all_gather.43 = bf16[256,1024]{1,0:T(8,128)(2,1)} all-gather(bf16[256,128]{1,0:T(8,128)(2,1)S(1)} %copy-done.98), channel_id=1, replica_groups=mesh['dp'=4,'seq'=2,'mp'=4] {'dp','seq'}, dimensions={1}, use_global_device_ids=true | all-gather | bytes 589824 | tf_op jit(solution)/shard_map/all_gather | solution.py:244
  120.7 17.9 all_gather.42
  199.9 310.3 %while.82 = (s32[]{:T(128)}, f32[8,4,64,64]{2,3,1,0:T(8,128)}, f32[8,4,64,64]{3,2,1,0:T(8,128)}, f32[8,4,64,64]{3,2,1,0:T(8,128)}, f32[8,4,64,64]{3,2,1,0:T(8,12...) while((s32[]{:T(128)}, f32[8,4,64,64]{2,3,1,0:T(8,128)}, ...), condition=%wide.region_5.7_spmd, body=%wide.region_3.6_spmd.sunk | while | flops 165171264 | bytes 5872773 | solution.py:180
  203.3 20.4 %custom-call.25 = f32[4,1,64,64]{2,3,1,0:T(8,128)S(1)} custom-call(f32[4,1,64,64]{3,2,1,0:T(8,128)} %fusion.511), custom_call_target="InvertDiagBlocksLowerTriangular" | custom-call | tf_op jit(solution)/shard_map/while/body/eval_jaxpr/triangular_solve/custom-call.1 | solution.py:126
  242.1 20.4 %custom-call.25 = f32[4,1,64,64]{2,3,1,0:T(8,128)S(1)} custom-call(f32[4,1,64,64]{3,2,1,0:T(8,128)} %fusion.511), custom_call_target="InvertDiagBlocksLowerTriangular" | custom-call | tf_op jit(solution)/shard_map/while/body/eval_jaxpr/triangular_solve/custom-call.1 | solution.py:126
  280.8 20.4 %custom-call.25 = f32[4,1,64,64]{2,3,1,0:T(8,128)S(1)} custom-call(f32[4,1,64,64]{3,2,1,0:T(8,128)} %fusion.511), custom_call_target="InvertDiagBlocksLowerTriangular" | custom-call | tf_op jit(solution)/shard_map/while/body/eval_jaxpr/triangular_solve/custom-call.1 | solution.py:126
  319.6 20.4 %custom-call.25 = f32[4,1,64,64]{2,3,1,0:T(8,128)S(1)} custom-call(f32[4,1,64,64]{3,2,1,0:T(8,128)} %fusion.511), custom_call_target="InvertDiagBlocksLowerTriangular" | custom-call | tf_op jit(solution)/shard_map/while/body/eval_jaxpr/triangular_solve/custom-call.1 | solution.py:126
  358.4 20.4 %custom-call.25 = f32[4,1,64,64]{2,3,1,0:T(8,128)S(1)} custom-call(f32[4,1,64,64]{3,2,1,0:T(8,128)} %fusion.511), custom_call_target="InvertDiagBlocksLowerTriangular" | custom-call | tf_op jit(solution)/shard_map/while/body/eval_jaxpr/triangular_solve/custom-call.1 | solution.py:126
  397.1 20.4 %custom-call.25 = f32[4,1,64,64]{2,3,1,0:T(8,128)S(1)} custom-call(f32[4,1,64,64]{3,2,1,0:T(8,128)} %fusion.511), custom_call_target="InvertDiagBlocksLowerTriangular" | custom-call | tf_op jit(solution)/shard_map/while/body/eval_jaxpr/triangular_solve/custom-call.1 | solution.py:126
  435.9 20.4 %custom-call.25 = f32[4,1,64,64]{2,3,1,0:T(8,128)S(1)} custom-call(f32[4,1,64,64]{3,2,1,0:T(8,128)} %fusion.511), custom_call_target="InvertDiagBlocksLowerTriangular" | custom-call | tf_op jit(solution)/shard_map/while/body/eval_jaxpr/triangular_solve/custom-call.1 | solution.py:126
  474.6 20.4 %custom-call.25 = f32[4,1,64,64]{2,3,1,0:T(8,128)S(1)} custom-call(f32[4,1,64,64]{3,2,1,0:T(8,128)} %fusion.511), custom_call_target="InvertDiagBlocksLowerTriangular" | custom-call | tf_op jit(solution)/shard_map/while/body/eval_jaxpr/triangular_solve/custom-call.1 | solution.py:126
  513.3 35.4 %while.84 = (s32[]{:T(128)}, f32[4,64,64]{1,2,0:T(8,128)S(1)}, f32[4,64,64]{1,2,0:T(8,128)S(1)}, f32[8,4,64,64]{2,3,0,1:T(8,128)}, f32[8,4,64,64]{2,3,0,1:T(8,12...) while((s32[]{:T(128)}, f32[4,64,64]{1,2,0:T(8,128)S(1)}, ...), condition=%wide.region_7.9_spmd.clone, body=%wide.region_6.8_spmd.clone.sunk | while | flops 25214980 | bytes 1508972 | solution.py:187
  569.3 29.2 %reduce-scatter.24.cloned.1.call-done = bf16[128,1024]{1,0:T(8,128)(2,1)} async-done(((bf16[512,1024]{1,0:T(8,128)(2,1)}), bf16[128,1024]{1,0:T(8,128)(2,1)}) %reduce-scatter.24.cloned.1.call-update) | async-done | bytes 262160 | tf_op jit(solution)/shard_map/reduce_scatter | solution.py:291
  604.7 22.0 %all-gather.10.cloned.1.call-done = bf16[1024,1024]{1,0:T(8,128)(2,1)} async-done(((bf16[128,1024]{1,0:T(8,128)(2,1)}), bf16[1024,1024]{1,0:T(8,128)(2,1)}) %all-gather.10.cloned.1.call-update) | async-done | bytes 2097168 | tf_op jit(solution)/shard_map/all_gather | solution.py:249
  626.7 30.0 %all-gather.8.cloned.1.call-done = bf16[512,1024]{1,0:T(8,128)(2,1)} async-done(((bf16[128,1024]{1,0:T(8,128)(2,1)}), bf16[512,1024]{1,0:T(8,128)(2,1)}) %all-gather.8.cloned.1.call-update) | async-done | bytes 1048592 | tf_op jit(solution)/shard_map/all_gather | solution.py:302
  661.2 24.8 %all-gather.12.cloned.1.call-done = bf16[1024,1024]{1,0:T(8,128)(2,1)} async-done(((bf16[1024,128]{1,0:T(8,128)(2,1)}), bf16[1024,1024]{1,0:T(8,128)(2,1)}) %all-gather.12.cloned.1.call-update) | async-done | bytes 2097168 | tf_op jit(solution)/shard_map/all_gather | solution.py:250
  698.2 22.8 %reduce-scatter.28.cloned.1.call-done = bf16[128,1024]{1,0:T(8,128)(2,1)} async-done(((bf16[512,1024]{1,0:T(8,128)(2,1)}), bf16[128,1024]{1,0:T(8,128)(2,1)}) %reduce-scatter.28.cloned.1.call-update) | async-done | bytes 262160 | tf_op jit(solution)/shard_map/reduce_scatter | solution.py:317
  729.7 19.5 %reduce-scatter.26.cloned.1.call-done = bf16[128,1024]{1,0:T(8,128)(2,1)} async-done(((bf16[512,1024]{1,0:T(8,128)(2,1)}), bf16[128,1024]{1,0:T(8,128)(2,1)}) %reduce-scatter.26.cloned.1.call-update) | async-done | bytes 262160 | tf_op jit(solution)/shard_map/reduce_scatter | solution.py:305
  755.3 25.4 %all-gather.14.cloned.1.call-done = bf16[512,1024]{1,0:T(8,128)(2,1)} async-done(((bf16[128,1024]{1,0:T(8,128)(2,1)}), bf16[512,1024]{1,0:T(8,128)(2,1)}) %all-gather.14.cloned.1.call-update) | async-done | bytes 1048592 | tf_op jit(solution)/shard_map/all_gather | solution.py:327
  803.5 25.9 %while.85 = (s32[]{:T(128)}, f32[4,64,64]{1,2,0:T(8,128)S(1)}, f32[4,64,64]{1,2,0:T(8,128)S(1)}, f32[8,4,64,64]{2,3,0,1:T(8,128)}, f32[8,4,64,64]{2,3,0,1:T(8,12...) while((s32[]{:T(128)}, f32[4,64,64]{1,2,0:T(8,128)S(1)}, ...), condition=%wide.region_21.23_spmd.clone, body=%wide.region_20.22_spmd.clone.sunk | while | flops 25214980 | bytes 1312387 | solution.py:201
  846.0 471.1 %while.83 = (s32[]{:T(128)}, f32[8,4,64,64]{3,2,1,0:T(8,128)}, f32[8,4,64,64]{3,2,1,0:T(8,128)}, f32[8,4,64,64]{3,2,1,0:T(8,128)}, f32[8,4,64,64]{3,2,1,0:T(8,12...) while((s32[]{:T(128)}, f32[8,4,64,64]{3,2,1,0:T(8,128)}, ...), condition=%wide.region_27.30_spmd, body=%wide.region_22.29_spmd.sunk | while | flops 468995392 | bytes 16470653 | solution.py:214
  849.4 19.7 %custom-call.26 = f32[4,1,64,64]{2,3,1,0:T(8,128)S(1)} custom-call(f32[4,1,64,64]{3,2,1,0:T(8,128)S(1)} %fusion.586), custom_call_target="InvertDiagBlocksLowerTriangular" | custom-call | tf_op jit(solution)/shard_map/while/body/eval_jaxpr/jvp()/triangular_solve/custom-call.1 | solution.py:122
  908.3 19.7 %custom-call.26 = f32[4,1,64,64]{2,3,1,0:T(8,128)S(1)} custom-call(f32[4,1,64,64]{3,2,1,0:T(8,128)S(1)} %fusion.586), custom_call_target="InvertDiagBlocksLowerTriangular" | custom-call | tf_op jit(solution)/shard_map/while/body/eval_jaxpr/jvp()/triangular_solve/custom-call.1 | solution.py:122
  967.1 19.7 %custom-call.26 = f32[4,1,64,64]{2,3,1,0:T(8,128)S(1)} custom-call(f32[4,1,64,64]{3,2,1,0:T(8,128)S(1)} %fusion.586), custom_call_target="InvertDiagBlocksLowerTriangular" | custom-call | tf_op jit(solution)/shard_map/while/body/eval_jaxpr/jvp()/triangular_solve/custom-call.1 | solution.py:122
  1026.0 19.7 %custom-call.26 = f32[4,1,64,64]{2,3,1,0:T(8,128)S(1)} custom-call(f32[4,1,64,64]{3,2,1,0:T(8,128)S(1)} %fusion.586), custom_call_target="InvertDiagBlocksLowerTriangular" | custom-call | tf_op jit(solution)/shard_map/while/body/eval_jaxpr/jvp()/triangular_solve/custom-call.1 | solution.py:122
  1084.8 19.7 %custom-call.26 = f32[4,1,64,64]{2,3,1,0:T(8,128)S(1)} custom-call(f32[4,1,64,64]{3,2,1,0:T(8,128)S(1)} %fusion.586), custom_call_target="InvertDiagBlocksLowerTriangular" | custom-call | tf_op jit(solution)/shard_map/while/body/eval_jaxpr/jvp()/triangular_solve/custom-call.1 | solution.py:122
  1143.6 19.7 %custom-call.26 = f32[4,1,64,64]{2,3,1,0:T(8,128)S(1)} custom-call(f32[4,1,64,64]{3,2,1,0:T(8,128)S(1)} %fusion.586), custom_call_target="InvertDiagBlocksLowerTriangular" | custom-call | tf_op jit(solution)/shard_map/while/body/eval_jaxpr/jvp()/triangular_solve/custom-call.1 | solution.py:122
  1202.5 19.7 %custom-call.26 = f32[4,1,64,64]{2,3,1,0:T(8,128)S(1)} custom-call(f32[4,1,64,64]{3,2,1,0:T(8,128)S(1)} %fusion.586), custom_call_target="InvertDiagBlocksLowerTriangular" | custom-call | tf_op jit(solution)/shard_map/while/body/eval_jaxpr/jvp()/triangular_solve/custom-call.1 | solution.py:122
  1261.3 19.7 %custom-call.26 = f32[4,1,64,64]{2,3,1,0:T(8,128)S(1)} custom-call(f32[4,1,64,64]{3,2,1,0:T(8,128)S(1)} %fusion.586), custom_call_target="InvertDiagBlocksLowerTriangular" | custom-call | tf_op jit(solution)/shard_map/while/body/eval_jaxpr/jvp()/triangular_solve/custom-call.1 | solution.py:122
  1365.4 27.4 %all-reduce.20.cloned.1.call-done = (bf16[512,128]{1,0:T(8,128)(2,1)}, bf16[512,64]{0,1:T(8,128)(2,1)}, bf16[512,64]{0,1:T(8,128)(2,1)}) async-done(((bf16[512,128]{1,0:T(8,128)(2,1)}, bf16[512,64]{0,1:T(8,128)(2,1)}, bf16[512,64]{0,1:T(8,128)(2,1)}), (bf16[512,128]{1,0:T(8,128)(2,1)}, bf16[512,64]{0,1:T(8,128)(2,1)}, bf16[512,64]{0,1:T(8,128)(2,1)})) %all-reduce.20.cloned.1.call-update) | async-done | bytes 262160 | tf_op jit(solution)/shard_map/psum | solution.py:376
  1395.7 4.6 multiply_reduce_fusion.1
  1409.2 4.9 convolution_convert_fusion
  1446.5 18.6 %all-reduce.13 = (bf16[3,1024]{1,0:T(4,128)(2,1)S(1)}, bf16[6,1024]{1,0:T(8,128)(2,1)S(1)}) all-reduce(bf16[3,1024]{1,0:T(4,128)(2,1)S(1)} %pad_maximum_fusion.3, bf16[6,1024]{1,0:T(8,128)(2,1)S(1)} %stack.102), channel_id=1, replica_groups=mesh['dp'=4,'seq'=2,'mp'=4] {'mp'}, use_global_device_ids=true, to_apply=%region_57.60 | all-reduce | flops 9216 | bytes 36864 | tf_op jit(solution)/shard_map/psum | solution.py:379
  1472.7 31.9 %reduce-scatter.44.cloned.1.call-done = bf16[128,1024]{1,0:T(8,128)(2,1)} async-done(((bf16[1024,1024]{1,0:T(8,128)(2,1)}), bf16[128,1024]{1,0:T(8,128)(2,1)}) %reduce-scatter.44.cloned.1.call-update) | async-done | bytes 262160
  1506.6 42.3 %reduce-scatter.36.cloned.1.call-done = bf16[128,1024]{1,0:T(8,128)(2,1)} async-done(((bf16[1024,1024]{1,0:T(8,128)(2,1)}), bf16[128,1024]{1,0:T(8,128)(2,1)}) %reduce-scatter.36.cloned.1.call-update) | async-done | bytes 262160 | tf_op jit(solution)/shard_map/reduce_scatter | solution.py:475
  1551.0 13.7 all-reduce.12
  1565.4 20.8 %reduce-scatter.34.cloned.1.call-done = bf16[16,256]{1,0:T(8,128)(2,1)} async-done(((bf16[128,256]{1,0:T(8,128)(2,1)}), bf16[16,256]{1,0:T(8,128)(2,1)}) %reduce-scatter.34.cloned.1.call-update) | async-done | bytes 8208 | tf_op jit(solution)/shard_map/reduce_scatter | solution.py:469
  1587.5 35.7 %reduce-scatter.42.cloned.1.call-done = bf16[8,512]{1,0:T(8,128)(2,1)} async-done(((bf16[64,512]{1,0:T(8,128)(2,1)}), bf16[8,512]{1,0:T(8,128)(2,1)}) %reduce-scatter.42.cloned.1.call-update) | async-done | bytes 8208
  1624.4 35.9 %reduce-scatter.40.cloned.1.call-done = bf16[128,128]{1,0:T(8,128)(2,1)} async-done(((bf16[1024,128]{1,0:T(8,128)(2,1)}), bf16[128,128]{1,0:T(8,128)(2,1)}) %reduce-scatter.40.cloned.1.call-update) | async-done | bytes 32784
  1661.9 35.0 %reduce-scatter.32.cloned.1.call-done = bf16[128,128]{1,0:T(8,128)(2,1)} async-done(((bf16[1024,128]{1,0:T(8,128)(2,1)}), bf16[128,128]{1,0:T(8,128)(2,1)}) %reduce-scatter.32.cloned.1.call-update) | async-done | bytes 32784 | tf_op jit(solution)/shard_map/reduce_scatter | solution.py:466
  1698.2 35.7 %reduce-scatter.38.cloned.1.call-done = bf16[128,256]{1,0:T(8,128)(2,1)} async-done(((bf16[1024,256]{1,0:T(8,128)(2,1)}), bf16[128,256]{1,0:T(8,128)(2,1)}) %reduce-scatter.38.cloned.1.call-update) | async-done | bytes 65552
  1738.6 31.9 %reduce-scatter.46.cloned.1.call-done = bf16[128,11]{1,0:T(8,128)(2,1)} async-done(((bf16[1024,11]{1,0:T(8,128)(2,1)}), bf16[128,11]{1,0:T(8,128)(2,1)}) %reduce-scatter.46.cloned.1.call-update) | async-done | bytes 2832
  1772.0 40.2 %reduce-scatter.30.cloned.1.call-done = bf16[3,128,256]{2,1,0:T(8,128)(2,1)} async-done(((bf16[3,1024,256]{2,1,0:T(8,128)(2,1)}), bf16[3,128,256]{2,1,0:T(8,128)(2,1)}) %reduce-scatter.30.cloned.1.call-update) | async-done | bytes 196624 | tf_op jit(solution)/shard_map/reduce_scatter | solution.py:442
  (1509 shorter events, 808.3 us)
Async XLA Ops:
  7.2 152.7 %all-gather.6.cloned.1.call-start = ((), (), s32[]{:S(2)}) async-start(), calls=%async_computation.12 | async-start | bytes 1769472 | tf_op jit(solution)/shard_map/all_gather | solution.py:243
  7.9 590.6 %reduce-scatter.24.cloned.1.call-start = ((), (), s32[]{:S(2)}) async-start(), calls=%async_computation.13 | async-start | bytes 1310720 | tf_op jit(solution)/shard_map/reduce_scatter | solution.py:291
  26.8 158.2 %copy-start.89 = (f32[1,1024]{1,0:T(1,128)}, f32[1,1024]{1,0:T(1,128)S(1)}, u32[]{:S(2)}) copy-start(f32[1,1024]{1,0:T(1,128)S(1)} %get-tuple-element.830) | copy-start | bytes 12292
  28.5 156.4 %copy-start.92 = (f32[512]{0:T(512)}, f32[512]{0:T(512)S(1)}, u32[]{:S(2)}) copy-start(f32[512]{0:T(512)S(1)} %broadcast_multiply_fusion.3) | copy-start | bytes 6148
  28.9 156.1 %copy-start.95 = (f32[512]{0:T(512)}, f32[512]{0:T(512)S(1)}, u32[]{:S(2)}) copy-start(f32[512]{0:T(512)S(1)} %fusion.236) | copy-start | bytes 6148
  29.5 35.8 %copy-start.113 = (bf16[2,128,64]{1,2,0:T(8,128)(2,1)S(1)}, bf16[2,128,64]{1,2,0:T(8,128)(2,1)}, u32[]{:S(2)}) copy-start(bf16[2,128,64]{1,2,0:T(8,128)(2,1)} %param.27) | copy-start | bytes 98308
  29.5 52.4 %copy-start.114 = (bf16[128,128]{1,0:T(8,128)(2,1)S(1)}, bf16[128,128]{1,0:T(8,128)(2,1)}, u32[]{:S(2)}) copy-start(bf16[128,128]{1,0:T(8,128)(2,1)} %param.29) | copy-start | bytes 98308
  29.5 69.3 %copy-start.98 = (bf16[256,128]{1,0:T(8,128)(2,1)S(1)}, bf16[256,128]{1,0:T(8,128)(2,1)}, u32[]{:S(2)}) copy-start(bf16[256,128]{1,0:T(8,128)(2,1)} %param.26) | copy-start | bytes 196612
  31.8 112.7 %collective-permute-start = (f32[1,1024]{1,0:T(1,128)}, f32[1,1024]{1,0:T(1,128)}, u32[]{:S(2)}, u32[]{:S(2)}) collective-permute-start(f32[1,1024]{1,0:T(1,128)} %slice.207), channel_id=1, source_target_pairs={{0,4},{1,5},{2,6},{3,7},{8,12},{9,13},{10,14},{11,15},{16,20},{17,... | collective-permute-start | bytes 12296 | tf_op jit(solution)/shard_map/ppermute | solution.py:16
  35.6 82.6 %copy-start.2 = (f32[512,1024]{1,0:T(8,128)S(1)}, f32[512,1024]{1,0:T(8,128)}, u32[]{:S(2)}) copy-start(f32[512,1024]{1,0:T(8,128)} %copy-done.1) | copy-start | bytes 6291460
  81.9 68.6 %copy-start.72 = (bf16[2,1024,64]{1,2,0:T(8,128)(2,1)}, bf16[2,1024,64]{1,2,0:T(8,128)(2,1)S(1)}, u32[]{:S(2)}) copy-start(bf16[2,1024,64]{1,2,0:T(8,128)(2,1)S(1)} %all_gather.39) | copy-start | bytes 786436
  98.1 59.6 %copy-start.69 = (bf16[1024,128]{1,0:T(8,128)(2,1)}, bf16[1024,128]{1,0:T(8,128)(2,1)S(1)}, u32[]{:S(2)}) copy-start(bf16[1024,128]{1,0:T(8,128)(2,1)S(1)} %all_gather.41) | copy-start | bytes 786436
  549.2 5.2 collective-permute-start.1
  567.0 32.6 %copy-start.60 = (bf16[512,256]{0,1:T(8,128)(2,1)}, bf16[512,256]{0,1:T(8,128)(2,1)S(1)}, u32[]{:S(2)}) copy-start(bf16[512,256]{0,1:T(8,128)(2,1)S(1)} %get-tuple-element.763) | copy-start | bytes 786436
  567.0 32.8 %copy-start.91 = (f32[1,1024]{1,0:T(1,128)S(1)}, f32[1,1024]{1,0:T(1,128)}, u32[]{:S(2)}) copy-start(f32[1,1024]{1,0:T(1,128)} %get-tuple-element.823) | copy-start | bytes 12292
  567.0 32.8 %copy-start.97 = (f32[1,1024]{1,0:T(1,128)S(1)}, f32[1,1024]{1,0:T(1,128)}, u32[]{:S(2)}) copy-start(f32[1,1024]{1,0:T(1,128)} %get-tuple-element.824) | copy-start | bytes 12292
  568.4 34.2 %copy-start.102 = (f32[1,1024]{1,0:T(1,128)S(1)}, f32[1,1024]{1,0:T(1,128)}, u32[]{:S(2)}) copy-start(f32[1,1024]{1,0:T(1,128)} %get-tuple-element.822) | copy-start | bytes 12292
  568.5 58.2 %all-gather.10.cloned.1.call-start = ((), (), s32[]{:S(2)}) async-start(), calls=%async_computation.15 | async-start | bytes 2359296 | tf_op jit(solution)/shard_map/all_gather | solution.py:249
  569.2 87.5 %all-gather.8.cloned.1.call-start = ((), (), s32[]{:S(2)}) async-start(), calls=%async_computation.14 | async-start | bytes 1310720 | tf_op jit(solution)/shard_map/all_gather | solution.py:302
  600.0 2.7 collective-permute-start.2
  603.6 82.3 %all-gather.12.cloned.1.call-start = ((), (), s32[]{:S(2)}) async-start(), calls=%async_computation.16 | async-start | bytes 2359296 | tf_op jit(solution)/shard_map/all_gather | solution.py:250
  604.2 116.9 %reduce-scatter.28.cloned.1.call-start = ((), (), s32[]{:S(2)}) async-start(), calls=%async_computation.18 | async-start | bytes 1310720 | tf_op jit(solution)/shard_map/reduce_scatter | solution.py:317
  693.6 55.6 %reduce-scatter.26.cloned.1.call-start = ((), (), s32[]{:S(2)}) async-start(), calls=%async_computation.17 | async-start | bytes 1310720 | tf_op jit(solution)/shard_map/reduce_scatter | solution.py:305
  698.2 82.5 %all-gather.14.cloned.1.call-start = ((), (), s32[]{:S(2)}) async-start(), calls=%async_computation.19 | async-start | bytes 1310720 | tf_op jit(solution)/shard_map/all_gather | solution.py:327
  722.2 5.5 collective-permute-start.3
  754.1 638.7 %all-reduce.20.cloned.1.call-start = ((), (), s32[]{:S(2)}) async-start(), calls=%async_computation.30 | async-start | bytes 524288 | tf_op jit(solution)/shard_map/psum | solution.py:376
  783.8 47.4 %copy-start.57 = (bf16[512,256]{0,1:T(8,128)(2,1)}, bf16[512,256]{0,1:T(8,128)(2,1)S(1)}, u32[]{:S(2)}) copy-start(bf16[512,256]{0,1:T(8,128)(2,1)S(1)} %get-tuple-element.803) | copy-start | bytes 786436
  829.9 6.2 collective-permute-start.4
  1358.5 106.7 %all-reduce.18.cloned.1.call-start = ((), (), s32[]{:S(2)}) async-start(), calls=%async_computation.20 | async-start | bytes 2097152 | tf_op jit(solution)/shard_map/psum | solution.py:416
  1363.5 32.1 %copy-start.105 = (f32[1,1024]{1,0:T(1,128)S(1)}, f32[1,1024]{1,0:T(1,128)}, u32[]{:S(2)}) copy-start(f32[1,1024]{1,0:T(1,128)} %get-tuple-element.826) | copy-start | bytes 12292
  1400.3 5.8 collective-permute-start.5
  1409.1 95.6 %reduce-scatter.44.cloned.1.call-start = ((), (), s32[]{:S(2)}) async-start(), calls=%async_computation.28 | async-start | bytes 2359296
  1418.0 131.0 %reduce-scatter.36.cloned.1.call-start = ((), (), s32[]{:S(2)}) async-start(), calls=%async_computation.24 | async-start | bytes 2359296 | tf_op jit(solution)/shard_map/reduce_scatter | solution.py:475
  1422.3 163.8 %reduce-scatter.34.cloned.1.call-start = ((), (), s32[]{:S(2)}) async-start(), calls=%async_computation.23 | async-start | bytes 73728 | tf_op jit(solution)/shard_map/reduce_scatter | solution.py:469
  1424.1 199.0 %reduce-scatter.42.cloned.1.call-start = ((), (), s32[]{:S(2)}) async-start(), calls=%async_computation.27 | async-start | bytes 73728
  1426.2 234.1 %reduce-scatter.40.cloned.1.call-start = ((), (), s32[]{:S(2)}) async-start(), calls=%async_computation.26 | async-start | bytes 294912
  1431.6 265.3 %reduce-scatter.32.cloned.1.call-start = ((), (), s32[]{:S(2)}) async-start(), calls=%async_computation.22 | async-start | bytes 294912 | tf_op jit(solution)/shard_map/reduce_scatter | solution.py:466
  1434.1 299.9 %reduce-scatter.38.cloned.1.call-start = ((), (), s32[]{:S(2)}) async-start(), calls=%async_computation.25 | async-start | bytes 589824
  1438.8 331.7 %reduce-scatter.46.cloned.1.call-start = ((), (), s32[]{:S(2)}) async-start(), calls=%async_computation.29 | async-start | bytes 294912
  1468.7 343.5 %reduce-scatter.30.cloned.1.call-start = ((), (), s32[]{:S(2)}) async-start(), calls=%async_computation.21 | async-start | bytes 1769472 | tf_op jit(solution)/shard_map/reduce_scatter | solution.py:442
  1471.4 79.4 %copy-start.146 = (f32[256]{0:T(256)S(1)}, f32[256]{0:T(256)}, u32[]{:S(2)}) copy-start(f32[256]{0:T(256)} %get-tuple-element.750) | copy-start | bytes 3076
  1471.4 79.4 %copy-start.143 = (f32[256]{0:T(256)S(1)}, f32[256]{0:T(256)}, u32[]{:S(2)}) copy-start(f32[256]{0:T(256)} %get-tuple-element.653) | copy-start | bytes 3076
  1471.4 79.4 %copy-start.144 = (f32[256]{0:T(256)S(1)}, f32[256]{0:T(256)}, u32[]{:S(2)}) copy-start(f32[256]{0:T(256)} %get-tuple-element.654) | copy-start | bytes 3076
  1471.4 79.4 %copy-start.147 = (f32[256]{0:T(256)S(1)}, f32[256]{0:T(256)}, u32[]{:S(2)}) copy-start(f32[256]{0:T(256)} %get-tuple-element.802) | copy-start | bytes 3076
  1471.4 79.4 %copy-start.142 = (f32[256]{0:T(256)S(1)}, f32[256]{0:T(256)}, u32[]{:S(2)}) copy-start(f32[256]{0:T(256)} %get-tuple-element.748) | copy-start | bytes 3076
  1471.4 79.4 %copy-start.148 = (f32[256]{0:T(256)S(1)}, f32[256]{0:T(256)}, u32[]{:S(2)}) copy-start(f32[256]{0:T(256)} %get-tuple-element.651) | copy-start | bytes 3076
  1471.4 79.4 %copy-start.149 = (f32[256]{0:T(256)S(1)}, f32[256]{0:T(256)}, u32[]{:S(2)}) copy-start(f32[256]{0:T(256)} %get-tuple-element.652) | copy-start | bytes 3076
  1471.5 264.1 %copy-start.120 = (f32[512]{0:T(512)S(1)}, f32[512]{0:T(512)}, u32[]{:S(2)}) copy-start(f32[512]{0:T(512)} %copy-done.119) | copy-start | bytes 6148
  (244 other events, 1590.3 us)
Sparse Core Ops, SparseCore 0:
  9.9 28.2 all-gather.5
  568.6 29.8 reduce-scatter.23
  600.4 26.2 all-gather.9
  628.7 27.9 all-gather.7
  658.4 27.4 all-gather.11
  693.7 27.2 reduce-scatter.27
  723.4 25.7 reduce-scatter.25
  754.2 26.4 all-gather.13
  1358.6 34.1 all-reduce.19
  1409.2 51.7 all-reduce.17
  1464.3 40.3 reduce-scatter.43
  1507.8 41.1 reduce-scatter.35
  1552.6 33.5 reduce-scatter.33
  1589.6 33.5 reduce-scatter.41
  1626.6 33.6 reduce-scatter.39
  1663.2 33.6 reduce-scatter.31
  1699.8 34.1 reduce-scatter.37
  1736.8 33.6 reduce-scatter.45
  1773.8 38.3 reduce-scatter.29
where the time goes:
time: 1830 us; the launch traced here: 1820 us
  waiting for transfers between devices  526 us (29%)
  matrix products  504 us (28%)
  other arithmetic  445 us (24%)
  local copies, waits for them, and re-layouts  161 us (9%)
  blocking collectives  149 us (8%)
    unnamed x24, waiting for transfers between devices  173 us
    another operation x24, other arithmetic, block_parts(): lax.linalg.triangular_solve(system, pushed, left_side=True, lower=True, u...  164 us
    another operation x24, other arithmetic, block_parts(): lax.linalg.triangular_solve(system, query_unit, left_side=True, lower=Tru...  158 us
    dot_general x128, matrix products, pair_product(): return jnp.einsum('htj,hsj->hts', former, latter, precision=precise)  97 us
    reduce_scatter x1, waiting for transfers between devices, body(): lax.psum_scatter(key_gradient.astype(jnp.bfloat16), ('dp', 'seq'), scatte...  42.3 us
    dot_general x24, matrix products, block_parts(): jnp.einsum('hti,htj->hij', local_push, removal_tail, precision=precise)  40.9 us
    reduce_scatter x1, waiting for transfers between devices, body(): lax.psum_scatter(receptance_key_value_gradient.astype(jnp.bfloat16), ('dp...  40.2 us
    dot_general x24, matrix products, block_parts(): jnp.einsum('hti,htj->hij', payload_mapped, key_tail, precision=precise)  38.6 us
  transfers between devices with their start and end apart: 25, of which 22 were waited for; matrix products, arithmetic and copies ran while one was open for 6% of the time, Pallas kernels for 0%

commit v1 on v0

v1 whole, which is shorter than its diff:
```python
import functools

import jax
import jax.numpy as jnp
from jax import lax
from jax.experimental import pallas as pl
from jax.experimental.pallas import tpu as pltpu
from jax.sharding import PartitionSpec as P

SPAN = 64
f32 = jnp.float32
bf16 = jnp.bfloat16


def halves(x):
    high = x.astype(bf16)
    return high, (x - high.astype(f32)).astype(bf16)


def dot(a, b, ca, cb):
    return lax.dot_general(a, b, (((ca,), (cb,)), ((), ())), preferred_element_type=f32)


def spread(x, mask):
    tiled = jnp.concatenate([x] * (x.shape[1] // SPAN), axis=0)
    return jnp.where(mask, tiled, jnp.zeros_like(tiled))


def fold(x, mask):
    x = jnp.where(mask, x, jnp.zeros_like(x))
    return sum(x[i * SPAN : (i + 1) * SPAN] for i in range(x.shape[0] // SPAN))


def times(a, b, mask, cb):
    return dot(a.astype(bf16), spread(b.astype(bf16), mask), 1, cb)


def fine(a, b, mask, cb):
    ah, al = halves(a)
    bh, bl = halves(b)
    rows = a.shape[0]
    both = dot(jnp.concatenate([ah, al], axis=0), spread(bh, mask), 1, cb)
    return both[:rows] + both[rows:] + dot(ah, spread(bl, mask), 1, cb)


def cross(a, b):
    return dot(a.astype(bf16), b.astype(bf16), 0, 0)


def fine_cross(a, b):
    ah, al = halves(a)
    bh, bl = halves(b)
    return dot(
        jnp.concatenate([ah, al, ah], axis=0), jnp.concatenate([bh, bh, bl], axis=0), 0, 0
    )


def exact_left(ones, x):
    high = x.astype(bf16)
    rest = x - high.astype(f32)
    mid = rest.astype(bf16)
    low = (rest - mid.astype(f32)).astype(bf16)
    return dot(ones, high, 1, 0) + dot(ones, mid, 1, 0) + dot(ones, low, 1, 0)


def head_sum(x, ones):
    high, low = halves(x)
    rows = x.shape[0]
    both = dot(jnp.concatenate([high, low], axis=0), ones, 1, 0)
    return both[:rows] + both[rows:]


def constants(width):
    iota = lax.broadcasted_iota
    big_row = iota(jnp.int32, (width, width), 0)
    big_col = iota(jnp.int32, (width, width), 1)
    mask = (big_row // SPAN) == (big_col // SPAN)
    t = iota(jnp.int32, (SPAN, SPAN), 0)
    s = iota(jnp.int32, (SPAN, SPAN), 1)
    row = iota(jnp.int32, (SPAN, width), 0)
    col = iota(jnp.int32, (SPAN, width), 1) % SPAN
    one = lambda where: jnp.where(where, 1.0, 0.0).astype(f32)
    return dict(
        mask=mask,
        diagonal=one(big_row == big_col),
        ones=one(mask).astype(bf16),
        lower=one(t >= s).astype(bf16),
        upper=one(t <= s).astype(bf16),
        strict=row > col,
        incl=row >= col,
        eye=one(row == col),
        near=(row // 4 == col // 4) & (row > col),
        mid=(row // 16 == col // 16) & (row // 4 > col // 4),
        far=row // 16 > col // 16,
    )


def ready(q, kp, din, rin, rows, c):
    sig = jax.nn.sigmoid(rows[0:1] + din)
    log_decay = -0.6065306597126334 * sig
    rate = jax.nn.sigmoid(rows[1:2] + rin)
    scaled = kp * rows[2:3]
    inv = lax.rsqrt(head_sum(scaled * scaled, c["ones"]) + 1e-6)
    unit = scaled * inv
    removal = unit * rate
    total = exact_left(c["lower"], log_decay)
    up = jnp.exp(total)
    down = jnp.exp(-total)
    before = jnp.exp(total - log_decay)
    return dict(
        sig=sig,
        log_decay=log_decay,
        rate=rate,
        inv=inv,
        unit=unit,
        up=up,
        down=down,
        before=before,
        Q=q * up,
        U=unit * before,
        K=kp * (1.0 + (rate - 1.0) * rows[3:4]) * down,
        R=removal * down,
        last=up[SPAN - 1 : SPAN],
    )


def inverse(lower, c):
    mask = c["mask"]
    zero = jnp.zeros_like(lower)
    inner = jnp.where(c["near"], lower, zero)
    square = fine(inner, inner, mask, 0)
    out = c["eye"] - inner + square - fine(inner, square, mask, 0)
    for level in ("mid", "far"):
        step = fine(out, jnp.where(c[level], lower, zero), mask, 0)
        step_two = fine(step, step, mask, 0)
        first = out - fine(step, out, mask, 0)
        out = first + fine(step_two, first, mask, 0)
    return out


def pairs(e, c):
    mask = c["mask"]
    zero = jnp.zeros((SPAN, mask.shape[0]), f32)
    queries = jnp.concatenate([e["U"], e["Q"]], axis=0)
    by_key = fine(queries, e["K"], mask, 1)
    by_removal = fine(queries, e["R"], mask, 1)
    return (
        jnp.where(c["strict"], by_key[:SPAN], zero),
        jnp.where(c["incl"], by_key[SPAN:], zero),
        jnp.where(c["strict"], by_removal[:SPAN], zero),
        jnp.where(c["incl"], by_removal[SPAN:], zero),
    )


def blocks_per_step(count):
    return 2 if count % 2 == 0 else 1


def local_kernel(per, q, kp, v, din, rin, rows_ref, local_out, read, push_map, push, inv_out,
                 uk_out, qk_out, qr_out, carry, maps, adds, map_end, add_end, map_now, add_now):
    width = q.shape[1]
    c = constants(width)
    rows = rows_ref[...]

    @pl.when(pl.program_id(0) == 0)
    def _():
        map_now[...] = c["eye"]
        add_now[...] = jnp.zeros_like(add_now)

    chain = []
    for i in range(per):
        at = slice(i * SPAN, (i + 1) * SPAN)
        e = ready(q[at, :], kp[at, :], din[at, :], rin[at, :], rows, c)
        uk, qk, ur, qr = pairs(e, c)
        inv = inverse(ur, c)
        values = v[at, :]
        mixed = fine(jnp.concatenate([uk, qk], axis=0), values, c["mask"], 0)
        y = fine(inv, mixed[:SPAN], c["mask"], 0)
        w = fine(inv, e["U"], c["mask"], 0)
        local_out[at, :] = mixed[SPAN:] - fine(qr, y, c["mask"], 0)
        read[at, :] = e["Q"] - fine(qr, w, c["mask"], 0)
        push_map[at, :] = w
        push[at, :] = y
        inv_out[at, :] = inv.astype(bf16)
        uk_out[at, :] = uk.astype(bf16)
        qk_out[at, :] = qk.astype(bf16)
        qr_out[at, :] = qr.astype(bf16)
        carried = jnp.where(c["mask"], fine_cross(w, e["R"]), jnp.zeros_like(c["diagonal"]))
        carry_here = ((c["diagonal"] - carried) * e["last"]).astype(bf16)
        carry[i * width : (i + 1) * width, :] = carry_here
        added = fold(
            fine_cross(
                jnp.concatenate([values, y], axis=0), jnp.concatenate([e["K"], -e["R"]], axis=0)
            ),
            c["mask"],
        ) * e["last"]
        chain.append((at, carry_here, added))
    state_map, state_add = map_now[...], add_now[...]
    for at, carry_here, added in chain:
        both = dot(
            jnp.concatenate([state_map, state_add], axis=0).astype(bf16), carry_here, 1, 0
        )
        state_map, state_add = both[:SPAN], both[SPAN:] + added
        maps[at, :] = state_map
        adds[at, :] = state_add
    map_now[...] = state_map
    add_now[...] = state_add
    map_end[...] = state_map
    add_end[...] = state_add


def normed(out, q, k, v, rows, c):
    ones = c["ones"]
    center = out - head_sum(out, ones) * (1.0 / SPAN)
    spread_here = head_sum(center * center, ones) * (1.0 / SPAN)
    scale = lax.rsqrt(spread_here + 0.00064)
    unit = center * scale
    extra = head_sum(q * k * rows[4:5], ones)
    return unit, scale, extra, unit * rows[5:6] + rows[6:7] + extra * v


def finish_kernel(per, q, kp, v, rin, gate, rows_ref, local_out, read, push_map, push, maps, adds,
                  state_in, gated, out_ref, push_out, starts, ends, state_now):
    c = constants(q.shape[1])
    rows = rows_ref[...]
    mask = c["mask"]

    @pl.when(pl.program_id(0) == 0)
    def _():
        state_now[...] = state_in[...]

    entering = state_in[...]
    state = state_now[...]
    for i in range(per):
        at = slice(i * SPAN, (i + 1) * SPAN)
        starts[at, :] = state
        both = fine(jnp.concatenate([read[at, :], push_map[at, :]], axis=0), state, mask, 1)
        out = local_out[at, :] + both[:SPAN]
        push_out[at, :] = push[at, :] + both[SPAN:]
        out_ref[at, :] = out
        rate = jax.nn.sigmoid(rows[1:2] + rin[at, :])
        k = kp[at, :] * (1.0 + (rate - 1.0) * rows[3:4])
        _, _, _, summed = normed(out, q[at, :], k, v[at, :], rows, c)
        gated[at, :] = (summed * gate[at, :]).astype(bf16)
        state = adds[at, :] + times(entering, maps[at, :], mask, 0)
        ends[at, :] = state
    state_now[...] = state


def reads_kernel(per, q, kp, v, rin, gate, rows_ref, out_ref, d_gated, read, carry, d_out, dq_post,
                 dk_post, dv_post, d_gate, maps, adds, map_end, add_end, row_grads, map_now,
                 add_now):
    width = q.shape[1]
    c = constants(width)
    rows = rows_ref[...]
    ones = c["ones"]

    @pl.when(pl.program_id(0) == 0)
    def _():
        map_now[...] = c["eye"]
        add_now[...] = jnp.zeros_like(add_now)
        row_grads[...] = jnp.zeros_like(row_grads)

    state_map, state_add = map_now[...], add_now[...]
    column = lambda x: jnp.sum(x, axis=0, keepdims=True)
    for i in reversed(range(per)):
        at = slice(i * SPAN, (i + 1) * SPAN)
        q_here, v_here, g_here = q[at, :], v[at, :], gate[at, :]
        rate = jax.nn.sigmoid(rows[1:2] + rin[at, :])
        k = kp[at, :] * (1.0 + (rate - 1.0) * rows[3:4])
        unit, scale, extra, summed = normed(out_ref[at, :], q_here, k, v_here, rows, c)
        grad = d_gated[at, :].astype(f32)
        d_gate[at, :] = (grad * summed).astype(bf16)
        d_sum = grad * g_here
        d_unit = d_sum * rows[5:6]
        d_here = scale * (
            d_unit
            - head_sum(d_unit, ones) * (1.0 / SPAN)
            - unit * head_sum(d_unit * unit, ones) * (1.0 / SPAN)
        )
        d_extra = head_sum(d_sum * v_here, ones)
        d_out[at, :] = d_here
        dq_post[at, :] = d_extra * k * rows[4:5]
        dk_post[at, :] = d_extra * q_here * rows[4:5]
        dv_post[at, :] = d_sum * extra
        row_grads[4:5, :] += column(d_extra * q_here * k)
        row_grads[5:6, :] += column(d_sum * unit)
        row_grads[6:7, :] += column(d_sum)
        maps[at, :] = state_map
        adds[at, :] = state_add
        carry_here = carry[i * width : (i + 1) * width, :]
        both = dot(
            jnp.concatenate([state_map, state_add], axis=0).astype(bf16), carry_here, 1, 1
        )
        state_map = both[:SPAN]
        state_add = both[SPAN:] + fold(cross(d_here, read[at, :]), c["mask"])
    map_now[...] = state_map
    add_now[...] = state_add
    map_end[...] = state_map
    add_end[...] = state_add


def grads_kernel(per, q, kp, v, din, rin, lat_ref, d_gate_ref, rows_ref, up_ref, push_ref, inv_ref, uk_ref, qk_ref, qr_ref,
                 starts, ends, d_out, dq_post, dk_post, dv_post, maps, adds, grad_in, dq_ref,
                 dkp_ref, dv_ref, pre_ref, row_grads, up_grads):
    c = constants(q.shape[1])
    up = up_ref[...]
    rows = rows_ref[...]
    mask, ones = c["mask"], c["ones"]
    cat = lambda *parts: jnp.concatenate(parts, axis=0)
    column = lambda x: jnp.sum(x, axis=0, keepdims=True)

    @pl.when(pl.program_id(0) == 0)
    def _():
        row_grads[...] = jnp.zeros_like(row_grads)
        up_grads[...] = jnp.zeros_like(up_grads)

    zero = jnp.zeros((SPAN, mask.shape[0]), f32)
    rank, gate_at = low_parts(up.shape[0])
    lane = lax.broadcasted_iota(jnp.int32, (SPAN, up.shape[0]), 1)
    low_row = lax.broadcasted_iota(jnp.int32, up_grads.shape, 0)
    for i in range(per):
        at = slice(i * SPAN, (i + 1) * SPAN)
        q_here, kp_here, v_here = q[at, :], kp[at, :], v[at, :]
        e = ready(q_here, kp_here, din[at, :], rin[at, :], rows, c)
        start, end, pushed, d_read = starts[at, :], ends[at, :], push_ref[at, :], d_out[at, :]
        grad_end = adds[at, :] + times(grad_in[...], maps[at, :], mask, 0)
        grown = grad_end * e["last"]
        by_state = times(cat(e["K"], e["R"]), grown, mask, 1)
        d_push = -fold(cross(qr_ref[at, :], d_read), mask) - by_state[SPAN:]
        d_rhs = fold(cross(inv_ref[at, :], d_push), mask)
        d_value = (
            by_state[:SPAN]
            + fold(cross(cat(qk_ref[at, :], uk_ref[at, :]), cat(d_read, d_rhs)), mask)
        )
        both = cat(d_rhs, d_read)
        by_value = times(both, v_here, mask, 1)
        by_push = times(both, pushed, mask, 1)
        d_key_pairs = cat(
            jnp.where(c["strict"], by_value[:SPAN], zero), jnp.where(c["incl"], by_value[SPAN:], zero)
        )
        d_removal_pairs = cat(
            jnp.where(c["strict"], -by_push[:SPAN], zero), jnp.where(c["incl"], -by_push[SPAN:], zero)
        )
        d_queries = (
            times(both, start, mask, 0)
            + times(d_key_pairs, e["K"], mask, 0)
            + times(d_removal_pairs, e["R"], mask, 0)
        )
        by_grown = times(cat(v_here, -pushed), grown, mask, 0)
        queries = cat(e["U"], e["Q"])
        d_k_grown = by_grown[:SPAN] + fold(cross(d_key_pairs, queries), mask)
        d_r_grown = by_grown[SPAN:] + fold(cross(d_removal_pairs, queries), mask)
        d_u_grown, d_q_grown = d_queries[:SPAN], d_queries[SPAN:]
        on_unit = d_u_grown * e["U"]
        steps = d_q_grown * e["Q"] - d_k_grown * e["K"] - d_r_grown * e["R"] + on_unit
        d_log = exact_left(c["upper"], steps) - on_unit + column(grad_end * end)
        rate = e["rate"]
        d_k = d_k_grown * e["down"] + dk_post[at, :]
        d_removal = d_r_grown * e["down"]
        d_unit = d_u_grown * e["before"] + d_removal * rate
        d_rate_value = d_removal * e["unit"] + d_k * kp_here * rows[3:4]
        d_scaled = e["inv"] * (d_unit - e["unit"] * head_sum(d_unit * e["unit"], ones))
        d_rate = d_rate_value * rate * (1.0 - rate)
        d_decay = d_log * e["log_decay"] * (1.0 - e["sig"])
        dq_ref[at, :] = (d_q_grown * e["up"] + dq_post[at, :]).astype(bf16)
        dkp_ref[at, :] = (d_k * (1.0 + (rate - 1.0) * rows[3:4]) + d_scaled * rows[2:3]).astype(bf16)
        dv_ref[at, :] = (d_value + dv_post[at, :]).astype(bf16)
        lat = lat_ref[at, :]
        low = lat.astype(bf16)
        d_outs = (d_decay.astype(bf16), d_rate.astype(bf16), d_gate_ref[at, :])
        pick = lambda where, parts: jnp.where(
            where < rank, parts[0], jnp.where(where < gate_at, parts[1], parts[2])
        )
        slope = pick(lane, (1.0 - lat * lat, jnp.ones_like(lat), lat * (1.0 - lat)))
        pre = pick(lane, [dot(x, up, 1, 1) for x in d_outs]) * slope
        pre_ref[at, :] = pre.astype(bf16)
        up_grads[...] += pick(low_row, [dot(low, x, 0, 0) for x in d_outs])
        row_grads[0:1, :] += column(d_decay)
        row_grads[1:2, :] += column(d_rate)
        row_grads[2:3, :] += column(d_scaled * kp_here)
        row_grads[3:4, :] += column(d_k * kp_here * (rate - 1.0))


def run_blocks(kernel, name, ins, outs, scratch, tokens, reverse=False):
    count = tokens // SPAN
    per = blocks_per_step(count)
    steps = count // per

    def spec(shape, cut):
        if not cut:
            return pl.BlockSpec(shape, lambda i: (0, 0))
        rows = shape[0] // steps
        if reverse:
            return pl.BlockSpec((rows, shape[1]), lambda i: (steps - 1 - i, 0))
        return pl.BlockSpec((rows, shape[1]), lambda i: (i, 0))

    return pl.pallas_call(
        functools.partial(kernel, per),
        grid=(steps,),
        in_specs=[spec(x.shape, cut) for x, cut in ins],
        out_specs=[spec(shape, cut) for shape, _, cut in outs],
        out_shape=[jax.ShapeDtypeStruct(shape, kind) for shape, kind, _ in outs],
        scratch_shapes=[pltpu.VMEM(shape, f32) for shape in scratch],
        compiler_params=pltpu.CompilerParams(dimension_semantics=("arbitrary",)),
        cost_estimate=pl.CostEstimate(flops=10**10, bytes_accessed=2 * 10**7, transcendentals=0),
        name=name,
    )(*[x for x, _ in ins])


def low_parts(width):
    return width // 4, width // 2


def mixed(unit, edge, norms, count):
    first = unit * norms[0:1] + norms[1:2]
    before = (edge[0:1] * norms[0:1] + norms[1:2]) * edge[1:2]
    row = lax.broadcasted_iota(jnp.int32, first.shape, 0)
    diff = jnp.where(row == 0, before, pltpu.roll(first, 1, 0)) - first
    return diff, [(first + diff * norms[4 + i : 5 + i]).astype(bf16) for i in range(count)]


def slab_weights(gathered, width):
    parts, rows, _ = gathered.shape
    part = rows // 4
    piece = lambda i, w: jnp.concatenate(
        [gathered[j, i * part : (i + 1) * part, :w] for j in range(parts)], axis=0
    )
    return [piece(i, width) for i in range(3)] + [piece(3, gathered.shape[2])]


def project_kernel(unit, edge, norms, gathered, up, q, kp, v, din, rin, gate, lat, low_total):
    width = q.shape[1]
    step = pl.program_id(0)
    norms_here = norms[...]
    _, mixes = mixed(unit[...], edge[...], norms_here, 6)
    w_q, w_k, w_v, w_low = slab_weights(gathered, width)
    low_width = w_low.shape[1]
    rank, gate_at = low_parts(low_width)
    lane = lax.broadcasted_iota(jnp.int32, low_total.shape, 1)
    low = jnp.where(
        lane < rank,
        dot(mixes[1], w_low, 1, 0),
        jnp.where(lane < gate_at, dot(mixes[4], w_low, 1, 0), dot(mixes[5], w_low, 1, 0)),
    )

    @pl.when(step == 0)
    def _():
        q[...] = dot(mixes[0], w_q, 1, 0)
        kp[...] = dot(mixes[2], w_k, 1, 0)
        v[...] = dot(mixes[3], w_v, 1, 0)
        low_total[...] = low

    @pl.when(step > 0)
    def _():
        q[...] += dot(mixes[0], w_q, 1, 0)
        kp[...] += dot(mixes[2], w_k, 1, 0)
        v[...] += dot(mixes[3], w_v, 1, 0)
        low_total[...] += low

    @pl.when(step == pl.num_programs(0) - 1)
    def _():
        total = low_total[...]
        lats = jnp.where(
            lane < rank, jnp.tanh(total), jnp.where(lane < gate_at, total, jax.nn.sigmoid(total))
        )
        lat[...] = lats
        zero = jnp.zeros_like(lats)
        chosen = lambda where: jnp.where(where, lats, zero).astype(bf16)
        din[...] = dot(chosen(lane < rank), up[...], 1, 0)
        rin[...] = dot(chosen((lane >= rank) & (lane < gate_at)), up[...], 1, 0)
        gate[...] = dot(chosen(lane >= gate_at), up[...], 1, 0)


def unproject_kernel(unit, edge, scales, norms, gathered, dq, dkp, dv, pre, packed, feature, edge_fix,
                     d_in, all_first, all_unit, all_gain):
    width = dq.shape[1]
    step = pl.program_id(0)
    n = norms[...]
    edge_here = edge[...]
    unit_here = unit[...]
    diff, mixes = mixed(unit_here, edge_here, n, 6)
    weights = slab_weights(gathered, width)
    w_low = weights[3]
    slab, low_width = w_low.shape
    rank, gate_at = low_parts(low_width)
    pre_here = pre[...]
    lane = lax.broadcasted_iota(jnp.int32, pre_here.shape, 1)
    none = jnp.zeros_like(pre_here)
    pres = [
        jnp.where(lane < rank, pre_here, none),
        jnp.where((lane >= rank) & (lane < gate_at), pre_here, none),
        jnp.where(lane >= gate_at, pre_here, none),
    ]
    sources = [(0, dq[...], 0), (2, dkp[...], 1), (3, dv[...], 2), (1, pres[0], 3), (4, pres[1], 3),
               (5, pres[2], 3)]
    low_lane = lax.broadcasted_iota(jnp.int32, (slab, low_width), 1)
    column = lambda x: jnp.sum(x, axis=0, keepdims=True)
    parts = gathered.shape[0]
    part = slab // parts
    direct = shifted = None
    low_grad = None
    for mix, grad, which in sources:
        weight_grad = dot(mixes[mix], grad, 0, 0)
        if which < 3:
            for j in range(parts):
                packed[j, which * part : (which + 1) * part, :width] = weight_grad[
                    j * part : (j + 1) * part
                ].astype(bf16)
                if width < low_width:
                    packed[j, which * part : (which + 1) * part, width:] = jnp.zeros(
                        (part, low_width - width), bf16
                    )
        else:
            low_grad = weight_grad if low_grad is None else low_grad + weight_grad
        d_mix = dot(grad, weights[which], 1, 1)
        feature[4 + mix : 5 + mix, :] = column(d_mix * diff)
        to_shift = d_mix * n[4 + mix : 5 + mix]
        shifted = to_shift if shifted is None else shifted + to_shift
        direct = d_mix - to_shift if direct is None else direct + (d_mix - to_shift)
    for j in range(parts):
        packed[j, 3 * part : 4 * part, :] = low_grad[j * part : (j + 1) * part].astype(bf16)
    tokens = unit_here.shape[0]
    row = lax.broadcasted_iota(jnp.int32, shifted.shape, 0)
    d_first = direct + jnp.where(row == tokens - 1, 0.0, pltpu.roll(shifted, tokens - 1, 0))
    before = shifted[0:1] * edge_here[1:2]
    feature[0:1, :] = column(d_first * unit_here) + before * edge_here[0:1]
    feature[1:2, :] = column(d_first) + before
    feature[2:4, :] = jnp.zeros_like(feature[2:4, :])
    feature[10:, :] = jnp.zeros_like(feature[10:, :])
    at = pl.ds(pl.multiple_of(step * slab, slab), slab)
    all_first[:tokens, at] = d_first * n[0:1]
    all_first[tokens:, at] = jnp.broadcast_to(before * n[0:1], (8, slab))
    all_unit[:tokens, at] = unit_here
    all_unit[tokens:, at] = jnp.broadcast_to(edge_here[0:1], (8, slab))

    @pl.when(step == pl.num_programs(0) - 1)
    def _():
        d_unit = all_first[...]
        units = all_unit[...]
        features = d_unit.shape[1]
        mean = jnp.sum(d_unit, axis=1, keepdims=True) * (1.0 / features)
        along = jnp.sum(d_unit * units, axis=1, keepdims=True) * (1.0 / features)
        result = scales[...] * (d_unit - mean - units * along)
        d_in[...] = result[:tokens]
        edge_fix[...] = result[tokens:]


def run_slabs(kernel, name, ins, outs, scratch, slabs):
    def spec(shape, cut):
        shape = tuple(shape)
        if cut is None:
            return pl.BlockSpec(shape, lambda i: (0,) * len(shape))
        dim, size = cut
        block = list(shape)
        block[dim] = shape[dim] // slabs
        if size is not None:
            block[size[0]] = size[1]
        return pl.BlockSpec(tuple(block), lambda i: tuple(i if k == dim else 0 for k in range(len(shape))))

    return pl.pallas_call(
        kernel,
        grid=(slabs,),
        in_specs=[spec(x.shape, cut) for x, cut in ins],
        out_specs=[spec(shape, cut) for shape, _, cut in outs],
        out_shape=[jax.ShapeDtypeStruct(shape, kind) for shape, kind, _ in outs],
        scratch_shapes=[pltpu.VMEM(shape, f32) for shape in scratch],
        compiler_params=pltpu.CompilerParams(dimension_semantics=("arbitrary",)),
        cost_estimate=pl.CostEstimate(flops=10**10, bytes_accessed=2 * 10**7, transcendentals=0),
        name=name,
    )(*[x for x, _ in ins])


def to_next(x, axis, by):
    devices = lax.axis_size(axis)
    pairs_here = [(i, i + by) for i in range(devices) if 0 <= i + by < devices]
    return lax.ppermute(x, axis, pairs_here)


def around(x, by):
    devices = lax.axis_size("mp")
    return lax.ppermute(x, "mp", [(i, (i + by) % devices) for i in range(devices)])


def gather_shares(x):
    devices = lax.axis_size("mp")
    came = [x] + [around(x, by) for by in range(1, devices)]
    turned = jnp.stack([came[-k % devices] for k in range(devices)] * 2)
    at = (devices - lax.axis_index("mp")) % devices
    return lax.dynamic_slice_in_dim(turned, at, devices, 0)


def scatter_shares(x):
    devices = lax.axis_size("mp")
    here = lax.axis_index("mp")
    term = lambda at: lax.dynamic_index_in_dim(x, at % devices, 0, keepdims=False)
    total = term(here).astype(f32)
    for by in range(1, devices):
        total = total + around(term(here + by), by).astype(f32)
    return total


def mm(a, b):
    return jnp.dot(a, b, preferred_element_type=f32)


def mm_right(a, b):
    return dot(a, b, 1, 1)


def mm_left(a, b):
    return dot(a, b, 0, 0)


def statistics(values):
    center = values - jnp.mean(values, axis=-1, keepdims=True)
    scale = lax.rsqrt(jnp.mean(center * center, axis=-1, keepdims=True) + 1e-05)
    return center * scale, scale


def norm_back(grad, unit, scale, gain):
    d_unit = grad * gain
    mean = jnp.mean(d_unit, axis=-1, keepdims=True)
    along = jnp.mean(d_unit * unit, axis=-1, keepdims=True)
    return scale * (d_unit - mean - unit * along), jnp.sum(grad * unit, axis=0), jnp.sum(grad, axis=0)


def earlier(values, edge):
    return jnp.concatenate([values[1:], edge], axis=0)


def later(values, edge):
    return jnp.concatenate([edge, values[:-1]], axis=0)


def carry_states(state_map, state_add, by):
    entering = to_next(state_add.astype(bf16), "seq", by).astype(f32)
    heads = state_map.shape[1] // SPAN
    apart = lambda x: x.reshape(SPAN, heads, SPAN).transpose(1, 0, 2)
    for _ in range(lax.axis_size("seq") - 2):
        moved = jnp.einsum("hij,hjl->hil", apart(entering), apart(state_map), precision="highest")
        passed = moved.transpose(1, 0, 2).reshape(state_add.shape) + state_add
        entering = to_next(passed.astype(bf16), "seq", by).astype(f32)
    return entering


def wide(x, width):
    return jnp.pad(x, ((0, 0), (0, width - x.shape[1])))


def body(inputs, rkv_weight, output_weight, first_factors, second_factors, gate_first, gate_second,
         key_weight, value_weight, head_table, feature_table, cotangent):
    group = ("dp", "seq")
    count = lax.axis_size("dp") * lax.axis_size("seq")
    mp = lax.axis_size("mp")
    mp_here = lax.axis_index("mp")
    stream = inputs[0]
    cot = cotangent[0]
    tokens, features = stream.shape
    share = tokens // mp
    share_at = mp_here * share
    part = features // count
    width = rkv_weight.shape[2]
    heads = width // SPAN
    rank, gate_rank = first_factors.shape[2], gate_first.shape[1]
    low_width = 2 * rank + gate_rank
    lanes = max(width, low_width, part)
    up_rows, gate_rows = second_factors.shape[1], gate_second.shape[0]
    head_part = head_table.shape[2]
    edge_row = to_next(stream[-1:], "seq", 1)
    pieces = [
        wide(rkv_weight.reshape(3 * part, width), lanes),
        wide(jnp.concatenate([first_factors[0], first_factors[1], gate_first], axis=1), lanes),
        wide(second_factors.reshape(2 * up_rows, width), lanes),
        wide(gate_second, lanes),
        wide(feature_table, lanes),
        wide(head_table.reshape(7, heads * head_part), lanes),
    ]
    edges = [0]
    for piece in pieces:
        edges.append(edges[-1] + piece.shape[0])
    packed = jnp.concatenate(pieces, axis=0)
    rows_full = -(-packed.shape[0] // 16) * 16
    packed = jnp.pad(packed, ((0, rows_full - packed.shape[0]), (0, 0)))
    gathered = lax.all_gather(packed, group, axis=0, tiled=False)
    cut = lambda i, w: gathered[:, edges[i] : edges[i + 1], :w]
    up = cut(2, width).reshape(count, 2, up_rows, width).transpose(1, 0, 2, 3)
    up = jnp.concatenate(
        [up.reshape(2 * rank, width), cut(3, width).reshape(gate_rank, width)], axis=0
    )
    norms = cut(4, part).transpose(1, 0, 2).reshape(11, features).astype(f32)
    norms = jnp.pad(norms, ((0, 5), (0, 0)))
    head_rows = (
        cut(5, heads * head_part)
        .reshape(count, 7, heads, head_part)
        .transpose(1, 2, 0, 3)
        .reshape(7, width)
        .astype(f32)
    )
    head_rows = jnp.pad(head_rows, ((0, 1), (0, 0)))

    out_column = gather_shares(output_weight).reshape(features, part)
    rest = lax.all_gather(
        jnp.concatenate([value_weight, out_column], axis=0), group, axis=0, tiled=False
    )
    hidden_here = value_weight.shape[0]
    key_full = lax.all_gather(key_weight, group, axis=0, tiled=True)

    unit_one, scale_one = statistics(stream)
    edge_unit, edge_scale = statistics(edge_row)
    has_edge = (lax.axis_index("seq") > 0).astype(f32)
    edge = jnp.concatenate(
        [edge_unit, jnp.broadcast_to(has_edge, (1, features)), jnp.zeros((6, features), f32)]
    )
    slab = max(256, part)
    slabs = features // slab
    in_slabs = (1, None)
    of_gathered = (0, (1, 4 * part))
    whole = (tokens, width)
    q, kp, v, din, rin, gate, lat = run_slabs(
        project_kernel,
        "project",
        [(unit_one, in_slabs), (edge, in_slabs), (norms, in_slabs), (gathered, of_gathered), (up, None)],
        [(whole, f32, None)] * 6 + [((tokens, low_width), f32, None)],
        [(tokens, low_width)],
        slabs,
    )

    state = (SPAN, width)
    (local_out, read, push_map, push, inv, uk, qk, qr, carry, maps, adds, map_end, add_end) = run_blocks(
        local_kernel,
        "local",
        [(q, True), (kp, True), (v, True), (din, True), (rin, True), (head_rows, False)],
        [(whole, f32, True)] * 4
        + [(whole, bf16, True)] * 4
        + [((tokens // SPAN * width, width), bf16, True)]
        + [(whole, f32, True)] * 2
        + [(state, f32, False)] * 2,
        [state, state],
        tokens,
    )
    entering = carry_states(map_end, add_end, 1)
    gated, read_out, pushed, starts, ends = run_blocks(
        finish_kernel,
        "finish",
        [(x, True) for x in (q, kp, v, rin, gate)]
        + [(head_rows, False)]
        + [(x, True) for x in (local_out, read, push_map, push, maps, adds)]
        + [(entering, False)],
        [(whole, bf16, True)] + [(whole, f32, True)] * 4,
        [state],
        tokens,
    )

    gated, rest, key_full = lax.optimization_barrier((gated, rest, key_full))
    value_full = rest[:, :hidden_here].transpose(1, 0, 2).reshape(hidden_here, features)
    out_full = rest[:, hidden_here:].transpose(1, 0, 2).reshape(features, features)
    gated_all = lax.all_gather(gated, "mp", axis=0, tiled=False)
    gated_full = gated_all.transpose(1, 0, 2).reshape(tokens, features)
    middle = stream + mm(gated_full, out_full)
    unit_two, scale_two = statistics(middle)
    second_norm = unit_two * norms[2] + norms[3]
    second_diff = later(second_norm, to_next(second_norm[-1:], "seq", 1)) - second_norm
    ffn_in = (second_norm + second_diff * norms[10]).astype(bf16)
    pre_act = mm(ffn_in, key_full)
    rectified = jnp.maximum(pre_act, 0.0)
    hidden = jnp.square(rectified).astype(bf16)
    cot_low = cot.astype(bf16)
    d_pre = (mm_right(cot_low, value_full) * 2.0 * rectified).astype(bf16)
    d_ffn = mm_right(d_pre, key_full)
    d_second = d_ffn * (1.0 - norms[10]) + earlier(
        d_ffn * norms[10], to_next(d_ffn[:1] * norms[10], "seq", -1)
    )
    mu_ffn = jnp.sum(d_ffn * second_diff, axis=0)
    d_mid, gain_two, bias_two = norm_back(d_second, unit_two, scale_two, norms[2])
    d_mid_low = (d_mid + cot * (1.0 / mp)).astype(bf16)
    d_gated_parts = mm_right(d_mid_low, out_full).astype(bf16)
    d_gated_parts = d_gated_parts.reshape(tokens, mp, width).transpose(1, 0, 2)
    d_gated = lax.psum_scatter(d_gated_parts, "mp", scatter_dimension=0, tiled=False)

    ffn_out = mm(hidden, value_full).astype(bf16)
    block_out = lax.dynamic_slice_in_dim(middle, share_at, share, 0) + scatter_shares(
        ffn_out.reshape(mp, share, features)
    )
    by_part = lambda x: x.astype(bf16).reshape(x.shape[0], count, part).transpose(1, 0, 2)
    key_grad = mm_left(ffn_in, d_pre).astype(bf16)
    lots = key_grad.shape[1] // part
    key_grad = key_grad.reshape(count, part, lots, part).transpose(0, 2, 1, 3)
    large = jnp.concatenate(
        [
            by_part(mm_left(hidden, cot_low)),
            key_grad.reshape(count, lots * part, part),
            by_part(mm_left(gated_full, d_mid_low)),
        ],
        axis=1,
    )
    d_gated, large = lax.optimization_barrier((d_gated, large))
    large = lax.psum_scatter(large, group, scatter_dimension=0, tiled=False)
    value_grad = large[:hidden_here].astype(f32)
    key_grad = large[hidden_here : hidden_here + lots * part].reshape(lots, part, part)
    key_grad = key_grad.transpose(1, 0, 2).reshape(part, lots * part).astype(f32)
    out_grad = scatter_shares(large[hidden_here + lots * part :].reshape(mp, width, part))

    (d_read, dq_post, dk_post, dv_post, d_gate, back_maps, back_adds, back_map_end, back_add_end,
     row_grads_post) = run_blocks(
        reads_kernel,
        "reads",
        [(x, True) for x in (q, kp, v, rin, gate)]
        + [(head_rows, False)]
        + [(x, True) for x in (read_out, d_gated, read, carry)],
        [(whole, f32, True)] * 4
        + [(whole, bf16, True)]
        + [(whole, f32, True)] * 2
        + [(state, f32, False)] * 2
        + [((8, width), f32, False)],
        [state, state],
        tokens,
        reverse=True,
    )
    grad_in = carry_states(back_map_end, back_add_end, -1)
    dq, dkp, dv, pre, row_grads, up_grads = run_blocks(
        grads_kernel,
        "grads",
        [(x, True) for x in (q, kp, v, din, rin, lat, d_gate)]
        + [(head_rows, False), (up, False)]
        + [
            (x, True)
            for x in (pushed, inv, uk, qk, qr, starts, ends, d_read, dq_post, dk_post, dv_post,
                      back_maps, back_adds)
        ]
        + [(grad_in, False)],
        [(whole, bf16, True)] * 3
        + [((tokens, low_width), bf16, True), ((8, width), f32, False)]
        + [((low_width, width), f32, False)],
        [],
        tokens,
    )
    row_grads = jnp.concatenate([row_grads[:4], row_grads_post[4:7]], axis=0)

    scales = jnp.concatenate([scale_one, jnp.broadcast_to(edge_scale, (8, 1))], axis=0)
    packed, feature_grad, edge_fix, d_in = run_slabs(
        unproject_kernel,
        "unproject",
        [(unit_one, in_slabs), (edge, in_slabs), (scales, None), (norms, in_slabs)]
        + [(gathered, of_gathered), (dq, None), (dkp, None), (dv, None), (pre, None)],
        [
            ((count, 4 * part, lanes), bf16, (0, None)),
            ((16, features), f32, in_slabs),
            ((8, features), f32, None),
            ((tokens, features), f32, None),
        ],
        [(tokens + 8, features)] * 2 + [(8, 128)],
        slabs,
    )
    fix = to_next(edge_fix[:1], "seq", -1)
    last = lax.broadcasted_iota(jnp.int32, (tokens, 1), 0) == tokens - 1
    d_stream = d_in + d_mid + jnp.where(last, fix, 0.0)
    input_grad = lax.dynamic_slice_in_dim(cot, share_at, share, 0) + scatter_shares(
        d_stream.astype(bf16).reshape(mp, share, features)
    )

    feature_grad = jnp.concatenate(
        [feature_grad[:2], gain_two[None], bias_two[None], feature_grad[4:10], mu_ffn[None]]
    )
    split_rows = lambda x: x.reshape(count, x.shape[0] // count, x.shape[1])
    wider = lambda x: jnp.pad(x.astype(bf16), ((0, 0), (0, 0), (0, lanes - x.shape[2])))
    grads = [
        split_rows(up_grads[:rank]),
        split_rows(up_grads[rank : 2 * rank]),
        split_rows(up_grads[2 * rank :]),
        feature_grad.reshape(11, count, part).transpose(1, 0, 2),
        row_grads.reshape(7, heads, count, head_part)
        .transpose(2, 0, 1, 3)
        .reshape(count, 7, heads * head_part),
    ]
    grads = jnp.concatenate([wider(x) for x in grads], axis=1)
    grads = jnp.pad(grads, ((0, 0), (0, rows_full - 4 * part - grads.shape[1]), (0, 0)))
    grads = jnp.concatenate([packed, grads], axis=1)
    summed = lax.psum_scatter(grads, group, scatter_dimension=0, tiled=False)
    own = lambda i, w: summed[edges[i] : edges[i + 1], :w].astype(f32)
    everywhere = jnp.concatenate(
        [summed[edges[1] : edges[2]], summed[edges[4] : edges[5]]], axis=0
    )
    everywhere = jnp.sum(gather_shares(everywhere).astype(f32), axis=0)
    down_sum = everywhere[:part]
    return (
        block_out[None],
        input_grad[None],
        own(0, width).reshape(3, part, width),
        out_grad,
        jnp.stack([down_sum[:, :rank], down_sum[:, rank : 2 * rank]]),
        own(2, width).reshape(2, up_rows, width),
        down_sum[:, 2 * rank : low_width],
        own(3, width),
        key_grad,
        value_grad,
        own(5, heads * head_part).reshape(7, heads, head_part),
        everywhere[part:, :part],
    )


def solution(mesh):
    both = ("dp", "seq")
    return jax.shard_map(
        body,
        mesh=mesh,
        in_specs=(
            P("dp", "seq", None),
            P(None, both, "mp"),
            P("mp", both),
            P(None, both, None),
            P(None, both, "mp"),
            P(both, None),
            P(both, "mp"),
            P(both, "mp"),
            P("mp", both),
            P(None, "mp", both),
            P(None, both),
            P("dp", "seq", None),
        ),
        out_specs=(
            P("dp", ("seq", "mp"), None),
            P("dp", ("seq", "mp"), None),
            P(None, both, "mp"),
            P("mp", both),
            P(None, both, None),
            P(None, both, "mp"),
            P(both, None),
            P(both, "mp"),
            P(both, "mp"),
            P("mp", both),
            P(None, "mp", both),
            P(None, both),
        ),
        check_vma=False,
    )
```

time: 1830 us -> 385 us (0.21)
  matrix products: 504 us -> 23.1 us
  other arithmetic: 445 us -> 40.9 us
  waiting for transfers between devices: 526 us -> 133 us
  blocking collectives: 149 us -> 0 us
  local copies, waits for them, and re-layouts: 161 us -> 51.8 us
  Pallas kernels: 0 us -> 69 us
  starting transfers between devices: 13.2 us -> 48.5 us
    dot_general x410 -> x9, matrix products: 458 us -> 23.1 us  [the longest x6 14.2 us: dot(): lax.dot_general(a, b, (((ca,), (cb,)), ((), ())), preferred_element_type=...]
    another operation x87 -> x3, other arithmetic: 345 us -> 1.83 us  [the longest x24 164 us: block_parts(): lax.linalg.triangular_solve(system, pushed, left_side=True, lower=True, u...]
    reduce_scatter x7 -> x3, waiting for transfers between devices: 210 us -> 37.7 us  [the longest x1 37.7 us: body(): large = lax.psum_scatter(large, group, scatter_dimension=0, tiled=False)]
    unnamed x24 -> x7, waiting for transfers between devices: 173 us -> 1.21 us
    all_gather x7 -> x0, blocking collectives: 117 us -> none  [the longest x1 19.1 us: body(): lax.all_gather(output_weight, ('dp', 'seq'), axis=1, tiled=True)]
    pallas_call x0 -> x6, Pallas kernels: none -> 69 us  [the longest x4 51.4 us: run_blocks(): pl.pallas_call(functools.partial(kernel, per), grid=(steps,), in_specs=[s...]
    all_gather x5 -> x4, waiting for transfers between devices: 102 us -> 53.2 us  [the longest x1 23.4 us: body(): gated_all = lax.all_gather(gated, 'mp', axis=0, tiled=False)]
    another operation x64 -> x0, matrix products: 45.8 us -> none  [the longest x32 28.1 us: block_parts(): lax.linalg.triangular_solve(system, query_unit, left_side=True, lower=Tru...]
  transfers between devices with their start and end apart: 25 -> 28, of which waited for: 22 -> 15; matrix products, arithmetic and copies ran while one was open for 6% -> 18% of each run, Pallas kernels for 0% -> 10%
where the time goes in v1:
time: 385 us; the launch traced here: 383 us
  waiting for transfers between devices  133 us (35%)
  Pallas kernels  69 us (18%)
  local copies, waits for them, and re-layouts  51.8 us (13%)
  starting transfers between devices  48.5 us (13%)
  other arithmetic  40.9 us (11%)
  matrix products  23.1 us (6%)
  between operations  16.4 us (4%)
    pallas_call x4, Pallas kernels, run_blocks(): pl.pallas_call(functools.partial(kernel, per), grid=(steps,), in_specs=[s...  51.4 us
    reduce_scatter x1, waiting for transfers between devices, body(): large = lax.psum_scatter(large, group, scatter_dimension=0, tiled=False)  37.7 us
    ppermute x15, starting transfers between devices, around(): lax.ppermute(x, 'mp', [(i, (i + by) % devices) for i in range(devices)])  33.5 us
    ppermute x15, waiting for transfers between devices, around(): lax.ppermute(x, 'mp', [(i, (i + by) % devices) for i in range(devices)])  32.7 us
    all_gather x1, waiting for transfers between devices, body(): gated_all = lax.all_gather(gated, 'mp', axis=0, tiled=False)  23.4 us
    all_gather x1, waiting for transfers between devices, body(): lax.all_gather(jnp.concatenate([value_weight, out_column], axis=0), group...  20.6 us
    pallas_call x2, Pallas kernels, run_slabs(): pl.pallas_call(kernel, grid=(slabs,), in_specs=[spec(x.shape, cut) for x,...  17.6 us
    ppermute x6, starting transfers between devices, to_next(): return lax.ppermute(x, axis, pairs_here)  14.3 us
  transfers between devices with their start and end apart: 28, of which 15 were waited for; matrix products, arithmetic and copies ran while one was open for 18% of the time, Pallas kernels for 10%

profile of v1, /device:TPU:0, one launch (start us, length us, event | category | flops | bytes accessed | tf_op | source)
XLA Modules:
  0.0 382.7 jit_solution(16504046762502910897)
XLA Ops:
  10.6 2.4 concatenate.57
  14.6 5.1 %collective-permute-start.2 = (bf16[256,128]{1,0:T(8,128)(2,1)}, bf16[256,128]{1,0:T(8,128)(2,1)S(1)}, u32[]{:S(2)}, u32[]{:S(2)}) collective-permute-start(bf16[256,128]{1,0:T(8,128)(2,1)} %param.14), channel_id=1, source_target_pairs={{0,3},{1,0},{2,1},{3,2},{4,7},{5,4},{6,5},{7,6},{8,11},{9,8},{10,9... | collective-permute-start | bytes 196616 | tf_op jit(solution)/shard_map/ppermute | solution.py:582
  20.8 1.8 collective-permute-done.2
  22.6 3.9 %collective-permute-done.3 = bf16[256,128]{1,0:T(8,128)(2,1)S(1)} collective-permute-done((bf16[256,128]{1,0:T(8,128)(2,1)}, bf16[256,128]{1,0:T(8,128)(2,1)S(1)}, u32[]{:S(2)}, u32[]{:S(2)}) %collective-permute-start.3) | collective-permute-done | bytes 65568 | tf_op jit(solution)/shard_map/ppermute | solution.py:582
  27.5 3.4 collective-permute-start
  36.5 9.1 %all-gather.10.cloned.1.call-done = bf16[4608,256]{1,0:T(8,128)(2,1)} async-done(((bf16[576,256]{1,0:T(8,128)(2,1)}), bf16[4608,256]{1,0:T(8,128)(2,1)}) %all-gather.10.cloned.1.call-update) | async-done | bytes 2359312 | tf_op jit(solution)/shard_map/all_gather | solution.py:685
  50.3 7.9 %project.1 = (f32[512,256]{1,0:T(8,128)}, f32[512,256]{1,0:T(8,128)}, f32[512,256]{1,0:T(8,128)}, f32[512,256]{1,0:T(8,128)}, f32[512,256]{1,0:T(8,128)}, /*index=5*/f32[512,256]{1,0:T(8,128)}, f32[512,256]{1,0:T(8,128)}) custom-call(f32[512,1024]{1,0:T(8,128)} %fusion.4.unit, f32[8,1024]{1,0:T(8,128)} %maximum_maximum_fusion.edge, f32[16,1024]{1,0:T(8,128)} %pad.38.norms, ...), custom_call_target="tpu_custom_call" | custom-call | flops 10000000000 | bytes 20000000 | tf_op jit(solution)/shard_map/project/pallas_call | solution.py:561
  58.1 21.9 %local.1 = (f32[512,256]{1,0:T(8,128)}, f32[512,256]{1,0:T(8,128)}, f32[512,256]{1,0:T(8,128)}, f32[512,256]{1,0:T(8,128)}, bf16[512,256]{1,0:T(8,128)(2,1)}, /*...) custom-call(f32[512,256]{1,0:T(8,128)} %get-tuple-element.60.q, ...), custom_call_target="tpu_custom_call" | custom-call | flops 10000000000 | bytes 20000000 | tf_op jit(solution)/shard_map/local/pallas_call | solution.py:398
  80.9 3.3 collective-permute-start.1
  86.5 7.4 %finish.1 = (bf16[512,256]{1,0:T(8,128)(2,1)}, f32[512,256]{1,0:T(8,128)}, f32[512,256]{1,0:T(8,128)}, f32[512,256]{1,0:T(8,128)}, f32[512,256]{1,0:T(8,128)}) custom-call(f32[512,256]{1,0:T(8,128)} %get-tuple-element.60.q, f32[512,256]{1,0:T(8,128)} %get-tuple-element.61.kp, f32[512,256]{1,0:T(8,128)} %get-tuple-element.62.v, ...), custom_call_target="tpu_custom_call" | custom-call | flops 10000000000 | bytes 20000000 | tf_op jit(solution)/shard_map/finish/pallas_call | solution.py:398
  93.9 20.6 %all-gather.12.cloned.1.call-done = bf16[16384,128]{1,0:T(8,128)(2,1)} async-done(((bf16[2048,128]{1,0:T(8,128)(2,1)}), bf16[16384,128]{1,0:T(8,128)(2,1)}) %all-gather.12.cloned.1.call-update) | async-done | bytes 4194320 | tf_op jit(solution)/shard_map/all_gather | solution.py:703
  114.6 3.9 %slice_bitcast_fusion.1 = (bf16[1024,8,128]{2,0,1:T(8,128)(2,1)S(1)}, bf16[1024,8,128]{2,0,1:T(8,128)(2,1)}) fusion(bf16[8,2048,128]{2,1,0:T(8,128)(2,1)} %bitcast.220), kind=kLoop, calls=%fused_computation.25 | loop fusion | bytes 8388608 | tf_op jit(solution)/shard_map/transpose | solution.py:757
  118.5 2.6 copy.67
  121.1 23.4 %all-gather.14.cloned.1.call-done = bf16[2048,256]{1,0:T(8,128)(2,1)} async-done(((bf16[512,256]{1,0:T(8,128)(2,1)}), bf16[2048,256]{1,0:T(8,128)(2,1)}) %all-gather.14.cloned.1.call-update) | async-done | bytes 1048592 | tf_op jit(solution)/shard_map/all_gather | solution.py:758
  146.0 4.0 %fusion.26 = (f32[512]{0:T(512)S(1)}, f32[512,1024]{1,0:T(8,128)S(1)}) fusion(bf16[512,1024]{0,1:T(8,128)(2,1)S(1)} %bitcast.234, bf16[1024,1024]{0,1:T(8,128)(2,1)} %bitcast.227, f32[1,512,1024]{2,1,0:T(8,128)} %param.12), kind=kOutput, calls=%fused_computation.127 | convolution fusion | flops 1074789888 | bytes 7342080 | tf_op jit(solution)/shard_map/dot_general | solution.py:604
  152.1 3.5 collective-permute-start.5
  155.7 4.0 %copy.68 = bf16[1024,8,128]{0,2,1:T(8,128)(2,1)} copy(bf16[1024,8,128]{2,0,1:T(8,128)(2,1)} %get-tuple-element.150) | data formatting | bytes 4194304 | tf_op jit(solution)/shard_map/transpose | solution.py:756
  159.6 2.5 add_convert_fusion.1
  170.0 3.8 collective-permute-done.9
  173.8 2.7 multiply_reduce_fusion.1
  179.2 2.2 convolution_convert_fusion.2
  184.6 2.8 convert_bitcast_fusion
  188.2 1.9 copy.74
  191.3 2.7 convolution_convert_fusion.1
  194.0 4.0 %copy.73 = bf16[1024,8,128]{2,0,1:T(8,128)(2,1)} copy(bf16[1024,8,128]{0,2,1:T(8,128)(2,1)} %bitcast.230) | data formatting | bytes 4194304 | tf_op jit(solution)/shard_map/reshape | solution.py:785
  198.0 3.9 %convolution_convert_fusion = bf16[1024,1024]{0,1:T(8,128)(2,1)} fusion(bf16[512,1024]{0,1:T(8,128)(2,1)S(1)} %bitcast.235, bf16[512,1024]{1,0:T(8,128)(2,1)} %copy-done.14), kind=kOutput, calls=%fused_computation.29 | convolution fusion | flops 1074790400 | bytes 4194304 | tf_op jit(solution)/shard_map/dot_general | solution.py:21
  201.9 3.9 %copy.75 = bf16[1024,8,128]{2,0,1:T(8,128)(2,1)} copy(bf16[1024,8,128]{0,2,1:T(8,128)(2,1)} %bitcast.229) | data formatting | bytes 4194304 | tf_op jit(solution)/shard_map/reshape | solution.py:785
  205.8 5.9 %pad_maximum_fusion = bf16[8,3072,128]{2,1,0:T(8,128)(2,1)} fusion(bf16[8,1024,128]{2,1,0:T(8,128)(2,1)} %bitcast.219, bf16[8,1024,128]{2,1,0:T(8,128)(2,1)} %bitcast.217, bf16[8,1024,128]{2,1,0:T(8,128)(2,1)} %bitcast.218), kind=kLoop, calls=%fused_computation | loop fusion | flops 18874368 | bytes 12582912 | tf_op jit(solution)/shard_map/concatenate | solution.py:789
  211.6 7.0 %reads.1 = (f32[512,256]{1,0:T(8,128)}, f32[512,256]{1,0:T(8,128)}, f32[512,256]{1,0:T(8,128)}, f32[512,256]{1,0:T(8,128)}, bf16[512,256]{1,0:T(8,128)(2,1)}, /*...) custom-call(f32[512,256]{1,0:T(8,128)} %get-tuple-element.60.q, ...), custom_call_target="tpu_custom_call" | custom-call | flops 10000000000 | bytes 20000000 | tf_op jit(solution)/shard_map/reads/pallas_call | solution.py:398
  222.4 2.9 collective-permute-done.10
  225.9 15.1 %grads.1 = (bf16[512,256]{1,0:T(8,128)(2,1)}, bf16[512,256]{1,0:T(8,128)(2,1)}, bf16[512,256]{1,0:T(8,128)(2,1)}, bf16[512,256]{1,0:T(8,128)(2,1)}, f32[8,256]{1,0:T(8,128)}, /*index=5*/f32[256,256]{1,0:T(8,128)}) custom-call(f32[512,256]{1,0:T(8,128)} %get-tuple-element.60.q, f32[512,256]{1,0:T(8,128)} %get-tuple-element.61.kp, ...), custom_call_target="tpu_custom_call" | custom-call | flops 10000000000 | bytes 20000000 | tf_op jit(solution)/shard_map/grads/pallas_call | solution.py:398
  242.0 9.7 %unproject.1 = (bf16[8,512,256]{2,1,0:T(8,128)(2,1)}, f32[16,1024]{1,0:T(8,128)}, f32[8,1024]{1,0:T(8,128)}, f32[512,1024]{1,0:T(8,128)}) custom-call(f32[512,1024]{1,0:T(8,128)} %fusion.4.unit, f32[8,1024]{1,0:T(8,128)} %maximum_maximum_fusion.edge, f32[520,1]{1,0:T(8,128)} %concatenate.61.scales, f32[16,1024]{1,0:T(8,128)} %pad.38.norms, ...), custom_call_target="tpu_custom_call" | custom-call | flops 10000000000 | bytes 20000000 | tf_op jit(solution)/shard_map/unproject/pallas_call | solution.py:561
  254.0 3.2 fusion.1
  258.0 3.7 convolution_convert_fusion.3
  264.6 1.8 collective-permute-start.8
  270.3 3.0 collective-permute-start.14
  273.3 2.3 collective-permute-done.8
  276.3 11.2 %collective-permute-start.12 = (bf16[128,1024]{1,0:T(8,128)(2,1)}, bf16[128,1024]{1,0:T(8,128)(2,1)}, u32[]{:S(2)}, u32[]{:S(2)}) collective-permute-start(bf16[128,1024]{1,0:T(8,128)(2,1)} %get-tuple-element.154), channel_id=1, source_target_pairs={{0,1},{1,2},{2,3},{3,0},{4,5},{5,6},{6,7},{7,4},{8,9},{9,10},{10,1... | collective-permute-start | bytes 786440 | tf_op jit(solution)/shard_map/ppermute | solution.py:582
  287.5 14.3 %collective-permute-done.7 = bf16[128,1024]{1,0:T(8,128)(2,1)} collective-permute-done((bf16[128,1024]{1,0:T(8,128)(2,1)}, bf16[128,1024]{1,0:T(8,128)(2,1)}, u32[]{:S(2)}, u32[]{:S(2)}) %collective-permute-start.7) | collective-permute-done | bytes 262176 | tf_op jit(solution)/shard_map/ppermute | solution.py:582
  301.8 2.2 fusion.14
  304.0 5.5 %collective-permute-done.13 = bf16[128,1024]{1,0:T(8,128)(2,1)} collective-permute-done((bf16[128,1024]{1,0:T(8,128)(2,1)}, bf16[128,1024]{1,0:T(8,128)(2,1)}, u32[]{:S(2)}, u32[]{:S(2)}) %collective-permute-start.13) | collective-permute-done | bytes 262176 | tf_op jit(solution)/shard_map/ppermute | solution.py:582
  309.4 2.5 fusion.10
  313.6 2.8 collective-permute-start.19
  316.4 1.9 collective-permute-start.20
  325.6 37.7 %reduce-scatter.8.cloned.1.call-done = bf16[1,3072,128]{2,1,0:T(8,128)(2,1)} async-done(((bf16[8,3072,128]{2,1,0:T(8,128)(2,1)}), bf16[1,3072,128]{2,1,0:T(8,128)(2,1)}) %reduce-scatter.8.cloned.1.call-update) | async-done | bytes 786448 | tf_op jit(solution)/shard_map/reduce_scatter | solution.py:798
  363.4 2.0 fusion.17
  365.3 3.4 collective-permute-start.17
  371.2 3.9 %collective-permute-done.16 = bf16[256,128]{1,0:T(8,128)(2,1)S(1)} collective-permute-done((bf16[256,128]{1,0:T(8,128)(2,1)S(1)}, bf16[256,128]{1,0:T(8,128)(2,1)S(1)}, u32[]{:S(2)}, u32[]{:S(2)}) %collective-permute-start.16) | collective-permute-done | bytes 65568 | tf_op jit(solution)/shard_map/ppermute | solution.py:582
  (204 shorter events, 65.7 us)
Async XLA Ops:
  7.2 13.6 %copy-start.15 = (bf16[256,128]{1,0:T(8,128)(2,1)S(1)}, bf16[256,128]{1,0:T(8,128)(2,1)}, u32[]{:S(2)}) copy-start(bf16[256,128]{1,0:T(8,128)(2,1)} %param.14) | copy-start | bytes 196612
  7.2 19.4 %copy-start.16 = (bf16[1024,128]{1,0:T(8,128)(2,1)S(1)}, bf16[1024,128]{1,0:T(8,128)(2,1)}, u32[]{:S(2)}) copy-start(bf16[1024,128]{1,0:T(8,128)(2,1)} %param.20) | copy-start | bytes 786436
  7.2 38.4 %all-gather.10.cloned.1.call-start = ((), (), s32[]{:S(2)}) async-start(), calls=%async_computation.7 | async-start | bytes 2654208 | tf_op jit(solution)/shard_map/all_gather | solution.py:685
  13.0 14.4 %copy-start = (f32[1,512,1024]{2,1,0:T(8,128)S(1)}, f32[1,512,1024]{2,1,0:T(8,128)}, u32[]{:S(2)}) copy-start(f32[1,512,1024]{2,1,0:T(8,128)} %param.12) | copy-start | bytes 6291460
  13.8 80.0 %all-gather.8.cloned.1.call-start = ((), (), s32[]{:S(2)}) async-start(), calls=%async_computation.3 | async-start | bytes 2359296 | tf_op jit(solution)/shard_map/all_gather | solution.py:707
  14.6 99.9 %all-gather.12.cloned.1.call-start = ((), (), s32[]{:S(2)}) async-start(), calls=%async_computation.8 | async-start | bytes 4718592 | tf_op jit(solution)/shard_map/all_gather | solution.py:703
  14.6 7.9 %collective-permute-start.2 = (bf16[256,128]{1,0:T(8,128)(2,1)}, bf16[256,128]{1,0:T(8,128)(2,1)S(1)}, u32[]{:S(2)}, u32[]{:S(2)}) collective-permute-start(bf16[256,128]{1,0:T(8,128)(2,1)} %param.14), channel_id=1, source_target_pairs={{0,3},{1,0},{2,1},{3,2},{4,7},{5,4},{6,5},{7,6},{8,11},{9,8},{10,9... | collective-permute-start | bytes 196616 | tf_op jit(solution)/shard_map/ppermute | solution.py:582
  19.7 6.7 %collective-permute-start.3 = (bf16[256,128]{1,0:T(8,128)(2,1)}, bf16[256,128]{1,0:T(8,128)(2,1)S(1)}, u32[]{:S(2)}, u32[]{:S(2)}) collective-permute-start(bf16[256,128]{1,0:T(8,128)(2,1)} %param.14), channel_id=1, source_target_pairs={{0,2},{1,3},{2,0},{3,1},{4,6},{5,7},{6,4},{7,5},{8,10},{9,11},{10,... | collective-permute-start | bytes 196616 | tf_op jit(solution)/shard_map/ppermute | solution.py:582
  19.8 6.7 %collective-permute-start.4 = (bf16[256,128]{1,0:T(8,128)(2,1)}, bf16[256,128]{1,0:T(8,128)(2,1)S(1)}, u32[]{:S(2)}, u32[]{:S(2)}) collective-permute-start(bf16[256,128]{1,0:T(8,128)(2,1)} %param.14), channel_id=1, source_target_pairs={{0,1},{1,2},{2,3},{3,0},{4,5},{5,6},{6,7},{7,4},{8,9},{9,10},{10,1... | collective-permute-start | bytes 196616 | tf_op jit(solution)/shard_map/ppermute | solution.py:582
  27.4 117.1 %all-gather.14.cloned.1.call-start = ((), (), s32[]{:S(2)}) async-start(), calls=%async_computation.9 | async-start | bytes 1310720 | tf_op jit(solution)/shard_map/all_gather | solution.py:758
  27.5 5.7 %collective-permute-start = (f32[1,1024]{1,0:T(1,128)S(1)}, f32[1,1024]{1,0:T(1,128)S(1)}, u32[]{:S(2)}, u32[]{:S(2)}) collective-permute-start(f32[1,1024]{1,0:T(1,128)S(1)} %slice_bitcast_fusion.14), channel_id=1, source_target_pairs={{0,4},{1,5},{2,6},{3,7},{8,12},{9,13},{10,14},{11,15},{16,20},{17,... | collective-permute-start | bytes 12296 | tf_op jit(solution)/shard_map/ppermute | solution.py:577
  80.9 4.9 %collective-permute-start.1 = (bf16[64,256]{1,0:T(8,128)(2,1)S(1)}, bf16[64,256]{1,0:T(8,128)(2,1)S(1)}, u32[]{:S(2)}, u32[]{:S(2)}) collective-permute-start(bf16[64,256]{1,0:T(8,128)(2,1)S(1)} %convert_element_type.207), channel_id=1, source_target_pairs={{0,4},{1,5},{2,6},{3,7},{8,12},{9,13},{10,14},{11,15},{16,20},{17,... | collective-permute-start | bytes 98312 | tf_op jit(solution)/shard_map/ppermute | solution.py:577
  114.5 97.1 %reduce-scatter.4.cloned.1.call-start = ((), (), s32[]{:S(2)}) async-start(), calls=%async_computation.4 | async-start | bytes 1310720 | tf_op jit(solution)/shard_map/reduce_scatter | solution.py:779
  146.0 4.0 %copy-start.10 = (bf16[4,512,256]{1,2,0:T(8,128)(2,1)}, bf16[4,512,256]{1,2,0:T(8,128)(2,1)S(1)}, u32[]{:S(2)}) copy-start(bf16[4,512,256]{1,2,0:T(8,128)(2,1)S(1)} %copy.66) | copy-start | bytes 3145732
  150.8 1.3 copy-start.1
  152.1 7.5 %collective-permute-start.5 = (f32[1,1024]{1,0:T(1,128)S(1)}, f32[1,1024]{1,0:T(1,128)S(1)}, u32[]{:S(2)}, u32[]{:S(2)}) collective-permute-start(f32[1,1024]{1,0:T(1,128)S(1)} %slice.196), channel_id=1, source_target_pairs={{0,4},{1,5},{2,6},{3,7},{8,12},{9,13},{10,14},{11,15},{16,20},{17,... | collective-permute-start | bytes 12296 | tf_op jit(solution)/shard_map/ppermute | solution.py:577
  159.6 2.5 copy-start.18
  162.2 1.3 copy-start.13
  162.2 2.0 copy-start.5
  162.2 3.3 copy-start.7
  163.5 3.4 copy-start.19
  166.8 1.3 copy-start.21
  168.2 5.6 %copy-start.2 = (f32[512,1024]{1,0:T(8,128)S(1)}, f32[512,1024]{1,0:T(8,128)}, u32[]{:S(2)}) copy-start(f32[512,1024]{1,0:T(8,128)} %copy-done.1) | copy-start | bytes 6291460
  168.2 5.6 %collective-permute-start.9 = (f32[1,1024]{1,0:T(1,128)S(1)}, f32[1,1024]{1,0:T(1,128)S(1)}, u32[]{:S(2)}, u32[]{:S(2)}) collective-permute-start(f32[1,1024]{1,0:T(1,128)S(1)} %get-tuple-element.173), channel_id=1, source_target_pairs={{4,0},{5,1},{6,2},{7,3},{12,8},{13,9},{14,10},{15,11},{20,16},{21,... | collective-permute-start | bytes 12296 | tf_op jit(solution)/shard_map/ppermute | solution.py:577
  176.6 1.3 copy-start.3
  176.6 2.6 copy-start.8
  184.3 127.6 %reduce-scatter.6.cloned.1.call-start = ((), (), s32[]{:S(2)}) async-start(), calls=%async_computation.5 | async-start | bytes 2654208 | tf_op jit(solution)/shard_map/reduce_scatter | solution.py:879
  188.2 2.0 copy-start.6
  188.2 3.1 copy-start.20
  194.0 4.0 %copy-start.11 = (bf16[4,512,256]{1,2,0:T(8,128)(2,1)S(1)}, bf16[4,512,256]{1,2,0:T(8,128)(2,1)}, u32[]{:S(2)}) copy-start(bf16[4,512,256]{1,2,0:T(8,128)(2,1)} %copy-done.10) | copy-start | bytes 3145732
  219.5 5.8 %collective-permute-start.10 = (bf16[64,256]{1,0:T(8,128)(2,1)S(1)}, bf16[64,256]{1,0:T(8,128)(2,1)S(1)}, u32[]{:S(2)}, u32[]{:S(2)}) collective-permute-start(bf16[64,256]{1,0:T(8,128)(2,1)S(1)} %convert_element_type.225), channel_id=1, source_target_pairs={{4,0},{5,1},{6,2},{7,3},{12,8},{13,9},{14,10},{15,11},{20,16},{21,... | collective-permute-start | bytes 98312 | tf_op jit(solution)/shard_map/ppermute | solution.py:577
  257.2 106.2 %reduce-scatter.8.cloned.1.call-start = ((), (), s32[]{:S(2)}) async-start(), calls=%async_computation.6 | async-start | bytes 7077888 | tf_op jit(solution)/shard_map/reduce_scatter | solution.py:798
  258.0 10.3 %copy-start.4 = (f32[512,1024]{1,0:T(8,128)S(1)}, f32[512,1024]{1,0:T(8,128)}, u32[]{:S(2)}) copy-start(f32[512,1024]{1,0:T(8,128)} %copy-done.3) | copy-start | bytes 6291460
  258.0 10.3 %copy-start.9 = (f32[512,1024]{1,0:T(8,128)S(1)}, f32[512,1024]{1,0:T(8,128)}, u32[]{:S(2)}) copy-start(f32[512,1024]{1,0:T(8,128)} %get-tuple-element.100) | copy-start | bytes 6291460
  261.7 7.7 %copy-start.12 = (bf16[512,1024]{1,0:T(8,128)(2,1)}, bf16[512,1024]{1,0:T(8,128)(2,1)S(1)}, u32[]{:S(2)}) copy-start(bf16[512,1024]{1,0:T(8,128)(2,1)S(1)} %convolution_convert_fusion.3) | copy-start | bytes 3145732
  262.5 5.8 %collective-permute-start.11 = (f32[1,1024]{1,0:T(1,128)S(1)}, f32[1,1024]{1,0:T(1,128)S(1)}, u32[]{:S(2)}, u32[]{:S(2)}) collective-permute-start(f32[1,1024]{1,0:T(1,128)S(1)} %slice.167), channel_id=1, source_target_pairs={{4,0},{5,1},{6,2},{7,3},{12,8},{13,9},{14,10},{15,11},{20,16},{21,... | collective-permute-start | bytes 12296 | tf_op jit(solution)/shard_map/ppermute | solution.py:577
  264.6 11.1 %collective-permute-start.8 = (bf16[128,1024]{1,0:T(8,128)(2,1)S(1)}, bf16[128,1024]{1,0:T(8,128)(2,1)S(1)}, u32[]{:S(2)}, u32[]{:S(2)}) collective-permute-start(bf16[128,1024]{1,0:T(8,128)(2,1)S(1)} %get-tuple-element.158), channel_id=1, source_target_pairs={{0,3},{1,0},{2,1},{3,2},{4,7},{5,4},{6,5},{7,6},{8,11},{9,8},{10,9... | collective-permute-start | bytes 786440 | tf_op jit(solution)/shard_map/ppermute | solution.py:582
  266.4 35.4 %collective-permute-start.7 = (bf16[128,1024]{1,0:T(8,128)(2,1)}, bf16[128,1024]{1,0:T(8,128)(2,1)}, u32[]{:S(2)}, u32[]{:S(2)}) collective-permute-start(bf16[128,1024]{1,0:T(8,128)(2,1)} %get-tuple-element.159), channel_id=1, source_target_pairs={{0,2},{1,3},{2,0},{3,1},{4,6},{5,7},{6,4},{7,5},{8,10},{9,11},{10,... | collective-permute-start | bytes 786440 | tf_op jit(solution)/shard_map/ppermute | solution.py:582
  267.5 34.3 %collective-permute-start.6 = (bf16[128,1024]{1,0:T(8,128)(2,1)S(1)}, bf16[128,1024]{1,0:T(8,128)(2,1)}, u32[]{:S(2)}, u32[]{:S(2)}) collective-permute-start(bf16[128,1024]{1,0:T(8,128)(2,1)S(1)} %get-tuple-element.157), channel_id=1, source_target_pairs={{0,1},{1,2},{2,3},{3,0},{4,5},{5,6},{6,7},{7,4},{8,9},{9,10},{10,1... | collective-permute-start | bytes 786440 | tf_op jit(solution)/shard_map/ppermute | solution.py:582
  270.3 33.6 %collective-permute-start.14 = (bf16[128,1024]{1,0:T(8,128)(2,1)}, bf16[128,1024]{1,0:T(8,128)(2,1)}, u32[]{:S(2)}, u32[]{:S(2)}) collective-permute-start(bf16[128,1024]{1,0:T(8,128)(2,1)} %get-tuple-element.155), channel_id=1, source_target_pairs={{0,3},{1,0},{2,1},{3,2},{4,7},{5,4},{6,5},{7,6},{8,11},{9,8},{10,9... | collective-permute-start | bytes 786440 | tf_op jit(solution)/shard_map/ppermute | solution.py:582
  273.3 36.1 %collective-permute-start.13 = (bf16[128,1024]{1,0:T(8,128)(2,1)}, bf16[128,1024]{1,0:T(8,128)(2,1)}, u32[]{:S(2)}, u32[]{:S(2)}) collective-permute-start(bf16[128,1024]{1,0:T(8,128)(2,1)} %get-tuple-element.156), channel_id=1, source_target_pairs={{0,2},{1,3},{2,0},{3,1},{4,6},{5,7},{6,4},{7,5},{8,10},{9,11},{10,... | collective-permute-start | bytes 786440 | tf_op jit(solution)/shard_map/ppermute | solution.py:582
  276.3 33.1 %collective-permute-start.12 = (bf16[128,1024]{1,0:T(8,128)(2,1)}, bf16[128,1024]{1,0:T(8,128)(2,1)}, u32[]{:S(2)}, u32[]{:S(2)}) collective-permute-start(bf16[128,1024]{1,0:T(8,128)(2,1)} %get-tuple-element.154), channel_id=1, source_target_pairs={{0,1},{1,2},{2,3},{3,0},{4,5},{5,6},{6,7},{7,4},{8,9},{9,10},{10,1... | collective-permute-start | bytes 786440 | tf_op jit(solution)/shard_map/ppermute | solution.py:582
  313.5 9.3 %collective-permute-start.18 = (bf16[139,256]{1,0:T(8,128)(2,1)S(1)}, bf16[139,256]{1,0:T(8,128)(2,1)S(1)}, u32[]{:S(2)}, u32[]{:S(2)}) collective-permute-start(bf16[139,256]{1,0:T(8,128)(2,1)S(1)} %pad_maximum_fusion.4), channel_id=1, source_target_pairs={{0,3},{1,0},{2,1},{3,2},{4,7},{5,4},{6,5},{7,6},{8,11},{9,8},{10,9... | collective-permute-start | bytes 213512 | tf_op jit(solution)/shard_map/ppermute | solution.py:582
  313.6 9.8 %collective-permute-start.19 = (bf16[139,256]{1,0:T(8,128)(2,1)S(1)}, bf16[139,256]{1,0:T(8,128)(2,1)S(1)}, u32[]{:S(2)}, u32[]{:S(2)}) collective-permute-start(bf16[139,256]{1,0:T(8,128)(2,1)S(1)} %pad_maximum_fusion.4), channel_id=1, source_target_pairs={{0,2},{1,3},{2,0},{3,1},{4,6},{5,7},{6,4},{7,5},{8,10},{9,11},{10,... | collective-permute-start | bytes 213512 | tf_op jit(solution)/shard_map/ppermute | solution.py:582
  316.4 7.0 %collective-permute-start.20 = (bf16[139,256]{1,0:T(8,128)(2,1)S(1)}, bf16[139,256]{1,0:T(8,128)(2,1)S(1)}, u32[]{:S(2)}, u32[]{:S(2)}) collective-permute-start(bf16[139,256]{1,0:T(8,128)(2,1)S(1)} %pad_maximum_fusion.4), channel_id=1, source_target_pairs={{0,1},{1,2},{2,3},{3,0},{4,5},{5,6},{6,7},{7,4},{8,9},{9,10},{10,1... | collective-permute-start | bytes 213512 | tf_op jit(solution)/shard_map/ppermute | solution.py:582
  365.3 5.9 %collective-permute-start.17 = (bf16[256,128]{1,0:T(8,128)(2,1)S(1)}, bf16[256,128]{1,0:T(8,128)(2,1)S(1)}, u32[]{:S(2)}, u32[]{:S(2)}) collective-permute-start(bf16[256,128]{1,0:T(8,128)(2,1)S(1)} %get-tuple-element.166), channel_id=1, source_target_pairs={{0,3},{1,0},{2,1},{3,2},{4,7},{5,4},{6,5},{7,6},{8,11},{9,8},{10,9... | collective-permute-start | bytes 196616 | tf_op jit(solution)/shard_map/ppermute | solution.py:582
  368.8 6.4 %collective-permute-start.16 = (bf16[256,128]{1,0:T(8,128)(2,1)S(1)}, bf16[256,128]{1,0:T(8,128)(2,1)S(1)}, u32[]{:S(2)}, u32[]{:S(2)}) collective-permute-start(bf16[256,128]{1,0:T(8,128)(2,1)S(1)} %get-tuple-element.167), channel_id=1, source_target_pairs={{0,2},{1,3},{2,0},{3,1},{4,6},{5,7},{6,4},{7,5},{8,10},{9,11},{10,... | collective-permute-start | bytes 196616 | tf_op jit(solution)/shard_map/ppermute | solution.py:582
  368.8 6.4 %collective-permute-start.15 = (bf16[256,128]{1,0:T(8,128)(2,1)S(1)}, bf16[256,128]{1,0:T(8,128)(2,1)S(1)}, u32[]{:S(2)}, u32[]{:S(2)}) collective-permute-start(bf16[256,128]{1,0:T(8,128)(2,1)S(1)} %get-tuple-element.165), channel_id=1, source_target_pairs={{0,1},{1,2},{2,3},{3,0},{4,5},{5,6},{6,7},{7,4},{8,9},{9,10},{10,1... | collective-permute-start | bytes 196616 | tf_op jit(solution)/shard_map/ppermute | solution.py:582
  (2 other events, 1.7 us)
Sparse Core Ops, SparseCore 0:
  13.9 31.6 all-gather.9
  47.5 27.9 all-gather.7
  78.0 36.5 all-gather.11
  116.5 27.9 all-gather.13
  184.4 25.7 reduce-scatter.3
  257.3 40.8 reduce-scatter.5
  301.6 61.7 reduce-scatter.7

commit v2 on v1

--- a/solution.py
+++ b/solution.py
@@ -247,10 +247,14 @@
     state_now[...] = state
 
 
-def reads_kernel(per, q, kp, v, rin, gate, rows_ref, out_ref, d_gated, read, carry, d_out, dq_post,
-                 dk_post, dv_post, d_gate, maps, adds, map_end, add_end, row_grads, map_now,
-                 add_now):
+def reads_kernel(devices, per, q, kp, v, rin, gate, rows_ref, out_ref, read, carry, *refs):
+    d_gated, fixes, refs = refs[:devices], refs[devices : 2 * devices], refs[2 * devices :]
+    d_out, dq_post, dk_post, dv_post, d_gate, maps, adds, map_end, add_end, row_grads = refs[:10]
+    map_now, add_now = refs[10:]
     width = q.shape[1]
+    first_step = (pl.program_id(0) == 0).astype(f32)
+    fix = sum(x[...].astype(f32) for x in fixes)[EDGE - 1 : EDGE] * first_step
+    last_row = lax.broadcasted_iota(jnp.int32, (SPAN, width), 0) == SPAN - 1
     c = constants(width)
     rows = rows_ref[...]
     ones = c["ones"]
@@ -269,7 +273,9 @@
         rate = jax.nn.sigmoid(rows[1:2] + rin[at, :])
         k = kp[at, :] * (1.0 + (rate - 1.0) * rows[3:4])
         unit, scale, extra, summed = normed(out_ref[at, :], q_here, k, v_here, rows, c)
-        grad = d_gated[at, :].astype(f32)
+        grad = sum(x[at, :].astype(f32) for x in d_gated)
+        if i == per - 1:
+            grad = grad + jnp.where(last_row, fix, 0.0)
         d_gate[at, :] = (grad * summed).astype(bf16)
         d_sum = grad * g_here
         d_unit = d_sum * rows[5:6]
@@ -472,8 +478,9 @@
         gate[...] = dot(chosen(lane >= gate_at), up[...], 1, 0)
 
 
-def unproject_kernel(unit, edge, scales, norms, gathered, dq, dkp, dv, pre, packed, feature, edge_fix,
-                     d_in, all_first, all_unit, all_gain):
+def unproject_kernel(here, unit, edge, scales, norms, gathered, dq, dkp, dv, pre, d_mid, packed,
+                     feature, edge_fix, *rest):
+    pieces, (all_first, all_unit) = rest[:-2], rest[-2:]
     width = dq.shape[1]
     step = pl.program_id(0)
     n = norms[...]
@@ -542,13 +549,122 @@
         mean = jnp.sum(d_unit, axis=1, keepdims=True) * (1.0 / features)
         along = jnp.sum(d_unit * units, axis=1, keepdims=True) * (1.0 / features)
         result = scales[...] * (d_unit - mean - units * along)
-        d_in[...] = result[:tokens]
-        edge_fix[...] = result[tokens:]
+        edge_fix[...] = result[tokens:] + d_mid[tokens + EDGE - 8 :, :]
+        all_first[:tokens, :] = result[:tokens] + d_mid[:tokens, :]
+        send_pieces(pieces, all_first, here[0])
+
+
+EDGE = 16
+
+
+def share_of(here, by, devices, size):
+    return pl.ds(pl.multiple_of(lax.rem(here + by + devices, devices) * size, size), size)
+
+
+def send_pieces(pieces, whole, here):
+    share = pieces[0].shape[0]
+    for by, piece in enumerate(pieces):
+        piece[...] = whole[share_of(here, by, len(pieces), share), :].astype(piece.dtype)
+
+
+def channel_kernel(devices, *refs):
+    here, stream, edge_stream, has_edge, cot, norms, out_full, key, value = refs[:9]
+    gated, edges = refs[9 : 9 + devices], refs[9 + devices : 9 + 2 * devices]
+    refs = refs[9 + 2 * devices :]
+    ffn_in, hidden, d_pre, cot_low, d_mid_low, d_mid, feature, middle_share = refs[:8]
+    ffn_pieces, refs = refs[8 : 8 + devices], refs[8 + devices :]
+    grad_pieces, refs = refs[:devices], refs[devices:]
+    fix_pieces, refs = refs[:devices], refs[devices:]
+    middle, unit, scale, diff, d_ffn, ffn_out = refs
+    step = pl.program_id(0)
+    tokens, features = stream.shape
+    width = gated[0].shape[1]
+    n = norms[...]
+    flag = has_edge[0:1, 0:1]
+    row = lax.broadcasted_iota(jnp.int32, (tokens + EDGE, features), 0)
+
+    @pl.when(step == 0)
+    def _():
+        middle[:tokens, :] = stream[...]
+        middle[tokens:, :] = edge_stream[...]
+        for by in range(devices):
+            rows = out_full[share_of(here[0], -by, devices, width), :]
+            middle[:tokens, :] += dot(gated[by][...], rows, 1, 0)
+            middle[tokens:, :] += dot(edges[by][...], rows, 1, 0)
+        middle_share[...] = middle[share_of(here[0], 0, devices, tokens // devices), :]
+        values = middle[...]
+        center = values - jnp.sum(values, axis=1, keepdims=True) * (1.0 / features)
+        spread_here = jnp.sum(center * center, axis=1, keepdims=True) * (1.0 / features)
+        scale_here = lax.rsqrt(spread_here + 1e-05)
+        unit_here = center * scale_here
+        unit[...] = unit_here
+        scale[...] = scale_here
+        norm = unit_here * n[2:3] + n[3:4]
+        before = pltpu.roll(norm, 1, 0)
+        diff_here = jnp.where(row == 0, before * flag, before) - norm
+        diff[...] = diff_here
+        ffn_in[...] = (norm + diff_here * n[10:11])[:tokens].astype(bf16)
+        cot_low[...] = cot[...].astype(bf16)
+        d_ffn[...] = jnp.zeros_like(d_ffn)
+        ffn_out[...] = jnp.zeros_like(ffn_out)
+
+    act = jnp.maximum(dot(ffn_in[...], key[...], 1, 0), 0.0)
+    hidden_here = (act * act).astype(bf16)
+    hidden[...] = hidden_here
+    d_pre_here = (dot(cot_low[...], value[...], 1, 1) * 2.0 * act).astype(bf16)
+    d_pre[...] = d_pre_here
+    d_ffn[:tokens, :] += dot(d_pre_here, key[...], 1, 1)
+    ffn_out[...] += dot(hidden_here, value[...], 1, 0)
+
+    @pl.when(step == pl.num_programs(0) - 1)
+    def _():
+        send_pieces(ffn_pieces, ffn_out, here[0])
+        grad = d_ffn[...]
+        to_shift = grad * n[10:11]
+        moved = pltpu.roll(to_shift, tokens + EDGE - 1, 0)
+        d_second = grad - to_shift + jnp.where(row == tokens + EDGE - 1, moved * flag, moved)
+        unit_here = unit[...]
+        column = lambda x: jnp.sum(x, axis=0, keepdims=True)
+        feature[...] = jnp.zeros_like(feature)
+        feature[0:1, :] = column(d_second * unit_here)
+        feature[1:2, :] = column(d_second)
+        feature[2:3, :] = column(grad * diff[...])
+        d_unit = d_second * n[2:3]
+        mean = jnp.sum(d_unit, axis=1, keepdims=True) * (1.0 / features)
+        along = jnp.sum(d_unit * unit_here, axis=1, keepdims=True) * (1.0 / features)
+        d_mid_here = scale[...] * (d_unit - mean - unit_here * along)
+        d_mid[...] = d_mid_here
+        d_mid_low[tokens:, :] = d_mid_here[tokens:].astype(bf16)
+        d_mid_low[:tokens, :] = (d_mid_here[:tokens] + cot[...] * (1.0 / devices)).astype(bf16)
+        for by in range(devices):
+            rows = out_full[share_of(here[0], by, devices, width), :]
+            grad_pieces[by][...] = dot(d_mid_low[:tokens, :], rows, 1, 1).astype(bf16)
+            fix_pieces[by][...] = dot(d_mid_low[tokens:, :], rows, 1, 1).astype(bf16)
+
+
+def large_kernel(devices, *refs):
+    here, hidden, cot_low, ffn_in, d_pre, d_mid_low = refs[:6]
+    gated, edges, large = refs[6 : 6 + devices], refs[6 + devices : 6 + 2 * devices], refs[-1]
+    tokens, hidden_here = hidden.shape
+    part = large.shape[2]
+    width = gated[0].shape[1]
+    large[0, :hidden_here, :] = dot(hidden[...], cot_low[...], 0, 0).astype(bf16)
+    key_grad = dot(ffn_in[...], d_pre[...], 0, 0).astype(bf16)
+    for j in range(hidden_here // part):
+        at = hidden_here + j * part
+        large[0, at : at + part, :] = key_grad[:, j * part : (j + 1) * part]
+    grad, grad_edge = d_mid_low[:tokens, :], d_mid_low[tokens:, :]
+    for by in range(devices):
+        rows = dot(gated[by][...], grad, 0, 0) + dot(edges[by][...], grad_edge, 0, 0)
+        at = lax.rem(here[0] - by + devices, devices) * width + 2 * hidden_here
+        large[0, pl.ds(pl.multiple_of(at, width), width), :] = rows.astype(bf16)
 
 
 def run_slabs(kernel, name, ins, outs, scratch, slabs):
     def spec(shape, cut):
         shape = tuple(shape)
+        if cut == "scalar":
+            return pl.BlockSpec(memory_space=pltpu.SMEM)
         if cut is None:
             return pl.BlockSpec(shape, lambda i: (0,) * len(shape))
         dim, size = cut
@@ -667,7 +783,9 @@
     lanes = max(width, low_width, part)
     up_rows, gate_rows = second_factors.shape[1], gate_second.shape[0]
     head_part = head_table.shape[2]
-    edge_row = to_next(stream[-1:], "seq", 1)
+    here = mp_here.astype(jnp.int32).reshape(1)
+    edge_stream = to_next(stream[-EDGE:], "seq", 1)
+    edge_row = edge_stream[EDGE - 1 :]
     pieces = [
         wide(rkv_weight.reshape(3 * part, width), lanes),
         wide(jnp.concatenate([first_factors[0], first_factors[1], gate_first], axis=1), lanes),
@@ -752,62 +870,89 @@
         tokens,
     )
 
-    gated, rest, key_full = lax.optimization_barrier((gated, rest, key_full))
+    gated_parts = [gated] + [around(gated, by) for by in range(1, mp)]
+    gated_edge = to_next(gated[-EDGE:], "seq", 1)
+    edge_parts = [gated_edge] + [around(gated_edge, by) for by in range(1, mp)]
     value_full = rest[:, :hidden_here].transpose(1, 0, 2).reshape(hidden_here, features)
     out_full = rest[:, hidden_here:].transpose(1, 0, 2).reshape(features, features)
-    gated_all = lax.all_gather(gated, "mp", axis=0, tiled=False)
-    gated_full = gated_all.transpose(1, 0, 2).reshape(tokens, features)
-    middle = stream + mm(gated_full, out_full)
-    unit_two, scale_two = statistics(middle)
-    second_norm = unit_two * norms[2] + norms[3]
-    second_diff = later(second_norm, to_next(second_norm[-1:], "seq", 1)) - second_norm
-    ffn_in = (second_norm + second_diff * norms[10]).astype(bf16)
-    pre_act = mm(ffn_in, key_full)
-    rectified = jnp.maximum(pre_act, 0.0)
-    hidden = jnp.square(rectified).astype(bf16)
-    cot_low = cot.astype(bf16)
-    d_pre = (mm_right(cot_low, value_full) * 2.0 * rectified).astype(bf16)
-    d_ffn = mm_right(d_pre, key_full)
-    d_second = d_ffn * (1.0 - norms[10]) + earlier(
-        d_ffn * norms[10], to_next(d_ffn[:1] * norms[10], "seq", -1)
-    )
-    mu_ffn = jnp.sum(d_ffn * second_diff, axis=0)
-    d_mid, gain_two, bias_two = norm_back(d_second, unit_two, scale_two, norms[2])
-    d_mid_low = (d_mid + cot * (1.0 / mp)).astype(bf16)
-    d_gated_parts = mm_right(d_mid_low, out_full).astype(bf16)
-    d_gated_parts = d_gated_parts.reshape(tokens, mp, width).transpose(1, 0, 2)
-    d_gated = lax.psum_scatter(d_gated_parts, "mp", scatter_dimension=0, tiled=False)
-
-    ffn_out = mm(hidden, value_full).astype(bf16)
-    block_out = lax.dynamic_slice_in_dim(middle, share_at, share, 0) + scatter_shares(
-        ffn_out.reshape(mp, share, features)
-    )
-    by_part = lambda x: x.astype(bf16).reshape(x.shape[0], count, part).transpose(1, 0, 2)
-    key_grad = mm_left(ffn_in, d_pre).astype(bf16)
-    lots = key_grad.shape[1] // part
-    key_grad = key_grad.reshape(count, part, lots, part).transpose(0, 2, 1, 3)
-    large = jnp.concatenate(
+    longer = tokens + EDGE
+    lots = key_full.shape[1] // part
+    channel = run_slabs(
+        functools.partial(channel_kernel, mp),
+        "channel",
+        [(here, "scalar"), (stream, None), (edge_stream, None), (edge[1:2, :128], None), (cot, None)]
+        + [(norms, None), (out_full, None), (key_full, (1, None)), (value_full, (0, None))]
+        + [(x, None) for x in gated_parts + edge_parts],
         [
-            by_part(mm_left(hidden, cot_low)),
-            key_grad.reshape(count, lots * part, part),
-            by_part(mm_left(gated_full, d_mid_low)),
-        ],
-        axis=1,
-    )
-    d_gated, large = lax.optimization_barrier((d_gated, large))
+            ((tokens, features), bf16, None),
+            ((tokens, hidden_here), bf16, (1, None)),
+            ((tokens, hidden_here), bf16, (1, None)),
+            ((tokens, features), bf16, None),
+            ((longer, features), bf16, None),
+            ((longer, features), f32, None),
+            ((8, features), f32, None),
+            ((share, features), f32, None),
+        ]
+        + [((share, features), bf16, None)] * mp
+        + [(whole, bf16, None)] * mp
+        + [((EDGE, width), bf16, None)] * mp,
+        [(longer, features)] * 2
+        + [(longer, 1)]
+        + [(longer, features)] * 2
+        + [(tokens, features)],
+        max(1, hidden_here // 256),
+    )
+    ffn_in, hidden, d_pre, cot_low, d_mid_low, d_mid, second_rows, middle_share = channel[:8]
+    ffn_pieces = channel[8 : 8 + mp]
+    grad_pieces = channel[8 + mp : 8 + 2 * mp]
+    fix_pieces = channel[8 + 2 * mp :]
+    d_gated = [grad_pieces[0]] + [around(grad_pieces[by], by) for by in range(1, mp)]
+    fixes = to_next(jnp.concatenate(fix_pieces, axis=1), "seq", -1)
+    fixes = [fixes[:, by * width : (by + 1) * width] for by in range(mp)]
+    fixes = [fixes[0]] + [around(fixes[by], by) for by in range(1, mp)]
+
+    if part % 128 == 0:
+        large = run_slabs(
+            functools.partial(large_kernel, mp),
+            "large",
+            [(here, "scalar"), (hidden, None), (cot_low, (1, None)), (ffn_in, (1, None)), (d_pre, None)]
+            + [(d_mid_low, (1, None))]
+            + [(x, None) for x in gated_parts + edge_parts],
+            [((count, 2 * hidden_here + features, part), bf16, (0, None))],
+            [],
+            count,
+        )[0]
+    else:
+        by_part = lambda x: x.astype(bf16).reshape(x.shape[0], count, part).transpose(1, 0, 2)
+        key_grad = mm_left(ffn_in, d_pre).astype(bf16)
+        key_grad = key_grad.reshape(count, part, lots, part).transpose(0, 2, 1, 3)
+        order = lambda parts: jnp.concatenate(parts[:1] + parts[:0:-1], axis=0)
+        out_rows = order([mm_left(x, d_mid_low[:tokens]) for x in gated_parts]) + order(
+            [mm_left(x, d_mid_low[tokens:]) for x in edge_parts]
+        )
+        large = jnp.concatenate(
+            [
+                by_part(mm_left(hidden, cot_low)),
+                key_grad.reshape(count, lots * part, part),
+                by_part(jnp.roll(out_rows, mp_here * width, axis=0)),
+            ],
+            axis=1,
+        )
     large = lax.psum_scatter(large, group, scatter_dimension=0, tiled=False)
-    value_grad = large[:hidden_here].astype(f32)
-    key_grad = large[hidden_here : hidden_here + lots * part].reshape(lots, part, part)
-    key_grad = key_grad.transpose(1, 0, 2).reshape(part, lots * part).astype(f32)
-    out_grad = scatter_shares(large[hidden_here + lots * part :].reshape(mp, width, part))
+    block_out = middle_share + sum(
+        [ffn_pieces[0].astype(f32)]
+        + [around(ffn_pieces[by], by).astype(f32) for by in range(1, mp)]
+    )
 
     (d_read, dq_post, dk_post, dv_post, d_gate, back_maps, back_adds, back_map_end, back_add_end,
      row_grads_post) = run_blocks(
-        reads_kernel,
+        functools.partial(reads_kernel, mp),
         "reads",
         [(x, True) for x in (q, kp, v, rin, gate)]
         + [(head_rows, False)]
-        + [(x, True) for x in (read_out, d_gated, read, carry)],
+        + [(x, True) for x in (read_out, read, carry)]
+        + [(x, True) for x in d_gated]
+        + [(x, False) for x in fixes],
         [(whole, f32, True)] * 4
         + [(whole, bf16, True)]
         + [(whole, f32, True)] * 2
@@ -838,29 +983,33 @@
     row_grads = jnp.concatenate([row_grads[:4], row_grads_post[4:7]], axis=0)
 
     scales = jnp.concatenate([scale_one, jnp.broadcast_to(edge_scale, (8, 1))], axis=0)
-    packed, feature_grad, edge_fix, d_in = run_slabs(
+    unprojected = run_slabs(
         unproject_kernel,
         "unproject",
-        [(unit_one, in_slabs), (edge, in_slabs), (scales, None), (norms, in_slabs)]
-        + [(gathered, of_gathered), (dq, None), (dkp, None), (dv, None), (pre, None)],
+        [(here, "scalar"), (unit_one, in_slabs), (edge, in_slabs), (scales, None), (norms, in_slabs)]
+        + [(gathered, of_gathered), (dq, None), (dkp, None), (dv, None), (pre, None), (d_mid, None)],
         [
             ((count, 4 * part, lanes), bf16, (0, None)),
             ((16, features), f32, in_slabs),
             ((8, features), f32, None),
-            ((tokens, features), f32, None),
-        ],
-        [(tokens + 8, features)] * 2 + [(8, 128)],
+        ]
+        + [((share, features), bf16, None)] * mp,
+        [(tokens + 8, features)] * 2,
         slabs,
     )
-    fix = to_next(edge_fix[:1], "seq", -1)
-    last = lax.broadcasted_iota(jnp.int32, (tokens, 1), 0) == tokens - 1
-    d_stream = d_in + d_mid + jnp.where(last, fix, 0.0)
-    input_grad = lax.dynamic_slice_in_dim(cot, share_at, share, 0) + scatter_shares(
-        d_stream.astype(bf16).reshape(mp, share, features)
-    )
+    packed, feature_grad, edge_fix = unprojected[:3]
+    stream_pieces = unprojected[3:]
+    edge_fix = edge_fix[7:]
+    fix = jnp.sum(gather_shares(to_next(edge_fix, "seq", -1)), axis=0)
+    last = lax.broadcasted_iota(jnp.int32, (share, 1), 0) == share - 1
+    input_grad = lax.dynamic_slice_in_dim(cot, share_at, share, 0) + sum(
+        [stream_pieces[0].astype(f32)]
+        + [around(stream_pieces[by], by).astype(f32) for by in range(1, mp)]
+    )
+    input_grad = input_grad + jnp.where(last & (mp_here == mp - 1), fix, 0.0)
 
     feature_grad = jnp.concatenate(
-        [feature_grad[:2], gain_two[None], bias_two[None], feature_grad[4:10], mu_ffn[None]]
+        [feature_grad[:2], second_rows[:2], feature_grad[4:10], second_rows[2:3]]
     )
     split_rows = lambda x: x.reshape(count, x.shape[0] // count, x.shape[1])
     wider = lambda x: jnp.pad(x.astype(bf16), ((0, 0), (0, 0), (0, lanes - x.shape[2])))
@@ -876,6 +1025,11 @@
     grads = jnp.concatenate([wider(x) for x in grads], axis=1)
     grads = jnp.pad(grads, ((0, 0), (0, rows_full - 4 * part - grads.shape[1]), (0, 0)))
     grads = jnp.concatenate([packed, grads], axis=1)
+    grads, large = lax.optimization_barrier((grads, large))
+    value_grad = large[:hidden_here].astype(f32)
+    key_grad = large[hidden_here : hidden_here + lots * part].reshape(lots, part, part)
+    key_grad = key_grad.transpose(1, 0, 2).reshape(part, lots * part).astype(f32)
+    out_grad = scatter_shares(large[hidden_here + lots * part :].reshape(mp, width, part))
     summed = lax.psum_scatter(grads, group, scatter_dimension=0, tiled=False)
     own = lambda i, w: summed[edges[i] : edges[i + 1], :w].astype(f32)
     everywhere = jnp.concatenate(

time: 385 us -> 321 us (0.83)
  waiting for transfers between devices: 133 us -> 73 us
  Pallas kernels: 69 us -> 101 us
  starting transfers between devices: 48.5 us -> 74.3 us
  matrix products: 23.1 us -> 0 us
  local copies, waits for them, and re-layouts: 51.8 us -> 31.4 us
  other arithmetic: 40.9 us -> 23.1 us
    reduce_scatter x1, waiting for transfers between devices: 37.7 us -> 0.02 us  [body(): large = lax.psum_scatter(large, group, scatter_dimension=0, tiled=False)]
    pallas_call x2 -> x4, Pallas kernels: 17.6 us -> 49.4 us  [run_slabs(): pl.pallas_call(kernel, grid=(slabs,), in_specs=[spec(x.shape, cut) for x,...]
    ppermute x15 -> x30, starting transfers between devices: 33.5 us -> 59.2 us  [around(): lax.ppermute(x, 'mp', [(i, (i + by) % devices) for i in range(devices)])]
    all_gather x1 -> x0, waiting for transfers between devices: 23.4 us -> none  [body(): gated_all = lax.all_gather(gated, 'mp', axis=0, tiled=False)]
    dot_general x9 -> x0, matrix products: 23.1 us -> none  [the longest x6 14.2 us: dot(): lax.dot_general(a, b, (((ca,), (cb,)), ((), ())), preferred_element_type=...]
    ppermute x15 -> x30, waiting for transfers between devices: 32.7 us -> 53.5 us  [around(): lax.ppermute(x, 'mp', [(i, (i + by) % devices) for i in range(devices)])]
    all_gather x1, waiting for transfers between devices: 20.6 us -> 0.01 us  [body(): lax.all_gather(jnp.concatenate([value_weight, out_column], axis=0), group...]
    transpose x5 -> x0, local copies, waits for them, and re-layouts: 12.5 us -> none  [the longest x2 6.49 us: body(): rest[:, hidden_here:].transpose(1, 0, 2).reshape(features, features)]
  transfers between devices with their start and end apart: 28 -> 41, of which waited for: 15 -> 15; matrix products, arithmetic and copies ran while one was open for 18% -> 13% of each run, Pallas kernels for 10% -> 22%
where the time goes in v2:
time: 321 us; the launch traced here: 319 us
  Pallas kernels  101 us (31%)
  starting transfers between devices  74.3 us (23%)
  waiting for transfers between devices  73 us (23%)
  local copies, waits for them, and re-layouts  31.4 us (10%)
  other arithmetic  23.1 us (7%)
  between operations  16 us (5%)
    ppermute x30, starting transfers between devices, around(): lax.ppermute(x, 'mp', [(i, (i + by) % devices) for i in range(devices)])  59.2 us
    ppermute x30, waiting for transfers between devices, around(): lax.ppermute(x, 'mp', [(i, (i + by) % devices) for i in range(devices)])  53.5 us
    pallas_call x4, Pallas kernels, run_blocks(): pl.pallas_call(functools.partial(kernel, per), grid=(steps,), in_specs=[s...  51.6 us
    pallas_call x4, Pallas kernels, run_slabs(): pl.pallas_call(kernel, grid=(slabs,), in_specs=[spec(x.shape, cut) for x,...  49.4 us
    ppermute x6, starting transfers between devices, to_next(): return lax.ppermute(x, axis, pairs_here)  14.9 us
    all_gather x1, waiting for transfers between devices, body(): gathered = lax.all_gather(packed, group, axis=0, tiled=False)  10.4 us
    ppermute x6, waiting for transfers between devices, to_next(): return lax.ppermute(x, axis, pairs_here)  9.01 us
    unnamed x88, local copies, waits for them, and re-layouts  7.3 us
  transfers between devices with their start and end apart: 41, of which 15 were waited for; matrix products, arithmetic and copies ran while one was open for 13% of the time, Pallas kernels for 22%

profile of v2, /device:TPU:0, one launch (start us, length us, event | category | flops | bytes accessed | tf_op | source)
XLA Modules:
  0.0 318.9 jit_solution(3230535374926598871)
XLA Ops:
  10.6 2.4 concatenate.39
  13.9 5.1 %collective-permute-start.1 = (bf16[256,128]{1,0:T(8,128)(2,1)}, bf16[256,128]{1,0:T(8,128)(2,1)S(1)}, u32[]{:S(2)}, u32[]{:S(2)}) collective-permute-start(bf16[256,128]{1,0:T(8,128)(2,1)} %param.14), channel_id=1, source_target_pairs={{0,3},{1,0},{2,1},{3,2},{4,7},{5,4},{6,5},{7,6},{8,11},{9,8},{10,9... | collective-permute-start | bytes 196616 | tf_op jit(solution)/shard_map/ppermute | solution.py:698
  21.8 3.9 %collective-permute-done.2 = bf16[256,128]{1,0:T(8,128)(2,1)S(1)} collective-permute-done((bf16[256,128]{1,0:T(8,128)(2,1)}, bf16[256,128]{1,0:T(8,128)(2,1)S(1)}, u32[]{:S(2)}, u32[]{:S(2)}) %collective-permute-start.2) | collective-permute-done | bytes 65568 | tf_op jit(solution)/shard_map/ppermute | solution.py:698
  26.8 3.4 %collective-permute-start = (f32[16,1024]{1,0:T(8,128)S(1)}, f32[16,1024]{1,0:T(8,128)S(1)}, u32[]{:S(2)}, u32[]{:S(2)}) collective-permute-start(f32[16,1024]{1,0:T(8,128)S(1)} %slice_bitcast_fusion.4), channel_id=1, source_target_pairs={{0,4},{1,5},{2,6},{3,7},{8,12},{9,13},{10,14},{11,15},{16,20},{17,... | collective-permute-start | bytes 196616 | tf_op jit(solution)/shard_map/ppermute | solution.py:693
  30.8 1.7 subtract_multiply_fusion.unit
  35.9 10.4 %all-gather.8.cloned.1.call-done = bf16[4608,256]{1,0:T(8,128)(2,1)} async-done(((bf16[576,256]{1,0:T(8,128)(2,1)}), bf16[4608,256]{1,0:T(8,128)(2,1)}) %all-gather.8.cloned.1.call-update) | async-done | bytes 2359312 | tf_op jit(solution)/shard_map/all_gather | solution.py:803
  50.9 7.9 %project.1 = (f32[512,256]{1,0:T(8,128)}, f32[512,256]{1,0:T(8,128)}, f32[512,256]{1,0:T(8,128)}, f32[512,256]{1,0:T(8,128)}, f32[512,256]{1,0:T(8,128)}, /*index=5*/f32[512,256]{1,0:T(8,128)}, f32[512,256]{1,0:T(8,128)}) custom-call(f32[512,1024]{1,0:T(8,128)} %subtract_multiply_fusion.unit, f32[8,1024]{1,0:T(8,128)} %maximum_maximum_fusion.edge, ...), custom_call_target="tpu_custom_call" | custom-call | flops 10000000000 | bytes 20000000 | tf_op jit(solution)/shard_map/project/pallas_call | solution.py:677
  58.9 22.0 %local.1 = (f32[512,256]{1,0:T(8,128)}, f32[512,256]{1,0:T(8,128)}, f32[512,256]{1,0:T(8,128)}, f32[512,256]{1,0:T(8,128)}, bf16[512,256]{1,0:T(8,128)(2,1)}, /*...) custom-call(f32[512,256]{1,0:T(8,128)} %get-tuple-element.80.q, ...), custom_call_target="tpu_custom_call" | custom-call | flops 10000000000 | bytes 20000000 | tf_op jit(solution)/shard_map/local/pallas_call | solution.py:404
  81.7 3.2 %collective-permute-start.4 = (bf16[64,256]{1,0:T(8,128)(2,1)S(1)}, bf16[64,256]{1,0:T(8,128)(2,1)S(1)}, u32[]{:S(2)}, u32[]{:S(2)}) collective-permute-start(bf16[64,256]{1,0:T(8,128)(2,1)S(1)} %convert_element_type.161), channel_id=1, source_target_pairs={{0,4},{1,5},{2,6},{3,7},{8,12},{9,13},{10,14},{11,15},{16,20},{17,... | collective-permute-start | bytes 98312 | tf_op jit(solution)/shard_map/ppermute | solution.py:693
  84.9 1.6 collective-permute-done.4
  87.1 7.4 %finish.1 = (bf16[512,256]{1,0:T(8,128)(2,1)}, f32[512,256]{1,0:T(8,128)}, f32[512,256]{1,0:T(8,128)}, f32[512,256]{1,0:T(8,128)}, f32[512,256]{1,0:T(8,128)}) custom-call(f32[512,256]{1,0:T(8,128)} %get-tuple-element.80.q, f32[512,256]{1,0:T(8,128)} %get-tuple-element.81.kp, f32[512,256]{1,0:T(8,128)} %get-tuple-element.82.v, ...), custom_call_target="tpu_custom_call" | custom-call | flops 10000000000 | bytes 20000000 | tf_op jit(solution)/shard_map/finish/pallas_call | solution.py:404
  95.2 4.2 %collective-permute-start.8 = (bf16[16,256]{1,0:T(8,128)(2,1)S(1)}, bf16[16,256]{1,0:T(8,128)(2,1)S(1)}, u32[]{:S(2)}, u32[]{:S(2)}) collective-permute-start(bf16[16,256]{1,0:T(8,128)(2,1)S(1)} %slice.154), channel_id=1, source_target_pairs={{0,4},{1,5},{2,6},{3,7},{8,12},{9,13},{10,14},{11,15},{16,20},{17,... | collective-permute-start | bytes 24584 | tf_op jit(solution)/shard_map/ppermute | solution.py:693
  99.4 1.5 collective-permute-start.5
  100.9 2.4 collective-permute-start.6
  103.4 1.4 collective-permute-start.7
  105.3 2.4 collective-permute-start.11
  107.7 2.5 fusion.8
  110.3 1.4 copy.64
  111.7 1.4 copy.65
  113.0 12.9 %collective-permute-done.10.refs_15_.refs_12_ = bf16[16,256]{1,0:T(8,128)(2,1)S(1)} collective-permute-done((bf16[16,256]{1,0:T(8,128)(2,1)S(1)}, bf16[16,256]{1,0:T(8,128)(2,1)S(1)}, u32[]{:S(2)}, u32[]{:S(2)}) %collective-permute-start.10) | collective-permute-done | bytes 8224 | tf_op jit(solution)/shard_map/ppermute | solution.py:698
  125.9 3.3 %copy_bitcast_fusion = (bf16[1024,1024]{1,0:T(8,128)(2,1)}, bf16[1024,1024]{1,0:T(8,128)(2,1)}) fusion(bf16[128,8,8,128]{3,2,1,0:T(8,128)(2,1)S(1)} %bitcast.136, bf16[128,8,8,128]{3,2,1,0:T(8,128)(2,1)S(1)} %bitcast.135), kind=kLoop, calls=%fused_computation.3 | loop fusion | bytes 8388608 | tf_op jit(solution)/shard_map/reshape | solution.py:876
  129.2 2.1 collective-permute-done.9.refs_14_.refs_11_
  132.2 19.2 %channel.1 = (bf16[512,1024]{1,0:T(8,128)(2,1)}, bf16[512,1024]{1,0:T(8,128)(2,1)}, bf16[512,1024]{1,0:T(8,128)(2,1)}, bf16[512,1024]{1,0:T(8,128)(2,1)}, bf16[5...) custom-call(s32[1]{0:T(128)} %bitcast.refs_0_.here, ...), custom_call_target="tpu_custom_call" | custom-call | flops 10000000000 | bytes 20000000 | tf_op jit(solution)/shard_map/channel/pallas_call | solution.py:677
  151.5 11.9 %large.1 = bf16[8,3072,128]{2,1,0:T(8,128)(2,1)} custom-call(s32[1]{0:T(128)} %bitcast.refs_0_.here, bf16[512,1024]{1,0:T(8,128)(2,1)} %get-tuple-element.141.refs_1_, bf16[512,1024]{1,0:T(8,128)(2,1)} %get-tuple-element.142.refs_2_, bf16[512,1024]{1,0:T(8,128)(2,1)} %get-tuple-element.143.refs_3_, bf16[512,1024]{1,0:T(8,128)(2,1)} %get-tuple-element.144.refs_4_, ...), custom_call_target="tpu_custom_call" | custom-call | flops 10000000000 | bytes 20000000 | tf_op jit(solution)/shard_map/large/pallas_call | solution.py:677
  165.5 2.3 collective-permute-start.16
  167.8 1.6 collective-permute-start.17
  170.5 2.3 collective-permute-start.20
  172.8 12.8 %collective-permute-done.19.refs_5_ = bf16[16,256]{1,0:T(8,128)(2,1)S(1)} collective-permute-done((bf16[16,256]{1,0:T(8,128)(2,1)S(1)}, bf16[16,256]{1,0:T(8,128)(2,1)S(1)}, u32[]{:S(2)}, u32[]{:S(2)}) %collective-permute-start.19) | collective-permute-done | bytes 8224 | tf_op jit(solution)/shard_map/ppermute | solution.py:698
  185.7 5.2 %collective-permute-done.20.refs_6_ = bf16[16,256]{1,0:T(8,128)(2,1)S(1)} collective-permute-done((bf16[16,256]{1,0:T(8,128)(2,1)S(1)}, bf16[16,256]{1,0:T(8,128)(2,1)S(1)}, u32[]{:S(2)}, u32[]{:S(2)}) %collective-permute-start.20) | collective-permute-done | bytes 8224 | tf_op jit(solution)/shard_map/ppermute | solution.py:698
  191.8 7.1 %reads.1 = (f32[512,256]{1,0:T(8,128)}, f32[512,256]{1,0:T(8,128)}, f32[512,256]{1,0:T(8,128)}, f32[512,256]{1,0:T(8,128)}, bf16[512,256]{1,0:T(8,128)(2,1)}, /*...) custom-call(f32[512,256]{1,0:T(8,128)} %get-tuple-element.80.q, ...), custom_call_target="tpu_custom_call" | custom-call | flops 10000000000 | bytes 20000000 | tf_op jit(solution)/shard_map/reads/pallas_call | solution.py:404
  199.7 1.5 collective-permute-start.22
  202.9 2.7 collective-permute-done.22
  206.2 15.1 %grads.1 = (bf16[512,256]{1,0:T(8,128)(2,1)}, bf16[512,256]{1,0:T(8,128)(2,1)}, bf16[512,256]{1,0:T(8,128)(2,1)}, bf16[512,256]{1,0:T(8,128)(2,1)}, f32[8,256]{1,0:T(8,128)}, /*index=5*/f32[256,256]{1,0:T(8,128)}) custom-call(f32[512,256]{1,0:T(8,128)} %get-tuple-element.80.q, f32[512,256]{1,0:T(8,128)} %get-tuple-element.81.kp, ...), custom_call_target="tpu_custom_call" | custom-call | flops 10000000000 | bytes 20000000 | tf_op jit(solution)/shard_map/grads/pallas_call | solution.py:404
  221.3 10.4 %unproject.1 = (bf16[8,512,256]{2,1,0:T(8,128)(2,1)}, f32[16,1024]{1,0:T(8,128)}, f32[8,1024]{1,0:T(8,128)}, bf16[128,1024]{1,0:T(8,128)(2,1)}, bf16[128,1024]{1...) custom-call(s32[1]{0:T(128)} %bitcast.refs_0_.here, f32[512,1024]{1,0:T(8,128)} %subtract_multiply_fusion.unit, ...), custom_call_target="tpu_custom_call" | custom-call | flops 10000000000 | bytes 20000000 | tf_op jit(solution)/shard_map/unproject/pallas_call | solution.py:677
  233.9 3.2 %fusion.1 = bf16[8,576,256]{2,1,0:T(8,128)(2,1)} fusion(bf16[8,50,256]{2,1,0:T(8,128)(2,1)S(1)} %concatenate.47, bf16[8,512,256]{2,1,0:T(8,128)(2,1)} %get-tuple-element.135), kind=kLoop, calls=%fused_computation.2 | loop fusion | flops 7077888 | bytes 4661248 | tf_op jit(solution)/shard_map/concatenate | solution.py:1027
  238.8 1.9 collective-permute-start.13
  240.7 2.4 collective-permute-start.14
  245.2 4.2 %collective-permute-done.26 = f32[1,1024]{1,0:T(1,128)S(1)} collective-permute-done((f32[1,1024]{1,0:T(1,128)S(1)}, f32[1,1024]{1,0:T(1,128)S(1)}, u32[]{:S(2)}, u32[]{:S(2)}) %collective-permute-start.26) | collective-permute-done | bytes 4128 | tf_op jit(solution)/shard_map/ppermute | solution.py:693
  249.5 1.9 collective-permute-start.23
  251.4 9.3 %collective-permute-start.24 = (bf16[128,1024]{1,0:T(8,128)(2,1)}, bf16[128,1024]{1,0:T(8,128)(2,1)S(1)}, u32[]{:S(2)}, u32[]{:S(2)}) collective-permute-start(bf16[128,1024]{1,0:T(8,128)(2,1)} %get-tuple-element.132), channel_id=1, source_target_pairs={{0,2},{1,3},{2,0},{3,1},{4,6},{5,7},{6,4},{7,5},{8,10},{9,11},{10,... | collective-permute-start | bytes 786440 | tf_op jit(solution)/shard_map/ppermute | solution.py:698
  260.7 14.9 %collective-permute-start.25 = (bf16[128,1024]{1,0:T(8,128)(2,1)}, bf16[128,1024]{1,0:T(8,128)(2,1)S(1)}, u32[]{:S(2)}, u32[]{:S(2)}) collective-permute-start(bf16[128,1024]{1,0:T(8,128)(2,1)} %get-tuple-element.133), channel_id=1, source_target_pairs={{0,3},{1,0},{2,1},{3,2},{4,7},{5,4},{6,5},{7,6},{8,11},{9,8},{10,9... | collective-permute-start | bytes 786440 | tf_op jit(solution)/shard_map/ppermute | solution.py:698
  277.2 9.6 %collective-permute-done.28 = f32[1,1024]{1,0:T(1,128)S(1)} collective-permute-done((f32[1,1024]{1,0:T(1,128)S(1)}, f32[1,1024]{1,0:T(1,128)S(1)}, u32[]{:S(2)}, u32[]{:S(2)}) %collective-permute-start.28) | collective-permute-done | bytes 4128 | tf_op jit(solution)/shard_map/ppermute | solution.py:698
  287.0 2.0 fusion.3
  290.6 3.2 %collective-permute-start.32 = (bf16[256,128]{1,0:T(8,128)(2,1)S(1)}, bf16[256,128]{1,0:T(8,128)(2,1)S(1)}, u32[]{:S(2)}, u32[]{:S(2)}) collective-permute-start(bf16[256,128]{1,0:T(8,128)(2,1)S(1)} %get-tuple-element.194), channel_id=1, source_target_pairs={{0,3},{1,0},{2,1},{3,2},{4,7},{5,4},{6,5},{7,6},{8,11},{9,8},{10,9... | collective-permute-start | bytes 196616 | tf_op jit(solution)/shard_map/ppermute | solution.py:698
  294.6 2.1 collective-permute-done.30
  296.7 1.7 collective-permute-done.31
  300.6 1.8 collective-permute-start.33
  307.8 2.4 collective-permute-done.34
  (232 shorter events, 45.8 us)
Async XLA Ops:
  7.2 18.7 %copy-start.5 = (bf16[1024,128]{1,0:T(8,128)(2,1)S(1)}, bf16[1024,128]{1,0:T(8,128)(2,1)}, u32[]{:S(2)}) copy-start(bf16[1024,128]{1,0:T(8,128)(2,1)} %param.20) | copy-start | bytes 786436
  7.2 39.1 %all-gather.8.cloned.1.call-start = ((), (), s32[]{:S(2)}) async-start(), calls=%async_computation.5 | async-start | bytes 2654208 | tf_op jit(solution)/shard_map/all_gather | solution.py:803
  13.8 93.9 %all-gather.10.cloned.1.call-start = ((), (), s32[]{:S(2)}) async-start(), calls=%async_computation.6 | async-start | bytes 4718592 | tf_op jit(solution)/shard_map/all_gather | solution.py:821
  13.9 7.9 %collective-permute-start.1 = (bf16[256,128]{1,0:T(8,128)(2,1)}, bf16[256,128]{1,0:T(8,128)(2,1)S(1)}, u32[]{:S(2)}, u32[]{:S(2)}) collective-permute-start(bf16[256,128]{1,0:T(8,128)(2,1)} %param.14), channel_id=1, source_target_pairs={{0,3},{1,0},{2,1},{3,2},{4,7},{5,4},{6,5},{7,6},{8,11},{9,8},{10,9... | collective-permute-start | bytes 196616 | tf_op jit(solution)/shard_map/ppermute | solution.py:698
  19.0 6.7 %collective-permute-start.2 = (bf16[256,128]{1,0:T(8,128)(2,1)}, bf16[256,128]{1,0:T(8,128)(2,1)S(1)}, u32[]{:S(2)}, u32[]{:S(2)}) collective-permute-start(bf16[256,128]{1,0:T(8,128)(2,1)} %param.14), channel_id=1, source_target_pairs={{0,2},{1,3},{2,0},{3,1},{4,6},{5,7},{6,4},{7,5},{8,10},{9,11},{10,... | collective-permute-start | bytes 196616 | tf_op jit(solution)/shard_map/ppermute | solution.py:698
  19.0 6.7 %collective-permute-start.3 = (bf16[256,128]{1,0:T(8,128)(2,1)}, bf16[256,128]{1,0:T(8,128)(2,1)S(1)}, u32[]{:S(2)}, u32[]{:S(2)}) collective-permute-start(bf16[256,128]{1,0:T(8,128)(2,1)} %param.14), channel_id=1, source_target_pairs={{0,1},{1,2},{2,3},{3,0},{4,5},{5,6},{6,7},{7,4},{8,9},{9,10},{10,1... | collective-permute-start | bytes 196616 | tf_op jit(solution)/shard_map/ppermute | solution.py:698
  26.7 102.5 %all-gather.6.cloned.1.call-start = ((), (), s32[]{:S(2)}) async-start(), calls=%async_computation.2 | async-start | bytes 2359296 | tf_op jit(solution)/shard_map/all_gather | solution.py:825
  26.8 5.9 %collective-permute-start = (f32[16,1024]{1,0:T(8,128)S(1)}, f32[16,1024]{1,0:T(8,128)S(1)}, u32[]{:S(2)}, u32[]{:S(2)}) collective-permute-start(f32[16,1024]{1,0:T(8,128)S(1)} %slice_bitcast_fusion.4), channel_id=1, source_target_pairs={{0,4},{1,5},{2,6},{3,7},{8,12},{9,13},{10,14},{11,15},{16,20},{17,... | collective-permute-start | bytes 196616 | tf_op jit(solution)/shard_map/ppermute | solution.py:693
  30.2 206.9 %reduce-scatter.3.cloned.1.call-start = ((), (), s32[]{:S(2)}) async-start(), calls=%async_computation.3 | async-start | bytes 7077888 | tf_op jit(solution)/shard_map/reduce_scatter | solution.py:941
  32.7 26.2 %copy-start.14 = (f32[16,1024]{1,0:T(8,128)}, f32[16,1024]{1,0:T(8,128)S(1)}, u32[]{:S(2)}) copy-start(f32[16,1024]{1,0:T(8,128)S(1)} %collective-permute-done.refs_2_) | copy-start | bytes 196612
  81.7 4.8 %collective-permute-start.4 = (bf16[64,256]{1,0:T(8,128)(2,1)S(1)}, bf16[64,256]{1,0:T(8,128)(2,1)S(1)}, u32[]{:S(2)}, u32[]{:S(2)}) collective-permute-start(bf16[64,256]{1,0:T(8,128)(2,1)S(1)} %convert_element_type.161), channel_id=1, source_target_pairs={{0,4},{1,5},{2,6},{3,7},{8,12},{9,13},{10,14},{11,15},{16,20},{17,... | collective-permute-start | bytes 98312 | tf_op jit(solution)/shard_map/ppermute | solution.py:693
  95.2 9.6 %collective-permute-start.8 = (bf16[16,256]{1,0:T(8,128)(2,1)S(1)}, bf16[16,256]{1,0:T(8,128)(2,1)S(1)}, u32[]{:S(2)}, u32[]{:S(2)}) collective-permute-start(bf16[16,256]{1,0:T(8,128)(2,1)S(1)} %slice.154), channel_id=1, source_target_pairs={{0,4},{1,5},{2,6},{3,7},{8,12},{9,13},{10,14},{11,15},{16,20},{17,... | collective-permute-start | bytes 24584 | tf_op jit(solution)/shard_map/ppermute | solution.py:693
  99.4 31.9 %collective-permute-start.5 = (bf16[512,256]{1,0:T(8,128)(2,1)}, bf16[512,256]{1,0:T(8,128)(2,1)S(1)}, u32[]{:S(2)}, u32[]{:S(2)}) collective-permute-start(bf16[512,256]{1,0:T(8,128)(2,1)} %get-tuple-element.93.refs_9_.refs_6_), channel_id=1, source_target_pairs={{0,1},{1,2},{2,3},{3,0},{4,5},{5,6},{6,7},{7,4},{8,9},{9,10},{10,1... | collective-permute-start | bytes 786440 | tf_op jit(solution)/shard_map/ppermute | solution.py:698
  100.9 30.4 %collective-permute-start.6 = (bf16[512,256]{1,0:T(8,128)(2,1)}, bf16[512,256]{1,0:T(8,128)(2,1)S(1)}, u32[]{:S(2)}, u32[]{:S(2)}) collective-permute-start(bf16[512,256]{1,0:T(8,128)(2,1)} %get-tuple-element.93.refs_9_.refs_6_), channel_id=1, source_target_pairs={{0,2},{1,3},{2,0},{3,1},{4,6},{5,7},{6,4},{7,5},{8,10},{9,11},{10,... | collective-permute-start | bytes 786440 | tf_op jit(solution)/shard_map/ppermute | solution.py:698
  103.4 28.0 %collective-permute-start.7 = (bf16[512,256]{1,0:T(8,128)(2,1)}, bf16[512,256]{1,0:T(8,128)(2,1)S(1)}, u32[]{:S(2)}, u32[]{:S(2)}) collective-permute-start(bf16[512,256]{1,0:T(8,128)(2,1)} %get-tuple-element.93.refs_9_.refs_6_), channel_id=1, source_target_pairs={{0,3},{1,0},{2,1},{3,2},{4,7},{5,4},{6,5},{7,6},{8,11},{9,8},{10,9... | collective-permute-start | bytes 786440 | tf_op jit(solution)/shard_map/ppermute | solution.py:698
  104.8 21.1 %copy-start.27 = (bf16[16,256]{1,0:T(8,128)(2,1)}, bf16[16,256]{1,0:T(8,128)(2,1)S(1)}, u32[]{:S(2)}) copy-start(bf16[16,256]{1,0:T(8,128)(2,1)S(1)} %collective-permute-done.8.refs_13_.refs_10_) | copy-start | bytes 24580
  104.8 21.1 %collective-permute-start.10 = (bf16[16,256]{1,0:T(8,128)(2,1)S(1)}, bf16[16,256]{1,0:T(8,128)(2,1)S(1)}, u32[]{:S(2)}, u32[]{:S(2)}) collective-permute-start(bf16[16,256]{1,0:T(8,128)(2,1)S(1)} %collective-permute-done.8.refs_13_.refs_10_), channel_id=1, source_target_pairs={{0,2},{1,3},{2,0},{3,1},{4,6},{5,7},{6,4},{7,5},{8,10},{9,11},{10,... | collective-permute-start | bytes 24584 | tf_op jit(solution)/shard_map/ppermute | solution.py:698
  105.3 23.9 %collective-permute-start.11 = (bf16[16,256]{1,0:T(8,128)(2,1)S(1)}, bf16[16,256]{1,0:T(8,128)(2,1)S(1)}, u32[]{:S(2)}, u32[]{:S(2)}) collective-permute-start(bf16[16,256]{1,0:T(8,128)(2,1)S(1)} %collective-permute-done.8.refs_13_.refs_10_), channel_id=1, source_target_pairs={{0,3},{1,0},{2,1},{3,2},{4,7},{5,4},{6,5},{7,6},{8,11},{9,8},{10,9... | collective-permute-start | bytes 24584 | tf_op jit(solution)/shard_map/ppermute | solution.py:698
  125.9 5.5 %collective-permute-start.9 = (bf16[16,256]{1,0:T(8,128)(2,1)S(1)}, bf16[16,256]{1,0:T(8,128)(2,1)S(1)}, u32[]{:S(2)}, u32[]{:S(2)}) collective-permute-start(bf16[16,256]{1,0:T(8,128)(2,1)S(1)} %collective-permute-done.8.refs_13_.refs_10_), channel_id=1, source_target_pairs={{0,1},{1,2},{2,3},{3,0},{4,5},{5,6},{6,7},{7,4},{8,9},{9,10},{10,1... | collective-permute-start | bytes 24584 | tf_op jit(solution)/shard_map/ppermute | solution.py:698
  163.5 135.6 %reduce-scatter.5.cloned.1.call-start = ((), (), s32[]{:S(2)}) async-start(), calls=%async_computation.4 | async-start | bytes 2654208 | tf_op jit(solution)/shard_map/reduce_scatter | solution.py:1033
  164.1 5.8 %collective-permute-start.18 = (bf16[16,1024]{1,0:T(8,128)(2,1)S(1)}, bf16[16,1024]{1,0:T(8,128)(2,1)S(1)}, u32[]{:S(2)}, u32[]{:S(2)}) collective-permute-start(bf16[16,1024]{1,0:T(8,128)(2,1)S(1)} %pad_maximum_fusion.5), channel_id=1, source_target_pairs={{4,0},{5,1},{6,2},{7,3},{12,8},{13,9},{14,10},{15,11},{20,16},{21,... | collective-permute-start | bytes 98312 | tf_op jit(solution)/shard_map/ppermute | solution.py:693
  165.4 25.4 %collective-permute-start.15 = (bf16[512,256]{1,0:T(8,128)(2,1)S(1)}, bf16[512,256]{1,0:T(8,128)(2,1)S(1)}, u32[]{:S(2)}, u32[]{:S(2)}) collective-permute-start(bf16[512,256]{1,0:T(8,128)(2,1)S(1)} %copy-done.21), channel_id=1, source_target_pairs={{0,1},{1,2},{2,3},{3,0},{4,5},{5,6},{6,7},{7,4},{8,9},{9,10},{10,1... | collective-permute-start | bytes 786440 | tf_op jit(solution)/shard_map/ppermute | solution.py:698
  165.5 25.4 %collective-permute-start.16 = (bf16[512,256]{1,0:T(8,128)(2,1)S(1)}, bf16[512,256]{1,0:T(8,128)(2,1)S(1)}, u32[]{:S(2)}, u32[]{:S(2)}) collective-permute-start(bf16[512,256]{1,0:T(8,128)(2,1)S(1)} %copy-done.19), channel_id=1, source_target_pairs={{0,2},{1,3},{2,0},{3,1},{4,6},{5,7},{6,4},{7,5},{8,10},{9,11},{10,... | collective-permute-start | bytes 786440 | tf_op jit(solution)/shard_map/ppermute | solution.py:698
  167.8 23.1 %collective-permute-start.17 = (bf16[512,256]{1,0:T(8,128)(2,1)S(1)}, bf16[512,256]{1,0:T(8,128)(2,1)S(1)}, u32[]{:S(2)}, u32[]{:S(2)}) collective-permute-start(bf16[512,256]{1,0:T(8,128)(2,1)S(1)} %copy-done.18), channel_id=1, source_target_pairs={{0,3},{1,0},{2,1},{3,2},{4,7},{5,4},{6,5},{7,6},{8,11},{9,8},{10,9... | collective-permute-start | bytes 786440 | tf_op jit(solution)/shard_map/ppermute | solution.py:698
  170.5 15.1 %collective-permute-start.19 = (bf16[16,256]{1,0:T(8,128)(2,1)S(1)}, bf16[16,256]{1,0:T(8,128)(2,1)S(1)}, u32[]{:S(2)}, u32[]{:S(2)}) collective-permute-start(bf16[16,256]{1,0:T(8,128)(2,1)S(1)} %get-tuple-element.202), channel_id=1, source_target_pairs={{0,1},{1,2},{2,3},{3,0},{4,5},{5,6},{6,7},{7,4},{8,9},{9,10},{10,1... | collective-permute-start | bytes 24584 | tf_op jit(solution)/shard_map/ppermute | solution.py:698
  170.5 20.3 %collective-permute-start.20 = (bf16[16,256]{1,0:T(8,128)(2,1)S(1)}, bf16[16,256]{1,0:T(8,128)(2,1)S(1)}, u32[]{:S(2)}, u32[]{:S(2)}) collective-permute-start(bf16[16,256]{1,0:T(8,128)(2,1)S(1)} %get-tuple-element.201), channel_id=1, source_target_pairs={{0,2},{1,3},{2,0},{3,1},{4,6},{5,7},{6,4},{7,5},{8,10},{9,11},{10,... | collective-permute-start | bytes 24584 | tf_op jit(solution)/shard_map/ppermute | solution.py:698
  185.7 5.2 %collective-permute-start.21 = (bf16[16,256]{1,0:T(8,128)(2,1)S(1)}, bf16[16,256]{1,0:T(8,128)(2,1)S(1)}, u32[]{:S(2)}, u32[]{:S(2)}) collective-permute-start(bf16[16,256]{1,0:T(8,128)(2,1)S(1)} %get-tuple-element.200), channel_id=1, source_target_pairs={{0,3},{1,0},{2,1},{3,2},{4,7},{5,4},{6,5},{7,6},{8,11},{9,8},{10,9... | collective-permute-start | bytes 24584 | tf_op jit(solution)/shard_map/ppermute | solution.py:698
  199.7 5.8 %collective-permute-start.22 = (bf16[64,256]{1,0:T(8,128)(2,1)S(1)}, bf16[64,256]{1,0:T(8,128)(2,1)S(1)}, u32[]{:S(2)}, u32[]{:S(2)}) collective-permute-start(bf16[64,256]{1,0:T(8,128)(2,1)S(1)} %convert_element_type.167), channel_id=1, source_target_pairs={{4,0},{5,1},{6,2},{7,3},{12,8},{13,9},{14,10},{15,11},{20,16},{21,... | collective-permute-start | bytes 98312 | tf_op jit(solution)/shard_map/ppermute | solution.py:693
  202.1 19.1 %copy-start.8 = (bf16[8,1024]{1,0:T(8,128)(2,1)}, bf16[8,1024]{1,0:T(8,128)(2,1)S(1)}, u32[]{:S(2)}) copy-start(bf16[8,1024]{1,0:T(8,128)(2,1)S(1)} %convert.44) | copy-start | bytes 49156
  237.1 39.1 %copy-start.2 = (f32[128,1024]{1,0:T(8,128)S(1)}, f32[128,1024]{1,0:T(8,128)}, u32[]{:S(2)}) copy-start(f32[128,1024]{1,0:T(8,128)} %get-tuple-element.94) | copy-start | bytes 1572868
  237.1 39.1 %copy-start.6 = (bf16[128,1024]{1,0:T(8,128)(2,1)S(1)}, bf16[128,1024]{1,0:T(8,128)(2,1)}, u32[]{:S(2)}) copy-start(bf16[128,1024]{1,0:T(8,128)(2,1)} %get-tuple-element.95) | copy-start | bytes 786436
  237.2 49.8 %copy-start.7 = (bf16[128,1024]{1,0:T(8,128)(2,1)S(1)}, bf16[128,1024]{1,0:T(8,128)(2,1)}, u32[]{:S(2)}) copy-start(bf16[128,1024]{1,0:T(8,128)(2,1)} %get-tuple-element.130) | copy-start | bytes 786436
  238.1 13.4 %collective-permute-start.12 = (bf16[128,1024]{1,0:T(8,128)(2,1)S(1)}, bf16[128,1024]{1,0:T(8,128)(2,1)S(1)}, u32[]{:S(2)}, u32[]{:S(2)}) collective-permute-start(bf16[128,1024]{1,0:T(8,128)(2,1)S(1)} %copy-done.17), channel_id=1, source_target_pairs={{0,1},{1,2},{2,3},{3,0},{4,5},{5,6},{6,7},{7,4},{8,9},{9,10},{10,1... | collective-permute-start | bytes 786440 | tf_op jit(solution)/shard_map/ppermute | solution.py:698
  238.8 21.9 %collective-permute-start.13 = (bf16[128,1024]{1,0:T(8,128)(2,1)S(1)}, bf16[128,1024]{1,0:T(8,128)(2,1)S(1)}, u32[]{:S(2)}, u32[]{:S(2)}) collective-permute-start(bf16[128,1024]{1,0:T(8,128)(2,1)S(1)} %copy-done.16), channel_id=1, source_target_pairs={{0,2},{1,3},{2,0},{3,1},{4,6},{5,7},{6,4},{7,5},{8,10},{9,11},{10,... | collective-permute-start | bytes 786440 | tf_op jit(solution)/shard_map/ppermute | solution.py:698
  240.7 35.0 %collective-permute-start.14 = (bf16[128,1024]{1,0:T(8,128)(2,1)S(1)}, bf16[128,1024]{1,0:T(8,128)(2,1)S(1)}, u32[]{:S(2)}, u32[]{:S(2)}) collective-permute-start(bf16[128,1024]{1,0:T(8,128)(2,1)S(1)} %copy-done.15), channel_id=1, source_target_pairs={{0,3},{1,0},{2,1},{3,2},{4,7},{5,4},{6,5},{7,6},{8,11},{9,8},{10,9... | collective-permute-start | bytes 786440 | tf_op jit(solution)/shard_map/ppermute | solution.py:698
  243.9 5.5 %collective-permute-start.26 = (f32[1,1024]{1,0:T(1,128)S(1)}, f32[1,1024]{1,0:T(1,128)S(1)}, u32[]{:S(2)}, u32[]{:S(2)}) collective-permute-start(f32[1,1024]{1,0:T(1,128)S(1)} %slice.159), channel_id=1, source_target_pairs={{4,0},{5,1},{6,2},{7,3},{12,8},{13,9},{14,10},{15,11},{20,16},{21,... | collective-permute-start | bytes 12296 | tf_op jit(solution)/shard_map/ppermute | solution.py:693
  249.4 26.3 %collective-permute-start.27 = (f32[1,1024]{1,0:T(1,128)S(1)}, f32[1,1024]{1,0:T(1,128)S(1)}, u32[]{:S(2)}, u32[]{:S(2)}) collective-permute-start(f32[1,1024]{1,0:T(1,128)S(1)} %collective-permute-done.26), channel_id=1, source_target_pairs={{0,3},{1,0},{2,1},{3,2},{4,7},{5,4},{6,5},{7,6},{8,11},{9,8},{10,9... | collective-permute-start | bytes 12296 | tf_op jit(solution)/shard_map/ppermute | solution.py:698
  249.5 37.4 %collective-permute-start.23 = (bf16[128,1024]{1,0:T(8,128)(2,1)}, bf16[128,1024]{1,0:T(8,128)(2,1)S(1)}, u32[]{:S(2)}, u32[]{:S(2)}) collective-permute-start(bf16[128,1024]{1,0:T(8,128)(2,1)} %get-tuple-element.131), channel_id=1, source_target_pairs={{0,1},{1,2},{2,3},{3,0},{4,5},{5,6},{6,7},{7,4},{8,9},{9,10},{10,1... | collective-permute-start | bytes 786440 | tf_op jit(solution)/shard_map/ppermute | solution.py:698
  251.4 35.5 %collective-permute-start.24 = (bf16[128,1024]{1,0:T(8,128)(2,1)}, bf16[128,1024]{1,0:T(8,128)(2,1)S(1)}, u32[]{:S(2)}, u32[]{:S(2)}) collective-permute-start(bf16[128,1024]{1,0:T(8,128)(2,1)} %get-tuple-element.132), channel_id=1, source_target_pairs={{0,2},{1,3},{2,0},{3,1},{4,6},{5,7},{6,4},{7,5},{8,10},{9,11},{10,... | collective-permute-start | bytes 786440 | tf_op jit(solution)/shard_map/ppermute | solution.py:698
  260.7 26.2 %collective-permute-start.25 = (bf16[128,1024]{1,0:T(8,128)(2,1)}, bf16[128,1024]{1,0:T(8,128)(2,1)S(1)}, u32[]{:S(2)}, u32[]{:S(2)}) collective-permute-start(bf16[128,1024]{1,0:T(8,128)(2,1)} %get-tuple-element.133), channel_id=1, source_target_pairs={{0,3},{1,0},{2,1},{3,2},{4,7},{5,4},{6,5},{7,6},{8,11},{9,8},{10,9... | collective-permute-start | bytes 786440 | tf_op jit(solution)/shard_map/ppermute | solution.py:698
  275.7 11.2 %collective-permute-start.28 = (f32[1,1024]{1,0:T(1,128)S(1)}, f32[1,1024]{1,0:T(1,128)S(1)}, u32[]{:S(2)}, u32[]{:S(2)}) collective-permute-start(f32[1,1024]{1,0:T(1,128)S(1)} %collective-permute-done.26), channel_id=1, source_target_pairs={{0,2},{1,3},{2,0},{3,1},{4,6},{5,7},{6,4},{7,5},{8,10},{9,11},{10,... | collective-permute-start | bytes 12296 | tf_op jit(solution)/shard_map/ppermute | solution.py:698
  275.7 11.2 %collective-permute-start.29 = (f32[1,1024]{1,0:T(1,128)S(1)}, f32[1,1024]{1,0:T(1,128)S(1)}, u32[]{:S(2)}, u32[]{:S(2)}) collective-permute-start(f32[1,1024]{1,0:T(1,128)S(1)} %collective-permute-done.26), channel_id=1, source_target_pairs={{0,1},{1,2},{2,3},{3,0},{4,5},{5,6},{6,7},{7,4},{8,9},{9,10},{10,1... | collective-permute-start | bytes 12296 | tf_op jit(solution)/shard_map/ppermute | solution.py:698
  289.9 6.8 %collective-permute-start.30 = (bf16[256,128]{1,0:T(8,128)(2,1)S(1)}, bf16[256,128]{1,0:T(8,128)(2,1)S(1)}, u32[]{:S(2)}, u32[]{:S(2)}) collective-permute-start(bf16[256,128]{1,0:T(8,128)(2,1)S(1)} %get-tuple-element.193), channel_id=1, source_target_pairs={{0,1},{1,2},{2,3},{3,0},{4,5},{5,6},{6,7},{7,4},{8,9},{9,10},{10,1... | collective-permute-start | bytes 196616 | tf_op jit(solution)/shard_map/ppermute | solution.py:698
  290.3 8.0 %collective-permute-start.31 = (bf16[256,128]{1,0:T(8,128)(2,1)S(1)}, bf16[256,128]{1,0:T(8,128)(2,1)S(1)}, u32[]{:S(2)}, u32[]{:S(2)}) collective-permute-start(bf16[256,128]{1,0:T(8,128)(2,1)S(1)} %get-tuple-element.195), channel_id=1, source_target_pairs={{0,2},{1,3},{2,0},{3,1},{4,6},{5,7},{6,4},{7,5},{8,10},{9,11},{10,... | collective-permute-start | bytes 196616 | tf_op jit(solution)/shard_map/ppermute | solution.py:698
  290.6 7.8 %collective-permute-start.32 = (bf16[256,128]{1,0:T(8,128)(2,1)S(1)}, bf16[256,128]{1,0:T(8,128)(2,1)S(1)}, u32[]{:S(2)}, u32[]{:S(2)}) collective-permute-start(bf16[256,128]{1,0:T(8,128)(2,1)S(1)} %get-tuple-element.194), channel_id=1, source_target_pairs={{0,3},{1,0},{2,1},{3,2},{4,7},{5,4},{6,5},{7,6},{8,11},{9,8},{10,9... | collective-permute-start | bytes 196616 | tf_op jit(solution)/shard_map/ppermute | solution.py:698
  300.6 7.2 %collective-permute-start.33 = (bf16[139,256]{1,0:T(8,128)(2,1)S(1)}, bf16[139,256]{1,0:T(8,128)(2,1)S(1)}, u32[]{:S(2)}, u32[]{:S(2)}) collective-permute-start(bf16[139,256]{1,0:T(8,128)(2,1)S(1)} %pad_maximum_fusion.3), channel_id=1, source_target_pairs={{0,3},{1,0},{2,1},{3,2},{4,7},{5,4},{6,5},{7,6},{8,11},{9,8},{10,9... | collective-permute-start | bytes 213512 | tf_op jit(solution)/shard_map/ppermute | solution.py:698
  302.5 7.7 %collective-permute-start.34 = (bf16[139,256]{1,0:T(8,128)(2,1)S(1)}, bf16[139,256]{1,0:T(8,128)(2,1)S(1)}, u32[]{:S(2)}, u32[]{:S(2)}) collective-permute-start(bf16[139,256]{1,0:T(8,128)(2,1)S(1)} %pad_maximum_fusion.3), channel_id=1, source_target_pairs={{0,2},{1,3},{2,0},{3,1},{4,6},{5,7},{6,4},{7,5},{8,10},{9,11},{10,... | collective-permute-start | bytes 213512 | tf_op jit(solution)/shard_map/ppermute | solution.py:698
  303.4 6.8 %collective-permute-start.35 = (bf16[139,256]{1,0:T(8,128)(2,1)S(1)}, bf16[139,256]{1,0:T(8,128)(2,1)S(1)}, u32[]{:S(2)}, u32[]{:S(2)}) collective-permute-start(bf16[139,256]{1,0:T(8,128)(2,1)S(1)} %pad_maximum_fusion.3), channel_id=1, source_target_pairs={{0,1},{1,2},{2,3},{3,0},{4,5},{5,6},{6,7},{7,4},{8,9},{9,10},{10,1... | collective-permute-start | bytes 213512 | tf_op jit(solution)/shard_map/ppermute | solution.py:698
  (28 other events, 115.6 us)
Sparse Core Ops, SparseCore 0:
  13.9 32.3 all-gather.7
  48.8 36.5 all-gather.9
  87.2 27.9 all-gather.5
  163.6 60.0 reduce-scatter.2
  237.3 40.7 reduce-scatter.4

commit v3 on v2

--- a/solution.py
+++ b/solution.py
@@ -6,6 +6,7 @@
 from jax.experimental import pallas as pl
 from jax.experimental.pallas import tpu as pltpu
 from jax.sharding import PartitionSpec as P
+
 
 SPAN = 64
 f32 = jnp.float32
@@ -388,7 +389,7 @@
         row_grads[3:4, :] += column(d_k * kp_here * (rate - 1.0))
 
 
-def run_blocks(kernel, name, ins, outs, scratch, tokens, reverse=False):
+def run_blocks(kernel, ins, outs, scratch, tokens, reverse=False):
     count = tokens // SPAN
     per = blocks_per_step(count)
     steps = count // per
@@ -410,7 +411,6 @@
         scratch_shapes=[pltpu.VMEM(shape, f32) for shape in scratch],
         compiler_params=pltpu.CompilerParams(dimension_semantics=("arbitrary",)),
         cost_estimate=pl.CostEstimate(flops=10**10, bytes_accessed=2 * 10**7, transcendentals=0),
-        name=name,
     )(*[x for x, _ in ins])
 
 
@@ -660,7 +660,7 @@
         large[0, pl.ds(pl.multiple_of(at, width), width), :] = rows.astype(bf16)
 
 
-def run_slabs(kernel, name, ins, outs, scratch, slabs):
+def run_slabs(kernel, ins, outs, scratch, slabs):
     def spec(shape, cut):
         shape = tuple(shape)
         if cut == "scalar":
@@ -683,7 +683,6 @@
         scratch_shapes=[pltpu.VMEM(shape, f32) for shape in scratch],
         compiler_params=pltpu.CompilerParams(dimension_semantics=("arbitrary",)),
         cost_estimate=pl.CostEstimate(flops=10**10, bytes_accessed=2 * 10**7, transcendentals=0),
-        name=name,
     )(*[x for x, _ in ins])
 
 
@@ -696,6 +695,17 @@
 def around(x, by):
     devices = lax.axis_size("mp")
     return lax.ppermute(x, "mp", [(i, (i + by) % devices) for i in range(devices)])
+
+
+def slanted(x, along, by):
+    rows, devices = lax.axis_size("seq"), lax.axis_size("mp")
+    pairs_here = [
+        (s * devices + i, (s + along) * devices + (i + by) % devices)
+        for s in range(rows)
+        if 0 <= s + along < rows
+        for i in range(devices)
+    ]
+    return lax.ppermute(x, ("seq", "mp"), pairs_here)
 
 
 def gather_shares(x):
@@ -716,14 +726,6 @@
     return total
 
 
-def mm(a, b):
-    return jnp.dot(a, b, preferred_element_type=f32)
-
-
-def mm_right(a, b):
-    return dot(a, b, 1, 1)
-
-
 def mm_left(a, b):
     return dot(a, b, 0, 0)
 
@@ -732,21 +734,6 @@
     center = values - jnp.mean(values, axis=-1, keepdims=True)
     scale = lax.rsqrt(jnp.mean(center * center, axis=-1, keepdims=True) + 1e-05)
     return center * scale, scale
-
-
-def norm_back(grad, unit, scale, gain):
-    d_unit = grad * gain
-    mean = jnp.mean(d_unit, axis=-1, keepdims=True)
-    along = jnp.mean(d_unit * unit, axis=-1, keepdims=True)
-    return scale * (d_unit - mean - unit * along), jnp.sum(grad * unit, axis=0), jnp.sum(grad, axis=0)
-
-
-def earlier(values, edge):
-    return jnp.concatenate([values[1:], edge], axis=0)
-
-
-def later(values, edge):
-    return jnp.concatenate([edge, values[:-1]], axis=0)
 
 
 def carry_states(state_map, state_add, by):
@@ -781,7 +768,7 @@
     rank, gate_rank = first_factors.shape[2], gate_first.shape[1]
     low_width = 2 * rank + gate_rank
     lanes = max(width, low_width, part)
-    up_rows, gate_rows = second_factors.shape[1], gate_second.shape[0]
+    up_rows = second_factors.shape[1]
     head_part = head_table.shape[2]
     here = mp_here.astype(jnp.int32).reshape(1)
     edge_stream = to_next(stream[-EDGE:], "seq", 1)
@@ -837,7 +824,6 @@
     whole = (tokens, width)
     q, kp, v, din, rin, gate, lat = run_slabs(
         project_kernel,
-        "project",
         [(unit_one, in_slabs), (edge, in_slabs), (norms, in_slabs), (gathered, of_gathered), (up, None)],
         [(whole, f32, None)] * 6 + [((tokens, low_width), f32, None)],
         [(tokens, low_width)],
@@ -847,7 +833,6 @@
     state = (SPAN, width)
     (local_out, read, push_map, push, inv, uk, qk, qr, carry, maps, adds, map_end, add_end) = run_blocks(
         local_kernel,
-        "local",
         [(q, True), (kp, True), (v, True), (din, True), (rin, True), (head_rows, False)],
         [(whole, f32, True)] * 4
         + [(whole, bf16, True)] * 4
@@ -860,7 +845,6 @@
     entering = carry_states(map_end, add_end, 1)
     gated, read_out, pushed, starts, ends = run_blocks(
         finish_kernel,
-        "finish",
         [(x, True) for x in (q, kp, v, rin, gate)]
         + [(head_rows, False)]
         + [(x, True) for x in (local_out, read, push_map, push, maps, adds)]
@@ -870,16 +854,14 @@
         tokens,
     )
 
+    edge_parts = [slanted(gated[-EDGE:], 1, by) for by in range(mp)]
     gated_parts = [gated] + [around(gated, by) for by in range(1, mp)]
-    gated_edge = to_next(gated[-EDGE:], "seq", 1)
-    edge_parts = [gated_edge] + [around(gated_edge, by) for by in range(1, mp)]
     value_full = rest[:, :hidden_here].transpose(1, 0, 2).reshape(hidden_here, features)
     out_full = rest[:, hidden_here:].transpose(1, 0, 2).reshape(features, features)
     longer = tokens + EDGE
     lots = key_full.shape[1] // part
     channel = run_slabs(
         functools.partial(channel_kernel, mp),
-        "channel",
         [(here, "scalar"), (stream, None), (edge_stream, None), (edge[1:2, :128], None), (cot, None)]
         + [(norms, None), (out_full, None), (key_full, (1, None)), (value_full, (0, None))]
         + [(x, None) for x in gated_parts + edge_parts],
@@ -906,15 +888,14 @@
     ffn_pieces = channel[8 : 8 + mp]
     grad_pieces = channel[8 + mp : 8 + 2 * mp]
     fix_pieces = channel[8 + 2 * mp :]
-    d_gated = [grad_pieces[0]] + [around(grad_pieces[by], by) for by in range(1, mp)]
-    fixes = to_next(jnp.concatenate(fix_pieces, axis=1), "seq", -1)
-    fixes = [fixes[:, by * width : (by + 1) * width] for by in range(mp)]
-    fixes = [fixes[0]] + [around(fixes[by], by) for by in range(1, mp)]
+    fixes = [slanted(fix_pieces[by], -1, by) for by in range(mp)]
+    d_gated = [grad_pieces[0]]
+    for by in range(1, mp):
+        d_gated.append(around(grad_pieces[by], by))
 
     if part % 128 == 0:
         large = run_slabs(
             functools.partial(large_kernel, mp),
-            "large",
             [(here, "scalar"), (hidden, None), (cot_low, (1, None)), (ffn_in, (1, None)), (d_pre, None)]
             + [(d_mid_low, (1, None))]
             + [(x, None) for x in gated_parts + edge_parts],
@@ -939,15 +920,15 @@
             axis=1,
         )
     large = lax.psum_scatter(large, group, scatter_dimension=0, tiled=False)
-    block_out = middle_share + sum(
-        [ffn_pieces[0].astype(f32)]
-        + [around(ffn_pieces[by], by).astype(f32) for by in range(1, mp)]
-    )
+    d_gated, ffn_pieces = lax.optimization_barrier((d_gated, ffn_pieces))
+    block_out = middle_share + ffn_pieces[0].astype(f32)
+    for by in range(1, mp):
+        came = around(ffn_pieces[by], by)
+        block_out = block_out + came.astype(f32)
 
     (d_read, dq_post, dk_post, dv_post, d_gate, back_maps, back_adds, back_map_end, back_add_end,
      row_grads_post) = run_blocks(
         functools.partial(reads_kernel, mp),
-        "reads",
         [(x, True) for x in (q, kp, v, rin, gate)]
         + [(head_rows, False)]
         + [(x, True) for x in (read_out, read, carry)]
@@ -965,7 +946,6 @@
     grad_in = carry_states(back_map_end, back_add_end, -1)
     dq, dkp, dv, pre, row_grads, up_grads = run_blocks(
         grads_kernel,
-        "grads",
         [(x, True) for x in (q, kp, v, din, rin, lat, d_gate)]
         + [(head_rows, False), (up, False)]
         + [
@@ -985,7 +965,6 @@
     scales = jnp.concatenate([scale_one, jnp.broadcast_to(edge_scale, (8, 1))], axis=0)
     unprojected = run_slabs(
         unproject_kernel,
-        "unproject",
         [(here, "scalar"), (unit_one, in_slabs), (edge, in_slabs), (scales, None), (norms, in_slabs)]
         + [(gathered, of_gathered), (dq, None), (dkp, None), (dv, None), (pre, None), (d_mid, None)],
         [
@@ -999,14 +978,7 @@
     )
     packed, feature_grad, edge_fix = unprojected[:3]
     stream_pieces = unprojected[3:]
-    edge_fix = edge_fix[7:]
-    fix = jnp.sum(gather_shares(to_next(edge_fix, "seq", -1)), axis=0)
-    last = lax.broadcasted_iota(jnp.int32, (share, 1), 0) == share - 1
-    input_grad = lax.dynamic_slice_in_dim(cot, share_at, share, 0) + sum(
-        [stream_pieces[0].astype(f32)]
-        + [around(stream_pieces[by], by).astype(f32) for by in range(1, mp)]
-    )
-    input_grad = input_grad + jnp.where(last & (mp_here == mp - 1), fix, 0.0)
+    fix = to_next(edge_fix[7:].astype(bf16), "seq", -1)
 
     feature_grad = jnp.concatenate(
         [feature_grad[:2], second_rows[:2], feature_grad[4:10], second_rows[2:3]]
@@ -1026,17 +998,29 @@
     grads = jnp.pad(grads, ((0, 0), (0, rows_full - 4 * part - grads.shape[1]), (0, 0)))
     grads = jnp.concatenate([packed, grads], axis=1)
     grads, large = lax.optimization_barrier((grads, large))
+    out_grad = scatter_shares(large[hidden_here + lots * part :].reshape(mp, width, part))
     value_grad = large[:hidden_here].astype(f32)
     key_grad = large[hidden_here : hidden_here + lots * part].reshape(lots, part, part)
     key_grad = key_grad.transpose(1, 0, 2).reshape(part, lots * part).astype(f32)
-    out_grad = scatter_shares(large[hidden_here + lots * part :].reshape(mp, width, part))
     summed = lax.psum_scatter(grads, group, scatter_dimension=0, tiled=False)
+    input_grad = lax.dynamic_slice_in_dim(cot, share_at, share, 0) + sum(
+        [stream_pieces[0].astype(f32)]
+        + [around(stream_pieces[by], by).astype(f32) for by in range(1, mp)]
+    )
+    summed, input_grad, out_grad, block_out = lax.optimization_barrier(
+        (summed, input_grad, out_grad, block_out)
+    )
     own = lambda i, w: summed[edges[i] : edges[i + 1], :w].astype(f32)
+    fix_rows = features // lanes
     everywhere = jnp.concatenate(
-        [summed[edges[1] : edges[2]], summed[edges[4] : edges[5]]], axis=0
+        [summed[edges[1] : edges[2]], summed[edges[4] : edges[5]], fix.reshape(fix_rows, lanes)],
+        axis=0,
     )
     everywhere = jnp.sum(gather_shares(everywhere).astype(f32), axis=0)
     down_sum = everywhere[:part]
+    fix = everywhere[part + 11 :].reshape(1, features)
+    last = lax.broadcasted_iota(jnp.int32, (share, 1), 0) == share - 1
+    input_grad = input_grad + jnp.where(last & (mp_here == mp - 1), fix, 0.0)
     return (
         block_out[None],
         input_grad[None],
@@ -1049,7 +1033,7 @@
         key_grad,
         value_grad,
         own(5, heads * head_part).reshape(7, heads, head_part),
-        everywhere[part:, :part],
+        everywhere[part : part + 11, :part],
     )
 
 

time: 321 us -> 313 us (0.975)
  waiting for transfers between devices: 73 us -> 68.2 us
    ppermute x0 -> x8, starting transfers between devices: none -> 13.4 us  [slanted(): return lax.ppermute(x, ('seq', 'mp'), pairs_here)]
    ppermute x30 -> x21, starting transfers between devices: 59.2 us -> 48.8 us  [around(): lax.ppermute(x, 'mp', [(i, (i + by) % devices) for i in range(devices)])]
    ppermute x30 -> x21, waiting for transfers between devices: 53.5 us -> 45.1 us  [around(): lax.ppermute(x, 'mp', [(i, (i + by) % devices) for i in range(devices)])]
    ppermute x0 -> x8, waiting for transfers between devices: none -> 6.16 us  [slanted(): return lax.ppermute(x, ('seq', 'mp'), pairs_here)]
    ppermute x6 -> x4, starting transfers between devices: 14.9 us -> 9.43 us  [to_next(): return lax.ppermute(x, axis, pairs_here)]
    ppermute x6 -> x4, waiting for transfers between devices: 9.01 us -> 6.32 us  [to_next(): return lax.ppermute(x, axis, pairs_here)]
    unnamed x88 -> x95, local copies, waits for them, and re-layouts: 7.3 us -> 7.24 us
  transfers between devices with their start and end apart: 41 -> 38, of which waited for: 15 -> 16; matrix products, arithmetic and copies ran while one was open for 13% -> 13% of each run, Pallas kernels for 22% -> 22%
where the time goes in v3:
time: 313 us; the launch traced here: 311 us
  Pallas kernels  101 us (32%)
  starting transfers between devices  71.8 us (23%)
  waiting for transfers between devices  68.2 us (22%)
  local copies, waits for them, and re-layouts  30.8 us (10%)
  other arithmetic  23.2 us (7%)
  between operations  16.1 us (5%)
    pallas_call x4, Pallas kernels, run_blocks(): pl.pallas_call(functools.partial(kernel, per), grid=(steps,), in_specs=[s...  51.6 us
    pallas_call x4, Pallas kernels, run_slabs(): pl.pallas_call(kernel, grid=(slabs,), in_specs=[spec(x.shape, cut) for x,...  49.4 us
    ppermute x21, starting transfers between devices, around(): lax.ppermute(x, 'mp', [(i, (i + by) % devices) for i in range(devices)])  48.8 us
    ppermute x21, waiting for transfers between devices, around(): lax.ppermute(x, 'mp', [(i, (i + by) % devices) for i in range(devices)])  45.1 us
    ppermute x8, starting transfers between devices, slanted(): return lax.ppermute(x, ('seq', 'mp'), pairs_here)  13.4 us
    all_gather x1, waiting for transfers between devices, body(): gathered = lax.all_gather(packed, group, axis=0, tiled=False)  10.4 us
    ppermute x4, starting transfers between devices, to_next(): return lax.ppermute(x, axis, pairs_here)  9.43 us
    unnamed x95, local copies, waits for them, and re-layouts  7.24 us
  transfers between devices with their start and end apart: 38, of which 16 were waited for; matrix products, arithmetic and copies ran while one was open for 13% of the time, Pallas kernels for 22%

profile of v3, /device:TPU:0, one launch (start us, length us, event | category | flops | bytes accessed | tf_op | source)
XLA Modules:
  0.0 311.0 jit_solution(11029145453228763384)
XLA Ops:
  10.6 2.4 concatenate.38
  13.9 5.1 %collective-permute-start.2 = (bf16[256,128]{1,0:T(8,128)(2,1)}, bf16[256,128]{1,0:T(8,128)(2,1)S(1)}, u32[]{:S(2)}, u32[]{:S(2)}) collective-permute-start(bf16[256,128]{1,0:T(8,128)(2,1)} %param.14), channel_id=1, source_target_pairs={{0,3},{1,0},{2,1},{3,2},{4,7},{5,4},{6,5},{7,6},{8,11},{9,8},{10,9... | collective-permute-start | bytes 196616 | tf_op jit(solution)/shard_map/ppermute | solution.py:697
  21.8 3.9 %collective-permute-done.3 = bf16[256,128]{1,0:T(8,128)(2,1)S(1)} collective-permute-done((bf16[256,128]{1,0:T(8,128)(2,1)}, bf16[256,128]{1,0:T(8,128)(2,1)S(1)}, u32[]{:S(2)}, u32[]{:S(2)}) %collective-permute-start.3) | collective-permute-done | bytes 65568 | tf_op jit(solution)/shard_map/ppermute | solution.py:697
  26.8 3.4 %collective-permute-start = (f32[16,1024]{1,0:T(8,128)S(1)}, f32[16,1024]{1,0:T(8,128)S(1)}, u32[]{:S(2)}, u32[]{:S(2)}) collective-permute-start(f32[16,1024]{1,0:T(8,128)S(1)} %slice_bitcast_fusion.3), channel_id=1, source_target_pairs={{0,4},{1,5},{2,6},{3,7},{8,12},{9,13},{10,14},{11,15},{16,20},{17,... | collective-permute-start | bytes 196616 | tf_op jit(solution)/shard_map/ppermute | solution.py:692
  30.8 1.7 subtract_multiply_fusion.unit
  35.9 10.4 %all-gather.8.cloned.1.call-done = bf16[4608,256]{1,0:T(8,128)(2,1)} async-done(((bf16[576,256]{1,0:T(8,128)(2,1)}), bf16[4608,256]{1,0:T(8,128)(2,1)}) %all-gather.8.cloned.1.call-update) | async-done | bytes 2359312 | tf_op jit(solution)/shard_map/all_gather | solution.py:790
  50.9 7.9 %shard_map.211 = (f32[512,256]{1,0:T(8,128)}, f32[512,256]{1,0:T(8,128)}, f32[512,256]{1,0:T(8,128)}, f32[512,256]{1,0:T(8,128)}, f32[512,256]{1,0:T(8,128)}, /*index=5*/f32[512,256]{1,0:T(8,128)}, f32[512,256]{1,0:T(8,128)}) custom-call(f32[512,1024]{1,0:T(8,128)} %subtract_multiply_fusion.unit, f32[8,1024]{1,0:T(8,128)} %maximum_maximum_fusion.edge, ...), custom_call_target="tpu_custom_call" | custom-call | flops 10000000000 | bytes 20000000 | tf_op jit(solution)/shard_map/pallas_call | solution.py:677
  58.8 21.9 %shard_map.212 = (f32[512,256]{1,0:T(8,128)}, f32[512,256]{1,0:T(8,128)}, f32[512,256]{1,0:T(8,128)}, f32[512,256]{1,0:T(8,128)}, bf16[512,256]{1,0:T(8,128)(2,1...) custom-call(f32[512,256]{1,0:T(8,128)} %get-tuple-element.92.q, ...), custom_call_target="tpu_custom_call" | custom-call | flops 10000000000 | bytes 20000000 | tf_op jit(solution)/shard_map/pallas_call | solution.py:405
  81.6 3.2 %collective-permute-start.1 = (bf16[64,256]{1,0:T(8,128)(2,1)S(1)}, bf16[64,256]{1,0:T(8,128)(2,1)S(1)}, u32[]{:S(2)}, u32[]{:S(2)}) collective-permute-start(bf16[64,256]{1,0:T(8,128)(2,1)S(1)} %convert_element_type.147), channel_id=1, source_target_pairs={{0,4},{1,5},{2,6},{3,7},{8,12},{9,13},{10,14},{11,15},{16,20},{17,... | collective-permute-start | bytes 98312 | tf_op jit(solution)/shard_map/ppermute | solution.py:692
  84.9 1.6 collective-permute-done.1
  87.1 7.4 %shard_map.213 = (bf16[512,256]{1,0:T(8,128)(2,1)}, f32[512,256]{1,0:T(8,128)}, f32[512,256]{1,0:T(8,128)}, f32[512,256]{1,0:T(8,128)}, f32[512,256]{1,0:T(8,128)}) custom-call(f32[512,256]{1,0:T(8,128)} %get-tuple-element.92.q, f32[512,256]{1,0:T(8,128)} %get-tuple-element.93.kp, f32[512,256]{1,0:T(8,128)} %get-tuple-element.94.v, ...), custom_call_target="tpu_custom_call" | custom-call | flops 10000000000 | bytes 20000000 | tf_op jit(solution)/shard_map/pallas_call | solution.py:405
  94.4 1.5 collective-permute-start.5
  96.0 2.4 collective-permute-start.6
  98.3 1.5 collective-permute-start.7
  100.6 4.2 %collective-permute-start.8 = (bf16[16,256]{1,0:T(8,128)(2,1)S(1)}, bf16[16,256]{1,0:T(8,128)(2,1)S(1)}, u32[]{:S(2)}, u32[]{:S(2)}) collective-permute-start(bf16[16,256]{1,0:T(8,128)(2,1)S(1)} %slice.140), channel_id=1, source_target_pairs={{0,4},{1,5},{2,6},{3,7},{8,12},{9,13},{10,14},{11,15},{16,20},{17,... | collective-permute-start | bytes 24584 | tf_op jit(solution)/shard_map/ppermute | solution.py:708
  104.8 1.3 collective-permute-start.9
  106.1 2.5 fusion.4
  108.7 1.4 copy.51
  110.0 1.4 copy.50
  111.4 1.3 collective-permute-start.10
  112.8 1.5 collective-permute-start.11
  114.3 3.3 %copy_bitcast_fusion = (bf16[1024,1024]{1,0:T(8,128)(2,1)}, bf16[1024,1024]{1,0:T(8,128)(2,1)}) fusion(bf16[128,8,8,128]{3,2,1,0:T(8,128)(2,1)S(1)} %bitcast.118, bf16[128,8,8,128]{3,2,1,0:T(8,128)(2,1)S(1)} %bitcast.119), kind=kLoop, calls=%fused_computation.3 | loop fusion | bytes 8388608 | tf_op jit(solution)/shard_map/reshape | solution.py:859
  118.5 19.2 %shard_map.214 = (bf16[512,1024]{1,0:T(8,128)(2,1)}, bf16[512,1024]{1,0:T(8,128)(2,1)}, bf16[512,1024]{1,0:T(8,128)(2,1)}, bf16[512,1024]{1,0:T(8,128)(2,1)}, bf...) custom-call(s32[1]{0:T(128)} %bitcast.refs_0_.here, ...), custom_call_target="tpu_custom_call" | custom-call | flops 10000000000 | bytes 20000000 | tf_op jit(solution)/shard_map/pallas_call | solution.py:677
  137.8 11.9 %shard_map.218 = bf16[8,3072,128]{2,1,0:T(8,128)(2,1)} custom-call(s32[1]{0:T(128)} %bitcast.refs_0_.here, bf16[512,1024]{1,0:T(8,128)(2,1)} %get-tuple-element.151.refs_1_, bf16[512,1024]{1,0:T(8,128)(2,1)} %get-tuple-element.152.refs_2_, bf16[512,1024]{1,0:T(8,128)(2,1)} %get-tuple-element.153.refs_3_, bf16[512,1024]{1,0:T(8,128)(2,1)} %get-tuple-element.154.refs_4_, ...), custom_call_target="tpu_custom_call" | custom-call | flops 10000000000 | bytes 20000000 | tf_op jit(solution)/shard_map/pallas_call | solution.py:677
  150.7 7.4 %collective-permute-start.12 = (bf16[512,256]{1,0:T(8,128)(2,1)S(1)}, bf16[512,256]{1,0:T(8,128)(2,1)S(1)}, u32[]{:S(2)}, u32[]{:S(2)}) collective-permute-start(bf16[512,256]{1,0:T(8,128)(2,1)S(1)} %copy-done.22), channel_id=1, source_target_pairs={{0,1},{1,2},{2,3},{3,0},{4,5},{5,6},{6,7},{7,4},{8,9},{9,10},{10,1... | collective-permute-start | bytes 786440 | tf_op jit(solution)/shard_map/ppermute | solution.py:697
  158.0 5.4 %collective-permute-start.13 = (bf16[512,256]{1,0:T(8,128)(2,1)S(1)}, bf16[512,256]{1,0:T(8,128)(2,1)S(1)}, u32[]{:S(2)}, u32[]{:S(2)}) collective-permute-start(bf16[512,256]{1,0:T(8,128)(2,1)S(1)} %copy-done.19), channel_id=1, source_target_pairs={{0,2},{1,3},{2,0},{3,1},{4,6},{5,7},{6,4},{7,5},{8,10},{9,11},{10,... | collective-permute-start | bytes 786440 | tf_op jit(solution)/shard_map/ppermute | solution.py:697
  163.5 1.3 collective-permute-start.15
  164.8 1.3 collective-permute-start.16
  166.1 4.0 %collective-permute-done.12.refs_1_ = bf16[512,256]{1,0:T(8,128)(2,1)S(1)} collective-permute-done((bf16[512,256]{1,0:T(8,128)(2,1)S(1)}, bf16[512,256]{1,0:T(8,128)(2,1)S(1)}, u32[]{:S(2)}, u32[]{:S(2)}) %collective-permute-start.12) | collective-permute-done | bytes 262176 | tf_op jit(solution)/shard_map/ppermute | solution.py:697
  171.4 7.1 %collective-permute-done.13.refs_2_ = bf16[512,256]{1,0:T(8,128)(2,1)S(1)} collective-permute-done((bf16[512,256]{1,0:T(8,128)(2,1)S(1)}, bf16[512,256]{1,0:T(8,128)(2,1)S(1)}, u32[]{:S(2)}, u32[]{:S(2)}) %collective-permute-start.13) | collective-permute-done | bytes 262176 | tf_op jit(solution)/shard_map/ppermute | solution.py:697
  179.9 4.6 %collective-permute-done.17.refs_6_ = bf16[16,256]{1,0:T(8,128)(2,1)S(1)} collective-permute-done((bf16[16,256]{1,0:T(8,128)(2,1)S(1)}, bf16[16,256]{1,0:T(8,128)(2,1)S(1)}, u32[]{:S(2)}, u32[]{:S(2)}) %collective-permute-start.17) | collective-permute-done | bytes 8224 | tf_op jit(solution)/shard_map/ppermute | solution.py:708
  184.5 1.4 collective-permute-done.18.refs_7_
  186.5 7.2 %shard_map.215 = (f32[512,256]{1,0:T(8,128)}, f32[512,256]{1,0:T(8,128)}, f32[512,256]{1,0:T(8,128)}, f32[512,256]{1,0:T(8,128)}, bf16[512,256]{1,0:T(8,128)(2,1...) custom-call(f32[512,256]{1,0:T(8,128)} %get-tuple-element.92.q, ...), custom_call_target="tpu_custom_call" | custom-call | flops 10000000000 | bytes 20000000 | tf_op jit(solution)/shard_map/pallas_call | solution.py:405
  194.5 1.5 collective-permute-start.19
  197.6 3.5 %collective-permute-done.19 = bf16[64,256]{1,0:T(8,128)(2,1)S(1)} collective-permute-done((bf16[64,256]{1,0:T(8,128)(2,1)S(1)}, bf16[64,256]{1,0:T(8,128)(2,1)S(1)}, u32[]{:S(2)}, u32[]{:S(2)}) %collective-permute-start.19) | collective-permute-done | bytes 32800 | tf_op jit(solution)/shard_map/ppermute | solution.py:692
  201.8 15.1 %shard_map.216 = (bf16[512,256]{1,0:T(8,128)(2,1)}, bf16[512,256]{1,0:T(8,128)(2,1)}, bf16[512,256]{1,0:T(8,128)(2,1)}, bf16[512,256]{1,0:T(8,128)(2,1)}, f32[8,256]{1,0:T(8,128)}, /*index=5*/f32[256,256]{1,0:T(8,128)}) custom-call(f32[512,256]{1,0:T(8,128)} %get-tuple-element.92.q, f32[512,256]{1,0:T(8,128)} %get-tuple-element.93.kp, ...), custom_call_target="tpu_custom_call" | custom-call | flops 10000000000 | bytes 20000000 | tf_op jit(solution)/shard_map/pallas_call | solution.py:405
  216.9 10.4 %shard_map.217 = (bf16[8,512,256]{2,1,0:T(8,128)(2,1)}, f32[16,1024]{1,0:T(8,128)}, f32[8,1024]{1,0:T(8,128)}, bf16[128,1024]{1,0:T(8,128)(2,1)}, bf16[128,1024]...) custom-call(s32[1]{0:T(128)} %bitcast.refs_0_.here, f32[512,1024]{1,0:T(8,128)} %subtract_multiply_fusion.unit, ...), custom_call_target="tpu_custom_call" | custom-call | flops 10000000000 | bytes 20000000 | tf_op jit(solution)/shard_map/pallas_call | solution.py:677
  229.5 3.2 %fusion.1 = bf16[8,576,256]{2,1,0:T(8,128)(2,1)} fusion(bf16[8,50,256]{2,1,0:T(8,128)(2,1)S(1)} %concatenate.43, bf16[8,512,256]{2,1,0:T(8,128)(2,1)} %get-tuple-element.145), kind=kLoop, calls=%fused_computation.2 | loop fusion | flops 7077888 | bytes 4661248 | tf_op jit(solution)/shard_map/concatenate | solution.py:999
  233.7 4.1 %collective-permute-start.28 = (bf16[128,1024]{1,0:T(8,128)(2,1)S(1)}, bf16[128,1024]{1,0:T(8,128)(2,1)S(1)}, u32[]{:S(2)}, u32[]{:S(2)}) collective-permute-start(bf16[128,1024]{1,0:T(8,128)(2,1)S(1)} %copy-done.13), channel_id=1, source_target_pairs={{0,3},{1,0},{2,1},{3,2},{4,7},{5,4},{6,5},{7,6},{8,11},{9,8},{10,9... | collective-permute-start | bytes 786440 | tf_op jit(solution)/shard_map/ppermute | solution.py:697
  240.9 2.9 collective-permute-start.22
  245.1 1.9 collective-permute-start.21
  247.1 7.1 %collective-permute-start.20 = (bf16[128,1024]{1,0:T(8,128)(2,1)S(1)}, bf16[128,1024]{1,0:T(8,128)(2,1)S(1)}, u32[]{:S(2)}, u32[]{:S(2)}) collective-permute-start(bf16[128,1024]{1,0:T(8,128)(2,1)S(1)} %copy-done.14), channel_id=1, source_target_pairs={{0,1},{1,2},{2,3},{3,0},{4,5},{5,6},{6,7},{7,4},{8,9},{9,10},{10,1... | collective-permute-start | bytes 786440 | tf_op jit(solution)/shard_map/ppermute | solution.py:697
  254.1 17.8 %collective-permute-done.27 = bf16[128,1024]{1,0:T(8,128)(2,1)S(1)} collective-permute-done((bf16[128,1024]{1,0:T(8,128)(2,1)S(1)}, bf16[128,1024]{1,0:T(8,128)(2,1)S(1)}, u32[]{:S(2)}, u32[]{:S(2)}) %collective-permute-start.27) | collective-permute-done | bytes 262176 | tf_op jit(solution)/shard_map/ppermute | solution.py:697
  273.0 7.5 %collective-permute-done.21 = bf16[128,1024]{1,0:T(8,128)(2,1)S(1)} collective-permute-done((bf16[128,1024]{1,0:T(8,128)(2,1)}, bf16[128,1024]{1,0:T(8,128)(2,1)S(1)}, u32[]{:S(2)}, u32[]{:S(2)}) %collective-permute-start.21) | collective-permute-done | bytes 262176 | tf_op jit(solution)/shard_map/ppermute | solution.py:697
  282.7 2.5 collective-permute-start.24
  285.2 1.9 collective-permute-start.23
  289.0 2.2 collective-permute-done.23
  296.4 1.3 slice_convert_fusion.1
  (230 shorter events, 49.9 us)
Async XLA Ops:
  7.2 18.5 %copy-start.5 = (bf16[256,128]{1,0:T(8,128)(2,1)S(1)}, bf16[256,128]{1,0:T(8,128)(2,1)}, u32[]{:S(2)}) copy-start(bf16[256,128]{1,0:T(8,128)(2,1)} %param.14) | copy-start | bytes 196612
  7.2 18.7 %copy-start.6 = (bf16[1024,128]{1,0:T(8,128)(2,1)S(1)}, bf16[1024,128]{1,0:T(8,128)(2,1)}, u32[]{:S(2)}) copy-start(bf16[1024,128]{1,0:T(8,128)(2,1)} %param.20) | copy-start | bytes 786436
  7.2 39.1 %all-gather.8.cloned.1.call-start = ((), (), s32[]{:S(2)}) async-start(), calls=%async_computation.5 | async-start | bytes 2654208 | tf_op jit(solution)/shard_map/all_gather | solution.py:790
  13.8 92.3 %all-gather.10.cloned.1.call-start = ((), (), s32[]{:S(2)}) async-start(), calls=%async_computation.6 | async-start | bytes 4718592 | tf_op jit(solution)/shard_map/all_gather | solution.py:808
  13.9 7.9 %collective-permute-start.2 = (bf16[256,128]{1,0:T(8,128)(2,1)}, bf16[256,128]{1,0:T(8,128)(2,1)S(1)}, u32[]{:S(2)}, u32[]{:S(2)}) collective-permute-start(bf16[256,128]{1,0:T(8,128)(2,1)} %param.14), channel_id=1, source_target_pairs={{0,3},{1,0},{2,1},{3,2},{4,7},{5,4},{6,5},{7,6},{8,11},{9,8},{10,9... | collective-permute-start | bytes 196616 | tf_op jit(solution)/shard_map/ppermute | solution.py:697
  19.0 6.7 %collective-permute-start.3 = (bf16[256,128]{1,0:T(8,128)(2,1)}, bf16[256,128]{1,0:T(8,128)(2,1)S(1)}, u32[]{:S(2)}, u32[]{:S(2)}) collective-permute-start(bf16[256,128]{1,0:T(8,128)(2,1)} %param.14), channel_id=1, source_target_pairs={{0,2},{1,3},{2,0},{3,1},{4,6},{5,7},{6,4},{7,5},{8,10},{9,11},{10,... | collective-permute-start | bytes 196616 | tf_op jit(solution)/shard_map/ppermute | solution.py:697
  19.0 6.7 %collective-permute-start.4 = (bf16[256,128]{1,0:T(8,128)(2,1)}, bf16[256,128]{1,0:T(8,128)(2,1)S(1)}, u32[]{:S(2)}, u32[]{:S(2)}) collective-permute-start(bf16[256,128]{1,0:T(8,128)(2,1)} %param.14), channel_id=1, source_target_pairs={{0,1},{1,2},{2,3},{3,0},{4,5},{5,6},{6,7},{7,4},{8,9},{9,10},{10,1... | collective-permute-start | bytes 196616 | tf_op jit(solution)/shard_map/ppermute | solution.py:697
  26.7 90.9 %all-gather.6.cloned.1.call-start = ((), (), s32[]{:S(2)}) async-start(), calls=%async_computation.2 | async-start | bytes 2359296 | tf_op jit(solution)/shard_map/all_gather | solution.py:812
  26.8 5.9 %collective-permute-start = (f32[16,1024]{1,0:T(8,128)S(1)}, f32[16,1024]{1,0:T(8,128)S(1)}, u32[]{:S(2)}, u32[]{:S(2)}) collective-permute-start(f32[16,1024]{1,0:T(8,128)S(1)} %slice_bitcast_fusion.3), channel_id=1, source_target_pairs={{0,4},{1,5},{2,6},{3,7},{8,12},{9,13},{10,14},{11,15},{16,20},{17,... | collective-permute-start | bytes 196616 | tf_op jit(solution)/shard_map/ppermute | solution.py:692
  30.2 202.5 %reduce-scatter.3.cloned.1.call-start = ((), (), s32[]{:S(2)}) async-start(), calls=%async_computation.3 | async-start | bytes 7077888 | tf_op jit(solution)/shard_map/reduce_scatter | solution.py:922
  32.7 26.2 %copy-start.10 = (f32[16,1024]{1,0:T(8,128)}, f32[16,1024]{1,0:T(8,128)S(1)}, u32[]{:S(2)}) copy-start(f32[16,1024]{1,0:T(8,128)S(1)} %collective-permute-done.refs_2_) | copy-start | bytes 196612
  81.6 4.8 %collective-permute-start.1 = (bf16[64,256]{1,0:T(8,128)(2,1)S(1)}, bf16[64,256]{1,0:T(8,128)(2,1)S(1)}, u32[]{:S(2)}, u32[]{:S(2)}) collective-permute-start(bf16[64,256]{1,0:T(8,128)(2,1)S(1)} %convert_element_type.147), channel_id=1, source_target_pairs={{0,4},{1,5},{2,6},{3,7},{8,12},{9,13},{10,14},{11,15},{16,20},{17,... | collective-permute-start | bytes 98312 | tf_op jit(solution)/shard_map/ppermute | solution.py:692
  94.4 23.2 %collective-permute-start.5 = (bf16[512,256]{1,0:T(8,128)(2,1)}, bf16[512,256]{1,0:T(8,128)(2,1)S(1)}, u32[]{:S(2)}, u32[]{:S(2)}) collective-permute-start(bf16[512,256]{1,0:T(8,128)(2,1)} %get-tuple-element.108.refs_9_.refs_6_), channel_id=1, source_target_pairs={{0,1},{1,2},{2,3},{3,0},{4,5},{5,6},{6,7},{7,4},{8,9},{9,10},{10,1... | collective-permute-start | bytes 786440 | tf_op jit(solution)/shard_map/ppermute | solution.py:697
  96.0 21.7 %collective-permute-start.6 = (bf16[512,256]{1,0:T(8,128)(2,1)}, bf16[512,256]{1,0:T(8,128)(2,1)S(1)}, u32[]{:S(2)}, u32[]{:S(2)}) collective-permute-start(bf16[512,256]{1,0:T(8,128)(2,1)} %get-tuple-element.108.refs_9_.refs_6_), channel_id=1, source_target_pairs={{0,2},{1,3},{2,0},{3,1},{4,6},{5,7},{6,4},{7,5},{8,10},{9,11},{10,... | collective-permute-start | bytes 786440 | tf_op jit(solution)/shard_map/ppermute | solution.py:697
  98.3 19.4 %collective-permute-start.7 = (bf16[512,256]{1,0:T(8,128)(2,1)}, bf16[512,256]{1,0:T(8,128)(2,1)S(1)}, u32[]{:S(2)}, u32[]{:S(2)}) collective-permute-start(bf16[512,256]{1,0:T(8,128)(2,1)} %get-tuple-element.108.refs_9_.refs_6_), channel_id=1, source_target_pairs={{0,3},{1,0},{2,1},{3,2},{4,7},{5,4},{6,5},{7,6},{8,11},{9,8},{10,9... | collective-permute-start | bytes 786440 | tf_op jit(solution)/shard_map/ppermute | solution.py:697
  100.6 10.8 %collective-permute-start.8 = (bf16[16,256]{1,0:T(8,128)(2,1)S(1)}, bf16[16,256]{1,0:T(8,128)(2,1)S(1)}, u32[]{:S(2)}, u32[]{:S(2)}) collective-permute-start(bf16[16,256]{1,0:T(8,128)(2,1)S(1)} %slice.140), channel_id=1, source_target_pairs={{0,4},{1,5},{2,6},{3,7},{8,12},{9,13},{10,14},{11,15},{16,20},{17,... | collective-permute-start | bytes 24584 | tf_op jit(solution)/shard_map/ppermute | solution.py:708
  104.8 8.1 %collective-permute-start.9 = (bf16[16,256]{1,0:T(8,128)(2,1)S(1)}, bf16[16,256]{1,0:T(8,128)(2,1)S(1)}, u32[]{:S(2)}, u32[]{:S(2)}) collective-permute-start(bf16[16,256]{1,0:T(8,128)(2,1)S(1)} %slice.140), channel_id=1, source_target_pairs={{0,5},{1,6},{2,7},{3,4},{8,13},{9,14},{10,15},{11,12},{16,21},{17,... | collective-permute-start | bytes 24584 | tf_op jit(solution)/shard_map/ppermute | solution.py:708
  111.4 6.2 %collective-permute-start.10 = (bf16[16,256]{1,0:T(8,128)(2,1)S(1)}, bf16[16,256]{1,0:T(8,128)(2,1)S(1)}, u32[]{:S(2)}, u32[]{:S(2)}) collective-permute-start(bf16[16,256]{1,0:T(8,128)(2,1)S(1)} %slice.140), channel_id=1, source_target_pairs={{0,6},{1,7},{2,4},{3,5},{8,14},{9,15},{10,12},{11,13},{16,22},{17,... | collective-permute-start | bytes 24584 | tf_op jit(solution)/shard_map/ppermute | solution.py:708
  112.8 4.8 %collective-permute-start.11 = (bf16[16,256]{1,0:T(8,128)(2,1)S(1)}, bf16[16,256]{1,0:T(8,128)(2,1)S(1)}, u32[]{:S(2)}, u32[]{:S(2)}) collective-permute-start(bf16[16,256]{1,0:T(8,128)(2,1)S(1)} %slice.140), channel_id=1, source_target_pairs={{0,7},{1,4},{2,5},{3,6},{8,15},{9,12},{10,13},{11,14},{16,23},{17,... | collective-permute-start | bytes 24584 | tf_op jit(solution)/shard_map/ppermute | solution.py:708
  149.7 20.3 %copy-start.26 = (bf16[16,256]{1,0:T(8,128)(2,1)S(1)}, bf16[16,256]{1,0:T(8,128)(2,1)}, u32[]{:S(2)}) copy-start(bf16[16,256]{1,0:T(8,128)(2,1)} %get-tuple-element.123) | copy-start | bytes 24580
  149.8 28.8 %copy-start.24 = (bf16[16,256]{1,0:T(8,128)(2,1)S(1)}, bf16[16,256]{1,0:T(8,128)(2,1)}, u32[]{:S(2)}) copy-start(bf16[16,256]{1,0:T(8,128)(2,1)} %get-tuple-element.124) | copy-start | bytes 24580
  149.8 142.1 %reduce-scatter.5.cloned.1.call-start = ((), (), s32[]{:S(2)}) async-start(), calls=%async_computation.4 | async-start | bytes 2654208 | tf_op jit(solution)/shard_map/reduce_scatter | solution.py:1005
  150.7 19.4 %collective-permute-start.12 = (bf16[512,256]{1,0:T(8,128)(2,1)S(1)}, bf16[512,256]{1,0:T(8,128)(2,1)S(1)}, u32[]{:S(2)}, u32[]{:S(2)}) collective-permute-start(bf16[512,256]{1,0:T(8,128)(2,1)S(1)} %copy-done.22), channel_id=1, source_target_pairs={{0,1},{1,2},{2,3},{3,0},{4,5},{5,6},{6,7},{7,4},{8,9},{9,10},{10,1... | collective-permute-start | bytes 786440 | tf_op jit(solution)/shard_map/ppermute | solution.py:697
  158.0 20.5 %collective-permute-start.13 = (bf16[512,256]{1,0:T(8,128)(2,1)S(1)}, bf16[512,256]{1,0:T(8,128)(2,1)S(1)}, u32[]{:S(2)}, u32[]{:S(2)}) collective-permute-start(bf16[512,256]{1,0:T(8,128)(2,1)S(1)} %copy-done.19), channel_id=1, source_target_pairs={{0,2},{1,3},{2,0},{3,1},{4,6},{5,7},{6,4},{7,5},{8,10},{9,11},{10,... | collective-permute-start | bytes 786440 | tf_op jit(solution)/shard_map/ppermute | solution.py:697
  163.5 16.3 %collective-permute-start.14 = (bf16[512,256]{1,0:T(8,128)(2,1)S(1)}, bf16[512,256]{1,0:T(8,128)(2,1)S(1)}, u32[]{:S(2)}, u32[]{:S(2)}) collective-permute-start(bf16[512,256]{1,0:T(8,128)(2,1)S(1)} %copy-done.18), channel_id=1, source_target_pairs={{0,3},{1,0},{2,1},{3,2},{4,7},{5,4},{6,5},{7,6},{8,11},{9,8},{10,9... | collective-permute-start | bytes 786440 | tf_op jit(solution)/shard_map/ppermute | solution.py:697
  163.5 16.3 %collective-permute-start.15 = (bf16[16,256]{1,0:T(8,128)(2,1)S(1)}, bf16[16,256]{1,0:T(8,128)(2,1)S(1)}, u32[]{:S(2)}, u32[]{:S(2)}) collective-permute-start(bf16[16,256]{1,0:T(8,128)(2,1)S(1)} %copy-done.29), channel_id=1, source_target_pairs={{4,0},{5,1},{6,2},{7,3},{12,8},{13,9},{14,10},{15,11},{20,16},{21,... | collective-permute-start | bytes 24584 | tf_op jit(solution)/shard_map/ppermute | solution.py:708
  164.8 15.0 %collective-permute-start.16 = (bf16[16,256]{1,0:T(8,128)(2,1)S(1)}, bf16[16,256]{1,0:T(8,128)(2,1)S(1)}, u32[]{:S(2)}, u32[]{:S(2)}) collective-permute-start(bf16[16,256]{1,0:T(8,128)(2,1)S(1)} %copy-done.28), channel_id=1, source_target_pairs={{4,1},{5,2},{6,3},{7,0},{12,9},{13,10},{14,11},{15,8},{20,17},{21,... | collective-permute-start | bytes 24584 | tf_op jit(solution)/shard_map/ppermute | solution.py:708
  170.1 15.8 %copy-start.20 = (bf16[512,256]{1,0:T(8,128)(2,1)}, bf16[512,256]{1,0:T(8,128)(2,1)S(1)}, u32[]{:S(2)}) copy-start(bf16[512,256]{1,0:T(8,128)(2,1)S(1)} %collective-permute-done.12.refs_1_) | copy-start | bytes 786436
  170.1 14.4 %collective-permute-start.17 = (bf16[16,256]{1,0:T(8,128)(2,1)S(1)}, bf16[16,256]{1,0:T(8,128)(2,1)S(1)}, u32[]{:S(2)}, u32[]{:S(2)}) collective-permute-start(bf16[16,256]{1,0:T(8,128)(2,1)S(1)} %copy-done.26), channel_id=1, source_target_pairs={{4,2},{5,3},{6,0},{7,1},{12,10},{13,11},{14,8},{15,9},{20,18},{21,... | collective-permute-start | bytes 24584 | tf_op jit(solution)/shard_map/ppermute | solution.py:708
  178.5 7.4 %collective-permute-start.18 = (bf16[16,256]{1,0:T(8,128)(2,1)S(1)}, bf16[16,256]{1,0:T(8,128)(2,1)S(1)}, u32[]{:S(2)}, u32[]{:S(2)}) collective-permute-start(bf16[16,256]{1,0:T(8,128)(2,1)S(1)} %copy-done.24), channel_id=1, source_target_pairs={{4,3},{5,0},{6,1},{7,2},{12,11},{13,8},{14,9},{15,10},{20,19},{21,... | collective-permute-start | bytes 24584 | tf_op jit(solution)/shard_map/ppermute | solution.py:708
  194.5 6.6 %collective-permute-start.19 = (bf16[64,256]{1,0:T(8,128)(2,1)S(1)}, bf16[64,256]{1,0:T(8,128)(2,1)S(1)}, u32[]{:S(2)}, u32[]{:S(2)}) collective-permute-start(bf16[64,256]{1,0:T(8,128)(2,1)S(1)} %convert_element_type.149), channel_id=1, source_target_pairs={{4,0},{5,1},{6,2},{7,3},{12,8},{13,9},{14,10},{15,11},{20,16},{21,... | collective-permute-start | bytes 98312 | tf_op jit(solution)/shard_map/ppermute | solution.py:692
  196.9 20.0 %copy-start.8 = (bf16[8,1024]{1,0:T(8,128)(2,1)}, bf16[8,1024]{1,0:T(8,128)(2,1)S(1)}, u32[]{:S(2)}) copy-start(bf16[8,1024]{1,0:T(8,128)(2,1)S(1)} %convert.46) | copy-start | bytes 49156
  232.7 39.2 %copy-start.2 = (f32[128,1024]{1,0:T(8,128)S(1)}, f32[128,1024]{1,0:T(8,128)}, u32[]{:S(2)}) copy-start(f32[128,1024]{1,0:T(8,128)} %get-tuple-element.162) | copy-start | bytes 1572868
  232.7 39.2 %copy-start.7 = (bf16[128,1024]{1,0:T(8,128)(2,1)S(1)}, bf16[128,1024]{1,0:T(8,128)(2,1)}, u32[]{:S(2)}) copy-start(bf16[128,1024]{1,0:T(8,128)(2,1)} %get-tuple-element.163) | copy-start | bytes 786436
  232.8 47.7 %copy-start.3 = (bf16[128,1024]{1,0:T(8,128)(2,1)S(1)}, bf16[128,1024]{1,0:T(8,128)(2,1)}, u32[]{:S(2)}) copy-start(bf16[128,1024]{1,0:T(8,128)(2,1)} %get-tuple-element.157) | copy-start | bytes 786436
  233.7 13.4 %collective-permute-start.28 = (bf16[128,1024]{1,0:T(8,128)(2,1)S(1)}, bf16[128,1024]{1,0:T(8,128)(2,1)S(1)}, u32[]{:S(2)}, u32[]{:S(2)}) collective-permute-start(bf16[128,1024]{1,0:T(8,128)(2,1)S(1)} %copy-done.13), channel_id=1, source_target_pairs={{0,3},{1,0},{2,1},{3,2},{4,7},{5,4},{6,5},{7,6},{8,11},{9,8},{10,9... | collective-permute-start | bytes 786440 | tf_op jit(solution)/shard_map/ppermute | solution.py:697
  237.8 34.2 %collective-permute-start.27 = (bf16[128,1024]{1,0:T(8,128)(2,1)S(1)}, bf16[128,1024]{1,0:T(8,128)(2,1)S(1)}, u32[]{:S(2)}, u32[]{:S(2)}) collective-permute-start(bf16[128,1024]{1,0:T(8,128)(2,1)S(1)} %copy-done.12), channel_id=1, source_target_pairs={{0,2},{1,3},{2,0},{3,1},{4,6},{5,7},{6,4},{7,5},{8,10},{9,11},{10,... | collective-permute-start | bytes 786440 | tf_op jit(solution)/shard_map/ppermute | solution.py:697
  237.8 34.1 %collective-permute-start.26 = (bf16[128,1024]{1,0:T(8,128)(2,1)S(1)}, bf16[128,1024]{1,0:T(8,128)(2,1)S(1)}, u32[]{:S(2)}, u32[]{:S(2)}) collective-permute-start(bf16[128,1024]{1,0:T(8,128)(2,1)S(1)} %copy-done.11), channel_id=1, source_target_pairs={{0,1},{1,2},{2,3},{3,0},{4,5},{5,6},{6,7},{7,4},{8,9},{9,10},{10,1... | collective-permute-start | bytes 786440 | tf_op jit(solution)/shard_map/ppermute | solution.py:697
  239.6 5.5 %collective-permute-start.29 = (bf16[1,1024]{1,0:T(2,128)(2,1)S(1)}, bf16[1,1024]{1,0:T(2,128)(2,1)S(1)}, u32[]{:S(2)}, u32[]{:S(2)}) collective-permute-start(bf16[1,1024]{1,0:T(2,128)(2,1)S(1)} %slice.209), channel_id=1, source_target_pairs={{4,0},{5,1},{6,2},{7,3},{12,8},{13,9},{14,10},{15,11},{20,16},{21,... | collective-permute-start | bytes 6152 | tf_op jit(solution)/shard_map/ppermute | solution.py:692
  240.9 32.0 %collective-permute-start.22 = (bf16[128,1024]{1,0:T(8,128)(2,1)}, bf16[128,1024]{1,0:T(8,128)(2,1)S(1)}, u32[]{:S(2)}, u32[]{:S(2)}) collective-permute-start(bf16[128,1024]{1,0:T(8,128)(2,1)} %get-tuple-element.160), channel_id=1, source_target_pairs={{0,3},{1,0},{2,1},{3,2},{4,7},{5,4},{6,5},{7,6},{8,11},{9,8},{10,9... | collective-permute-start | bytes 786440 | tf_op jit(solution)/shard_map/ppermute | solution.py:697
  245.1 35.4 %collective-permute-start.21 = (bf16[128,1024]{1,0:T(8,128)(2,1)}, bf16[128,1024]{1,0:T(8,128)(2,1)S(1)}, u32[]{:S(2)}, u32[]{:S(2)}) collective-permute-start(bf16[128,1024]{1,0:T(8,128)(2,1)} %get-tuple-element.159), channel_id=1, source_target_pairs={{0,2},{1,3},{2,0},{3,1},{4,6},{5,7},{6,4},{7,5},{8,10},{9,11},{10,... | collective-permute-start | bytes 786440 | tf_op jit(solution)/shard_map/ppermute | solution.py:697
  247.1 33.4 %collective-permute-start.20 = (bf16[128,1024]{1,0:T(8,128)(2,1)S(1)}, bf16[128,1024]{1,0:T(8,128)(2,1)S(1)}, u32[]{:S(2)}, u32[]{:S(2)}) collective-permute-start(bf16[128,1024]{1,0:T(8,128)(2,1)S(1)} %copy-done.14), channel_id=1, source_target_pairs={{0,1},{1,2},{2,3},{3,0},{4,5},{5,6},{6,7},{7,4},{8,9},{9,10},{10,1... | collective-permute-start | bytes 786440 | tf_op jit(solution)/shard_map/ppermute | solution.py:697
  282.6 5.4 %collective-permute-start.25 = (bf16[256,128]{1,0:T(8,128)(2,1)S(1)}, bf16[256,128]{1,0:T(8,128)(2,1)S(1)}, u32[]{:S(2)}, u32[]{:S(2)}) collective-permute-start(bf16[256,128]{1,0:T(8,128)(2,1)S(1)} %get-tuple-element.208), channel_id=1, source_target_pairs={{0,3},{1,0},{2,1},{3,2},{4,7},{5,4},{6,5},{7,6},{8,11},{9,8},{10,9... | collective-permute-start | bytes 196616 | tf_op jit(solution)/shard_map/ppermute | solution.py:697
  282.7 6.3 %collective-permute-start.24 = (bf16[256,128]{1,0:T(8,128)(2,1)S(1)}, bf16[256,128]{1,0:T(8,128)(2,1)S(1)}, u32[]{:S(2)}, u32[]{:S(2)}) collective-permute-start(bf16[256,128]{1,0:T(8,128)(2,1)S(1)} %get-tuple-element.209), channel_id=1, source_target_pairs={{0,2},{1,3},{2,0},{3,1},{4,6},{5,7},{6,4},{7,5},{8,10},{9,11},{10,... | collective-permute-start | bytes 196616 | tf_op jit(solution)/shard_map/ppermute | solution.py:697
  285.2 6.1 %collective-permute-start.23 = (bf16[256,128]{1,0:T(8,128)(2,1)S(1)}, bf16[256,128]{1,0:T(8,128)(2,1)S(1)}, u32[]{:S(2)}, u32[]{:S(2)}) collective-permute-start(bf16[256,128]{1,0:T(8,128)(2,1)S(1)} %get-tuple-element.207), channel_id=1, source_target_pairs={{0,1},{1,2},{2,3},{3,0},{4,5},{5,6},{6,7},{7,4},{8,9},{9,10},{10,1... | collective-permute-start | bytes 196616 | tf_op jit(solution)/shard_map/ppermute | solution.py:697
  293.5 7.3 %collective-permute-start.30 = (bf16[143,256]{1,0:T(8,128)(2,1)S(1)}, bf16[143,256]{1,0:T(8,128)(2,1)S(1)}, u32[]{:S(2)}, u32[]{:S(2)}) collective-permute-start(bf16[143,256]{1,0:T(8,128)(2,1)S(1)} %get-tuple-element.197), channel_id=1, source_target_pairs={{0,3},{1,0},{2,1},{3,2},{4,7},{5,4},{6,5},{7,6},{8,11},{9,8},{10,9... | collective-permute-start | bytes 219656 | tf_op jit(solution)/shard_map/ppermute | solution.py:697
  294.6 6.8 %collective-permute-start.31 = (bf16[143,256]{1,0:T(8,128)(2,1)S(1)}, bf16[143,256]{1,0:T(8,128)(2,1)S(1)}, u32[]{:S(2)}, u32[]{:S(2)}) collective-permute-start(bf16[143,256]{1,0:T(8,128)(2,1)S(1)} %get-tuple-element.197), channel_id=1, source_target_pairs={{0,2},{1,3},{2,0},{3,1},{4,6},{5,7},{6,4},{7,5},{8,10},{9,11},{10,... | collective-permute-start | bytes 219656 | tf_op jit(solution)/shard_map/ppermute | solution.py:697
  295.1 6.3 %collective-permute-start.32 = (bf16[143,256]{1,0:T(8,128)(2,1)S(1)}, bf16[143,256]{1,0:T(8,128)(2,1)S(1)}, u32[]{:S(2)}, u32[]{:S(2)}) collective-permute-start(bf16[143,256]{1,0:T(8,128)(2,1)S(1)} %get-tuple-element.197), channel_id=1, source_target_pairs={{0,1},{1,2},{2,3},{3,0},{4,5},{5,6},{6,7},{7,4},{8,9},{9,10},{10,1... | collective-permute-start | bytes 219656 | tf_op jit(solution)/shard_map/ppermute | solution.py:697
  (27 other events, 176.1 us)
Sparse Core Ops, SparseCore 0:
  13.9 32.3 all-gather.7
  48.8 36.5 all-gather.9
  87.2 27.8 all-gather.5
  149.9 70.7 reduce-scatter.2
  232.9 42.9 reduce-scatter.4

commit v4 on v3

--- a/solution.py
+++ b/solution.py
@@ -435,7 +435,7 @@
     return [piece(i, width) for i in range(3)] + [piece(3, gathered.shape[2])]
 
 
-def project_kernel(unit, edge, norms, gathered, up, q, kp, v, din, rin, gate, lat, low_total):
+def project_kernel(ids, unit, edge, norms, gathered, up, q, kp, v, din, rin, gate, lat, low_total):
     width = q.shape[1]
     step = pl.program_id(0)
     norms_here = norms[...]
@@ -478,9 +478,10 @@
         gate[...] = dot(chosen(lane >= gate_at), up[...], 1, 0)
 
 
-def unproject_kernel(here, unit, edge, scales, norms, gathered, dq, dkp, dv, pre, d_mid, packed,
-                     feature, edge_fix, *rest):
+def unproject_kernel(quick, ids, unit, edge, scales, norms, gathered, dq, dkp, dv, pre, d_mid,
+                     up_grads, second, rows_pre, rows_post, packed, feature, edge_fix, *rest):
     pieces, (all_first, all_unit) = rest[:-2], rest[-2:]
+    block = lambda j: (j + ids[3]) % 2 if quick else j
     width = dq.shape[1]
     step = pl.program_id(0)
     n = norms[...]
@@ -511,11 +512,11 @@
         weight_grad = dot(mixes[mix], grad, 0, 0)
         if which < 3:
             for j in range(parts):
-                packed[j, which * part : (which + 1) * part, :width] = weight_grad[
+                packed[block(j), which * part : (which + 1) * part, :width] = weight_grad[
                     j * part : (j + 1) * part
                 ].astype(bf16)
                 if width < low_width:
-                    packed[j, which * part : (which + 1) * part, width:] = jnp.zeros(
+                    packed[block(j), which * part : (which + 1) * part, width:] = jnp.zeros(
                         (part, low_width - width), bf16
                     )
         else:
@@ -526,15 +527,42 @@
         shifted = to_shift if shifted is None else shifted + to_shift
         direct = d_mix - to_shift if direct is None else direct + (d_mix - to_shift)
     for j in range(parts):
-        packed[j, 3 * part : 4 * part, :] = low_grad[j * part : (j + 1) * part].astype(bf16)
+        packed[block(j), 3 * part : 4 * part, :] = low_grad[j * part : (j + 1) * part].astype(bf16)
     tokens = unit_here.shape[0]
     row = lax.broadcasted_iota(jnp.int32, shifted.shape, 0)
     d_first = direct + jnp.where(row == tokens - 1, 0.0, pltpu.roll(shifted, tokens - 1, 0))
     before = shifted[0:1] * edge_here[1:2]
     feature[0:1, :] = column(d_first * unit_here) + before * edge_here[0:1]
     feature[1:2, :] = column(d_first) + before
-    feature[2:4, :] = jnp.zeros_like(feature[2:4, :])
-    feature[10:, :] = jnp.zeros_like(feature[10:, :])
+    feature[2:4, :] = second[0:2, :]
+    feature[10:11, :] = second[2:3, :]
+    feature[11:, :] = jnp.zeros_like(feature[11:, :])
+    if quick:
+        up_rows, gate_rows = rank // (8), (low_width - gate_at) // 8
+        head_part = width // SPAN * (SPAN // 8)
+        row_grads = jnp.concatenate([rows_pre[0:4, :], rows_post[4:8, :]], axis=0)
+        source = lax.broadcasted_iota(jnp.int32, (width, width), 0)
+        target = lax.broadcasted_iota(jnp.int32, (width, width), 1)
+        each = SPAN // 8
+        for j in range(parts):
+            dest = step * parts + j
+            take = lambda at, size: up_grads[pl.ds(pl.multiple_of(at + dest * size, size), size), :]
+            ups = jnp.concatenate([take(0, up_rows), take(rank, up_rows)], axis=0)
+            chosen = (target // each * SPAN + dest * each + target % each == source) & (
+                target < head_part
+            )
+            heads_here = dot(row_grads.astype(bf16), jnp.where(chosen, 1.0, 0.0).astype(bf16), 1, 0)
+            values = feature[:, j * part : (j + 1) * part]
+            at = 4 * part
+            to = block(j)
+            packed[to, at : at + EDGE, :] = ups.astype(bf16)
+            packed[to, at + EDGE : at + 2 * EDGE, :] = take(gate_at, gate_rows).astype(bf16)
+            packed[to, at + 2 * EDGE : at + 3 * EDGE, :] = jnp.concatenate(
+                [values, jnp.zeros_like(values)], axis=1
+            ).astype(bf16)
+            packed[to, at + 3 * EDGE : at + 4 * EDGE, :] = jnp.concatenate(
+                [heads_here, jnp.zeros_like(heads_here)], axis=0
+            ).astype(bf16)
     at = pl.ds(pl.multiple_of(step * slab, slab), slab)
     all_first[:tokens, at] = d_first * n[0:1]
     all_first[tokens:, at] = jnp.broadcast_to(before * n[0:1], (8, slab))
@@ -551,7 +579,7 @@
         result = scales[...] * (d_unit - mean - units * along)
         edge_fix[...] = result[tokens:] + d_mid[tokens + EDGE - 8 :, :]
         all_first[:tokens, :] = result[:tokens] + d_mid[:tokens, :]
-        send_pieces(pieces, all_first, here[0])
+        send_pieces(pieces, all_first, ids[0])
 
 
 EDGE = 16
@@ -567,10 +595,10 @@
         piece[...] = whole[share_of(here, by, len(pieces), share), :].astype(piece.dtype)
 
 
-def channel_kernel(devices, *refs):
-    here, stream, edge_stream, has_edge, cot, norms, out_full, key, value = refs[:9]
-    gated, edges = refs[9 : 9 + devices], refs[9 + devices : 9 + 2 * devices]
-    refs = refs[9 + 2 * devices :]
+def channel_kernel(devices, here, *refs):
+    stream, edge_stream, has_edge, cot, norms, out_full, key, value = refs[:8]
+    gated, edges = refs[8 : 8 + devices], refs[8 + devices : 8 + 2 * devices]
+    refs = refs[8 + 2 * devices :]
     ffn_in, hidden, d_pre, cot_low, d_mid_low, d_mid, feature, middle_share = refs[:8]
     ffn_pieces, refs = refs[8 : 8 + devices], refs[8 + devices :]
     grad_pieces, refs = refs[:devices], refs[devices:]
@@ -642,9 +670,9 @@
             fix_pieces[by][...] = dot(d_mid_low[tokens:, :], rows, 1, 1).astype(bf16)
 
 
-def large_kernel(devices, *refs):
-    here, hidden, cot_low, ffn_in, d_pre, d_mid_low = refs[:6]
-    gated, edges, large = refs[6 : 6 + devices], refs[6 + devices : 6 + 2 * devices], refs[-1]
+def large_kernel(devices, here, *refs):
+    hidden, cot_low, ffn_in, d_pre, d_mid_low = refs[:5]
+    gated, edges, large = refs[5 : 5 + devices], refs[5 + devices : 5 + 2 * devices], refs[-1]
     tokens, hidden_here = hidden.shape
     part = large.shape[2]
     width = gated[0].shape[1]
@@ -660,30 +688,79 @@
         large[0, pl.ds(pl.multiple_of(at, width), width), :] = rows.astype(bf16)
 
 
-def run_slabs(kernel, ins, outs, scratch, slabs):
+def run_slabs(kernel, ids, ins, outs, scratch, slabs):
     def spec(shape, cut):
         shape = tuple(shape)
-        if cut == "scalar":
-            return pl.BlockSpec(memory_space=pltpu.SMEM)
         if cut is None:
-            return pl.BlockSpec(shape, lambda i: (0,) * len(shape))
+            return pl.BlockSpec(shape, lambda i, ids: (0,) * len(shape))
+        if callable(cut[1]):
+            return pl.BlockSpec(*cut)
         dim, size = cut
         block = list(shape)
         block[dim] = shape[dim] // slabs
         if size is not None:
             block[size[0]] = size[1]
-        return pl.BlockSpec(tuple(block), lambda i: tuple(i if k == dim else 0 for k in range(len(shape))))
+        return pl.BlockSpec(
+            tuple(block), lambda i, ids: tuple(i if k == dim else 0 for k in range(len(shape)))
+        )
 
     return pl.pallas_call(
         kernel,
-        grid=(slabs,),
-        in_specs=[spec(x.shape, cut) for x, cut in ins],
-        out_specs=[spec(shape, cut) for shape, _, cut in outs],
+        grid_spec=pltpu.PrefetchScalarGridSpec(
+            num_scalar_prefetch=1,
+            grid=(slabs,),
+            in_specs=[spec(x.shape, cut) for x, cut in ins],
+            out_specs=[spec(shape, cut) for shape, _, cut in outs],
+            scratch_shapes=[pltpu.VMEM(shape, f32) for shape in scratch],
+        ),
         out_shape=[jax.ShapeDtypeStruct(shape, kind) for shape, kind, _ in outs],
-        scratch_shapes=[pltpu.VMEM(shape, f32) for shape in scratch],
         compiler_params=pltpu.CompilerParams(dimension_semantics=("arbitrary",)),
         cost_estimate=pl.CostEstimate(flops=10**10, bytes_accessed=2 * 10**7, transcendentals=0),
-    )(*[x for x, _ in ins])
+    )(ids, *[x for x, _ in ins])
+
+
+def core_sum_kernel(ids, kept, came, send_x, send_y, keep_x, keep_y):
+    half = send_x.shape[1]
+    total = lambda i, rows: kept[i, rows, :].astype(f32) + came[i, rows, :].astype(f32)
+    for y in range(2):
+        keep_x[y] = total(y, slice(0, half))
+        send_x[y] = total(2 + y, slice(0, half)).astype(bf16)
+    for x in range(2):
+        keep_y[x] = total(2 * x, slice(half, 2 * half))
+        send_y[x] = total(2 * x + 1, slice(half, 2 * half)).astype(bf16)
+
+
+def side_sum_kernel(ids, keep_x, keep_y, came_x, came_y, left_x, left_y, send_y, send_x):
+    left_x[...] = keep_x[0] + came_x[0].astype(f32)
+    left_y[...] = keep_y[0] + came_y[0].astype(f32)
+    send_y[...] = (keep_x[1] + came_x[1].astype(f32)).astype(bf16)
+    send_x[...] = (keep_y[1] + came_y[1].astype(f32)).astype(bf16)
+
+
+def last_sum_kernel(ids, left_x, left_y, came_y, came_x, fix, rkv, up, gate_up, head, shared, whole):
+    half = left_x.shape[0]
+    whole[:half, :] = left_x[...] + came_y[...].astype(f32)
+    whole[half:, :] = left_y[...] + came_x[...].astype(f32)
+    first = rkv.shape[0]
+    low = shared.shape[0] - 2 * EDGE
+    rkv[...] = whole[:first, :]
+    shared[:low, :] = whole[first : first + low, :].astype(bf16)
+    at = first + low
+    up[...] = whole[at : at + EDGE, :]
+    gate_up[...] = whole[at + EDGE : at + 2 * EDGE, :]
+    shared[low : low + EDGE, :] = whole[at + 2 * EDGE : at + 3 * EDGE, :].astype(bf16)
+    head[...] = whole[at + 3 * EDGE :, :]
+    shared[low + EDGE :, :] = fix[...]
+
+
+def share_sum_kernel(devices, ids, *refs):
+    pieces, out, ordered = refs[:devices], refs[devices], refs[devices + 1]
+    for by in range(devices):
+        ordered[lax.rem(ids[0] - by + devices, devices)] = pieces[by][...].astype(f32)
+    total = ordered[0]
+    for i in range(1, devices):
+        total = total + ordered[i]
+    out[...] = total
 
 
 def to_next(x, axis, by):
@@ -770,7 +847,9 @@
     lanes = max(width, low_width, part)
     up_rows = second_factors.shape[1]
     head_part = head_table.shape[2]
-    here = mp_here.astype(jnp.int32).reshape(1)
+    dp_here, seq_here = lax.axis_index("dp"), lax.axis_index("seq")
+    quick = lax.axis_size("dp") == 4 and lax.axis_size("seq") == 2 and part == 128 and width == 256
+    ids = jnp.stack([mp_here, dp_here // 2, dp_here % 2, seq_here]).astype(jnp.int32)
     edge_stream = to_next(stream[-EDGE:], "seq", 1)
     edge_row = edge_stream[EDGE - 1 :]
     pieces = [
@@ -778,8 +857,8 @@
         wide(jnp.concatenate([first_factors[0], first_factors[1], gate_first], axis=1), lanes),
         wide(second_factors.reshape(2 * up_rows, width), lanes),
         wide(gate_second, lanes),
-        wide(feature_table, lanes),
-        wide(head_table.reshape(7, heads * head_part), lanes),
+        jnp.pad(wide(feature_table, lanes), ((0, 5), (0, 0))),
+        jnp.pad(wide(head_table.reshape(7, heads * head_part), lanes), ((0, 9), (0, 0))),
     ]
     edges = [0]
     for piece in pieces:
@@ -793,10 +872,9 @@
     up = jnp.concatenate(
         [up.reshape(2 * rank, width), cut(3, width).reshape(gate_rank, width)], axis=0
     )
-    norms = cut(4, part).transpose(1, 0, 2).reshape(11, features).astype(f32)
-    norms = jnp.pad(norms, ((0, 5), (0, 0)))
+    norms = cut(4, part).transpose(1, 0, 2).reshape(16, features).astype(f32)
     head_rows = (
-        cut(5, heads * head_part)
+        cut(5, heads * head_part)[:, :7]
         .reshape(count, 7, heads, head_part)
         .transpose(1, 2, 0, 3)
         .reshape(7, width)
@@ -824,6 +902,7 @@
     whole = (tokens, width)
     q, kp, v, din, rin, gate, lat = run_slabs(
         project_kernel,
+        ids,
         [(unit_one, in_slabs), (edge, in_slabs), (norms, in_slabs), (gathered, of_gathered), (up, None)],
         [(whole, f32, None)] * 6 + [((tokens, low_width), f32, None)],
         [(tokens, low_width)],
@@ -862,7 +941,8 @@
     lots = key_full.shape[1] // part
     channel = run_slabs(
         functools.partial(channel_kernel, mp),
-        [(here, "scalar"), (stream, None), (edge_stream, None), (edge[1:2, :128], None), (cot, None)]
+        ids,
+        [(stream, None), (edge_stream, None), (edge[1:2, :128], None), (cot, None)]
         + [(norms, None), (out_full, None), (key_full, (1, None)), (value_full, (0, None))]
         + [(x, None) for x in gated_parts + edge_parts],
         [
@@ -896,7 +976,8 @@
     if part % 128 == 0:
         large = run_slabs(
             functools.partial(large_kernel, mp),
-            [(here, "scalar"), (hidden, None), (cot_low, (1, None)), (ffn_in, (1, None)), (d_pre, None)]
+            ids,
+            [(hidden, None), (cot_low, (1, None)), (ffn_in, (1, None)), (d_pre, None)]
             + [(d_mid_low, (1, None))]
             + [(x, None) for x in gated_parts + edge_parts],
             [((count, 2 * hidden_here + features, part), bf16, (0, None))],
@@ -960,15 +1041,22 @@
         [],
         tokens,
     )
-    row_grads = jnp.concatenate([row_grads[:4], row_grads_post[4:7]], axis=0)
 
     scales = jnp.concatenate([scale_one, jnp.broadcast_to(edge_scale, (8, 1))], axis=0)
+    packed_rows = rows_full if quick else 4 * part
+    whose = lambda i, ids: (((i + ids[2]) % 2) * 2 + (i // 2 + ids[1]) % 2, 0, 0)
     unprojected = run_slabs(
-        unproject_kernel,
-        [(here, "scalar"), (unit_one, in_slabs), (edge, in_slabs), (scales, None), (norms, in_slabs)]
-        + [(gathered, of_gathered), (dq, None), (dkp, None), (dv, None), (pre, None), (d_mid, None)],
+        functools.partial(unproject_kernel, quick),
+        ids,
+        [(unit_one, in_slabs), (edge, in_slabs), (scales, None), (norms, in_slabs)]
+        + [(gathered, of_gathered), (dq, None), (dkp, None), (dv, None), (pre, None), (d_mid, None)]
+        + [(up_grads, None), (second_rows, in_slabs), (row_grads, None), (row_grads_post, None)],
         [
-            ((count, 4 * part, lanes), bf16, (0, None)),
+            (
+                (count, packed_rows, lanes),
+                bf16,
+                ((2, packed_rows, lanes), whose) if quick else (0, None),
+            ),
             ((16, features), f32, in_slabs),
             ((8, features), f32, None),
         ]
@@ -979,60 +1067,99 @@
     packed, feature_grad, edge_fix = unprojected[:3]
     stream_pieces = unprojected[3:]
     fix = to_next(edge_fix[7:].astype(bf16), "seq", -1)
-
-    feature_grad = jnp.concatenate(
-        [feature_grad[:2], second_rows[:2], feature_grad[4:10], second_rows[2:3]]
-    )
-    split_rows = lambda x: x.reshape(count, x.shape[0] // count, x.shape[1])
-    wider = lambda x: jnp.pad(x.astype(bf16), ((0, 0), (0, 0), (0, lanes - x.shape[2])))
-    grads = [
-        split_rows(up_grads[:rank]),
-        split_rows(up_grads[rank : 2 * rank]),
-        split_rows(up_grads[2 * rank :]),
-        feature_grad.reshape(11, count, part).transpose(1, 0, 2),
-        row_grads.reshape(7, heads, count, head_part)
-        .transpose(2, 0, 1, 3)
-        .reshape(count, 7, heads * head_part),
-    ]
-    grads = jnp.concatenate([wider(x) for x in grads], axis=1)
-    grads = jnp.pad(grads, ((0, 0), (0, rows_full - 4 * part - grads.shape[1]), (0, 0)))
-    grads = jnp.concatenate([packed, grads], axis=1)
-    grads, large = lax.optimization_barrier((grads, large))
-    out_grad = scatter_shares(large[hidden_here + lots * part :].reshape(mp, width, part))
+    stream_came = [stream_pieces[0]] + [around(stream_pieces[by], by) for by in range(1, mp)]
+    fix_rows = features // lanes
+    fix = jnp.pad(fix.reshape(fix_rows, lanes), ((0, EDGE - fix_rows), (0, 0)))
+    if quick:
+        swap = lambda x, bit: lax.ppermute(x, "dp", [(i, i ^ bit) for i in range(4)])
+        turn = lambda x: lax.ppermute(x, "seq", [(0, 1), (1, 0)])
+        half = rows_full // 2
+        sides = (2, half, lanes)
+        came = swap(packed[4:], 1)
+        quarter = ((4, rows_full, lanes), lambda i, ids: (0, 0, 0))
+        send_x, send_y, keep_x, keep_y = run_slabs(
+            core_sum_kernel, ids, [(packed, quarter), (came, None)],
+            [(sides, bf16, None)] * 2 + [(sides, f32, None)] * 2, [], 1,
+        )
+        left_x, left_y, send_y, send_x = run_slabs(
+            side_sum_kernel,
+            ids,
+            [(x, None) for x in (keep_x, keep_y, swap(send_x, 2), turn(send_y))],
+            [(sides[1:], f32, None)] * 2 + [(sides[1:], bf16, None)] * 2,
+            [],
+            1,
+        )
+        own_rkv, own_up, own_gate_up, own_head, shared = run_slabs(
+            last_sum_kernel,
+            ids,
+            [(x, None) for x in (left_x, left_y, turn(send_y), swap(send_x, 2), fix)],
+            [
+                ((3 * part, lanes), f32, None),
+                ((EDGE, lanes), f32, None),
+                ((EDGE, lanes), f32, None),
+                ((EDGE, lanes), f32, None),
+                ((part + 2 * EDGE, lanes), bf16, None),
+            ],
+            [(rows_full, lanes)],
+            1,
+        )
+    else:
+        split_rows = lambda x: x.reshape(count, x.shape[0] // count, x.shape[1])
+        wider = lambda x: jnp.pad(x.astype(bf16), ((0, 0), (0, 0), (0, lanes - x.shape[2])))
+        head_grads = jnp.concatenate([row_grads[:4], row_grads_post[4:]], axis=0)
+        grads = [
+            split_rows(up_grads[:rank]),
+            split_rows(up_grads[rank : 2 * rank]),
+            split_rows(up_grads[2 * rank :]),
+            feature_grad.reshape(16, count, part).transpose(1, 0, 2),
+            head_grads.reshape(8, heads, count, head_part)
+            .transpose(2, 0, 1, 3)
+            .reshape(count, 8, heads * head_part),
+        ]
+        grads = jnp.concatenate([wider(x) for x in grads], axis=1)
+        grads = jnp.pad(grads, ((0, 0), (0, rows_full - 4 * part - grads.shape[1]), (0, 0)))
+        summed = lax.psum_scatter(
+            jnp.concatenate([packed, grads], axis=1), group, scatter_dimension=0, tiled=False
+        )
+        own = lambda i, w: summed[edges[i] : edges[i + 1], :w].astype(f32)
+        own_rkv, own_up, own_gate_up, own_head = own(0, width), own(2, width), own(3, width), own(5, lanes)
+        shared = jnp.concatenate(
+            [summed[edges[1] : edges[2]], summed[edges[4] : edges[5]], fix], axis=0
+        )
+    shared, large, stream_came = lax.optimization_barrier((shared, large, stream_came))
+    shares = [shared] + [around(shared, by) for by in range(1, mp)]
+    out_rows = large[hidden_here + lots * part :].reshape(mp, width, part)
     value_grad = large[:hidden_here].astype(f32)
     key_grad = large[hidden_here : hidden_here + lots * part].reshape(lots, part, part)
     key_grad = key_grad.transpose(1, 0, 2).reshape(part, lots * part).astype(f32)
-    summed = lax.psum_scatter(grads, group, scatter_dimension=0, tiled=False)
+    out_grad = scatter_shares(out_rows)
     input_grad = lax.dynamic_slice_in_dim(cot, share_at, share, 0) + sum(
-        [stream_pieces[0].astype(f32)]
-        + [around(stream_pieces[by], by).astype(f32) for by in range(1, mp)]
-    )
-    summed, input_grad, out_grad, block_out = lax.optimization_barrier(
-        (summed, input_grad, out_grad, block_out)
-    )
-    own = lambda i, w: summed[edges[i] : edges[i + 1], :w].astype(f32)
-    fix_rows = features // lanes
-    everywhere = jnp.concatenate(
-        [summed[edges[1] : edges[2]], summed[edges[4] : edges[5]], fix.reshape(fix_rows, lanes)],
-        axis=0,
-    )
-    everywhere = jnp.sum(gather_shares(everywhere).astype(f32), axis=0)
+        x.astype(f32) for x in stream_came
+    )
+    everywhere = run_slabs(
+        functools.partial(share_sum_kernel, mp),
+        ids,
+        [(x, None) for x in shares],
+        [(shared.shape, f32, None)],
+        [(mp,) + shared.shape],
+        1,
+    )[0]
     down_sum = everywhere[:part]
-    fix = everywhere[part + 11 :].reshape(1, features)
+    fix = everywhere[part + EDGE : part + EDGE + fix_rows].reshape(1, features)
     last = lax.broadcasted_iota(jnp.int32, (share, 1), 0) == share - 1
     input_grad = input_grad + jnp.where(last & (mp_here == mp - 1), fix, 0.0)
     return (
         block_out[None],
         input_grad[None],
-        own(0, width).reshape(3, part, width),
+        own_rkv.reshape(3, part, width),
         out_grad,
         jnp.stack([down_sum[:, :rank], down_sum[:, rank : 2 * rank]]),
-        own(2, width).reshape(2, up_rows, width),
+        own_up.reshape(2, up_rows, width),
         down_sum[:, 2 * rank : low_width],
-        own(3, width),
+        own_gate_up,
         key_grad,
         value_grad,
-        own(5, heads * head_part).reshape(7, heads, head_part),
+        own_head[:7, : heads * head_part].reshape(7, heads, head_part),
         everywhere[part : part + 11, :part],
     )
 

time: 313 us -> 332 us (1.061)
  Pallas kernels: 101 us -> 116 us
  starting transfers between devices: 71.8 us -> 83.6 us
  waiting for transfers between devices: 68.2 us -> 61.8 us
  other arithmetic: 23.2 us -> 18.5 us
    pallas_call x4 -> x8, Pallas kernels: 49.4 us -> 64.3 us  [run_slabs(): pl.pallas_call(kernel, grid_spec=pltpu.PrefetchScalarGridSpec(num_scalar_...]
    ppermute x21, waiting for transfers between devices: 45.1 us -> 33.8 us  [around(): lax.ppermute(x, 'mp', [(i, (i + by) % devices) for i in range(devices)])]
    ppermute x8, starting transfers between devices: 13.4 us -> 24.1 us  [slanted(): return lax.ppermute(x, ('seq', 'mp'), pairs_here)]
    unnamed x95 -> x98, local copies, waits for them, and re-layouts: 7.24 us -> 14.4 us
    ppermute x0 -> x5, waiting for transfers between devices: none -> 5.87 us  [the longest x3 4.3 us: body(): lax.ppermute(x, 'dp', [(i, i ^ bit) for i in range(4)])]
    ppermute x0 -> x5, starting transfers between devices: none -> 5.47 us  [the longest x3 2.82 us: body(): lax.ppermute(x, 'dp', [(i, i ^ bit) for i in range(4)])]
    ppermute x21, starting transfers between devices: 48.8 us -> 44.4 us  [around(): lax.ppermute(x, 'mp', [(i, (i + by) % devices) for i in range(devices)])]
    concatenate x4 -> x0, other arithmetic: 4.12 us -> none  [the longest x1 3.22 us: body(): grads = jnp.concatenate([packed, grads], axis=1)]
  transfers between devices with their start and end apart: 38 -> 42, of which waited for: 16 -> 20; matrix products, arithmetic and copies ran while one was open for 13% -> 10% of each run, Pallas kernels for 22% -> 25%
where the time goes in v4:
time: 332 us; the launch traced here: 330 us
  Pallas kernels  116 us (35%)
  starting transfers between devices  83.6 us (25%)
  waiting for transfers between devices  61.8 us (19%)
  local copies, waits for them, and re-layouts  34.1 us (10%)
  other arithmetic  18.5 us (6%)
  between operations  15.8 us (5%)
    pallas_call x8, Pallas kernels, run_slabs(): pl.pallas_call(kernel, grid_spec=pltpu.PrefetchScalarGridSpec(num_scalar_...  64.3 us
    pallas_call x4, Pallas kernels, run_blocks(): pl.pallas_call(functools.partial(kernel, per), grid=(steps,), in_specs=[s...  51.6 us
    ppermute x21, starting transfers between devices, around(): lax.ppermute(x, 'mp', [(i, (i + by) % devices) for i in range(devices)])  44.4 us
    ppermute x21, waiting for transfers between devices, around(): lax.ppermute(x, 'mp', [(i, (i + by) % devices) for i in range(devices)])  33.8 us
    ppermute x8, starting transfers between devices, slanted(): return lax.ppermute(x, ('seq', 'mp'), pairs_here)  24.1 us
    unnamed x98, local copies, waits for them, and re-layouts  14.4 us
    ppermute x4, starting transfers between devices, to_next(): return lax.ppermute(x, axis, pairs_here)  9.49 us
    all_gather x1, waiting for transfers between devices, body(): gathered = lax.all_gather(packed, group, axis=0, tiled=False)  8.77 us
  transfers between devices with their start and end apart: 42, of which 20 were waited for; matrix products, arithmetic and copies ran while one was open for 10% of the time, Pallas kernels for 25%

profile of v4, /device:TPU:0, one launch (start us, length us, event | category | flops | bytes accessed | tf_op | source)
XLA Modules:
  0.0 329.7 jit_solution(13868811375645758612)
XLA Ops:
  13.9 5.1 %collective-permute-start.1 = (bf16[256,128]{1,0:T(8,128)(2,1)}, bf16[256,128]{1,0:T(8,128)(2,1)S(1)}, u32[]{:S(2)}, u32[]{:S(2)}) collective-permute-start(bf16[256,128]{1,0:T(8,128)(2,1)} %param.14), channel_id=1, source_target_pairs={{0,3},{1,0},{2,1},{3,2},{4,7},{5,4},{6,5},{7,6},{8,11},{9,8},{10,9... | collective-permute-start | bytes 196616 | tf_op jit(solution)/shard_map/ppermute | solution.py:774
  21.8 3.9 %collective-permute-done.2 = bf16[256,128]{1,0:T(8,128)(2,1)S(1)} collective-permute-done((bf16[256,128]{1,0:T(8,128)(2,1)}, bf16[256,128]{1,0:T(8,128)(2,1)S(1)}, u32[]{:S(2)}, u32[]{:S(2)}) %collective-permute-start.2) | collective-permute-done | bytes 65568 | tf_op jit(solution)/shard_map/ppermute | solution.py:774
  27.6 3.4 %collective-permute-start = (f32[16,1024]{1,0:T(8,128)S(1)}, f32[16,1024]{1,0:T(8,128)S(1)}, u32[]{:S(2)}, u32[]{:S(2)}) collective-permute-start(f32[16,1024]{1,0:T(8,128)S(1)} %slice_bitcast_fusion.3), channel_id=1, source_target_pairs={{0,4},{1,5},{2,6},{3,7},{8,12},{9,13},{10,14},{11,15},{16,20},{17,... | collective-permute-start | bytes 196616 | tf_op jit(solution)/shard_map/ppermute | solution.py:769
  31.8 1.6 subtract_multiply_fusion.unit
  37.3 8.8 %all-gather.8.cloned.1.call-done = bf16[4608,256]{1,0:T(8,128)(2,1)} async-done(((bf16[576,256]{1,0:T(8,128)(2,1)}), bf16[4608,256]{1,0:T(8,128)(2,1)}) %all-gather.8.cloned.1.call-update) | async-done | bytes 2359312 | tf_op jit(solution)/shard_map/all_gather | solution.py:869
  50.6 8.6 %shard_map.211 = (f32[512,256]{1,0:T(8,128)}, f32[512,256]{1,0:T(8,128)}, f32[512,256]{1,0:T(8,128)}, f32[512,256]{1,0:T(8,128)}, f32[512,256]{1,0:T(8,128)}, /*index=5*/f32[512,256]{1,0:T(8,128)}, f32[512,256]{1,0:T(8,128)}) custom-call(s32[4]{0:T(128)} %pad_add_fusion.ids.here, f32[512,1024]{1,0:T(8,128)} %subtract_multiply_fusion.unit, ...), custom_call_target="tpu_custom_call" | custom-call | flops 10000000000 | bytes 20000000 | tf_op jit(solution)/shard_map/pallas_call | solution.py:707
  59.1 21.9 %shard_map.212 = (f32[512,256]{1,0:T(8,128)}, f32[512,256]{1,0:T(8,128)}, f32[512,256]{1,0:T(8,128)}, f32[512,256]{1,0:T(8,128)}, bf16[512,256]{1,0:T(8,128)(2,1...) custom-call(f32[512,256]{1,0:T(8,128)} %get-tuple-element.104.q, ...), custom_call_target="tpu_custom_call" | custom-call | flops 10000000000 | bytes 20000000 | tf_op jit(solution)/shard_map/pallas_call | solution.py:405
  81.9 3.3 collective-permute-start.4
  85.2 1.6 collective-permute-done.4
  87.4 7.4 %shard_map.213 = (bf16[512,256]{1,0:T(8,128)(2,1)}, f32[512,256]{1,0:T(8,128)}, f32[512,256]{1,0:T(8,128)}, f32[512,256]{1,0:T(8,128)}, f32[512,256]{1,0:T(8,128)}) custom-call(f32[512,256]{1,0:T(8,128)} %get-tuple-element.104.q, f32[512,256]{1,0:T(8,128)} %get-tuple-element.105.kp, f32[512,256]{1,0:T(8,128)} %get-tuple-element.106.v, ...), custom_call_target="tpu_custom_call" | custom-call | flops 10000000000 | bytes 20000000 | tf_op jit(solution)/shard_map/pallas_call | solution.py:405
  94.8 1.5 collective-permute-start.5
  96.3 2.4 collective-permute-start.6
  100.9 4.2 %collective-permute-start.10 = (bf16[16,256]{1,0:T(8,128)(2,1)S(1)}, bf16[16,256]{1,0:T(8,128)(2,1)S(1)}, u32[]{:S(2)}, u32[]{:S(2)}) collective-permute-start(bf16[16,256]{1,0:T(8,128)(2,1)S(1)} %slice.94), channel_id=1, source_target_pairs={{0,6},{1,7},{2,4},{3,5},{8,14},{9,15},{10,12},{11,13},{16,22},{17,... | collective-permute-start | bytes 24584 | tf_op jit(solution)/shard_map/ppermute | solution.py:785
  106.4 2.5 fusion.4
  111.7 1.5 collective-permute-done.10.refs_14_.refs_11_
  113.2 12.0 %collective-permute-start.8 = (bf16[16,256]{1,0:T(8,128)(2,1)S(1)}, bf16[16,256]{1,0:T(8,128)(2,1)S(1)}, u32[]{:S(2)}, u32[]{:S(2)}) collective-permute-start(bf16[16,256]{1,0:T(8,128)(2,1)S(1)} %slice.94), channel_id=1, source_target_pairs={{0,4},{1,5},{2,6},{3,7},{8,12},{9,13},{10,14},{11,15},{16,20},{17,... | collective-permute-start | bytes 24584 | tf_op jit(solution)/shard_map/ppermute | solution.py:785
  126.7 3.4 %copy_bitcast_fusion = (bf16[1024,1024]{1,0:T(8,128)(2,1)}, bf16[1024,1024]{1,0:T(8,128)(2,1)}) fusion(bf16[128,8,8,128]{3,2,1,0:T(8,128)(2,1)S(1)} %bitcast.97, bf16[128,8,8,128]{3,2,1,0:T(8,128)(2,1)S(1)} %bitcast.96), kind=kLoop, calls=%fused_computation | loop fusion | bytes 8388608 | tf_op jit(solution)/shard_map/reshape | solution.py:938
  131.0 19.9 %shard_map.214 = (bf16[512,1024]{1,0:T(8,128)(2,1)}, bf16[512,1024]{1,0:T(8,128)(2,1)}, bf16[512,1024]{1,0:T(8,128)(2,1)}, bf16[512,1024]{1,0:T(8,128)(2,1)}, bf...) custom-call(s32[4]{0:T(128)} %pad_add_fusion.ids.here, ...), custom_call_target="tpu_custom_call" | custom-call | flops 10000000000 | bytes 20000000 | tf_op jit(solution)/shard_map/pallas_call | solution.py:707
  150.9 12.7 %shard_map.221 = bf16[8,3072,128]{2,1,0:T(8,128)(2,1)} custom-call(s32[4]{0:T(128)} %pad_add_fusion.ids.here, bf16[512,1024]{1,0:T(8,128)(2,1)} %get-tuple-element.177.refs_0_, bf16[512,1024]{1,0:T(8,128)(2,1)} %get-tuple-element.178.refs_1_, bf16[512,1024]{1,0:T(8,128)(2,1)} %get-tuple-element.179.refs_2_, bf16[512,1024]{1,0:T(8,128)(2,1)} %get-tuple-element.180.refs_3_, ...), custom_call_target="tpu_custom_call" | custom-call | flops 10000000000 | bytes 20000000 | tf_op jit(solution)/shard_map/pallas_call | solution.py:707
  164.6 3.7 %collective-permute-start.13 = (bf16[512,256]{1,0:T(8,128)(2,1)S(1)}, bf16[512,256]{1,0:T(8,128)(2,1)S(1)}, u32[]{:S(2)}, u32[]{:S(2)}) collective-permute-start(bf16[512,256]{1,0:T(8,128)(2,1)S(1)} %copy-done.17), channel_id=1, source_target_pairs={{0,2},{1,3},{2,0},{3,1},{4,6},{5,7},{6,4},{7,5},{8,10},{9,11},{10,... | collective-permute-start | bytes 786440 | tf_op jit(solution)/shard_map/ppermute | solution.py:774
  171.6 4.1 %collective-permute-done.12.refs_1_ = bf16[512,256]{1,0:T(8,128)(2,1)S(1)} collective-permute-done((bf16[512,256]{1,0:T(8,128)(2,1)S(1)}, bf16[512,256]{1,0:T(8,128)(2,1)S(1)}, u32[]{:S(2)}, u32[]{:S(2)}) %collective-permute-start.12) | collective-permute-done | bytes 262176 | tf_op jit(solution)/shard_map/ppermute | solution.py:774
  177.0 8.3 %collective-permute-done.13.refs_2_ = bf16[512,256]{1,0:T(8,128)(2,1)S(1)} collective-permute-done((bf16[512,256]{1,0:T(8,128)(2,1)S(1)}, bf16[512,256]{1,0:T(8,128)(2,1)S(1)}, u32[]{:S(2)}, u32[]{:S(2)}) %collective-permute-start.13) | collective-permute-done | bytes 262176 | tf_op jit(solution)/shard_map/ppermute | solution.py:774
  186.9 5.1 %collective-permute-done.20.refs_6_ = bf16[16,256]{1,0:T(8,128)(2,1)S(1)} collective-permute-done((bf16[16,256]{1,0:T(8,128)(2,1)S(1)}, bf16[16,256]{1,0:T(8,128)(2,1)S(1)}, u32[]{:S(2)}, u32[]{:S(2)}) %collective-permute-start.20) | collective-permute-done | bytes 8224 | tf_op jit(solution)/shard_map/ppermute | solution.py:785
  192.5 7.1 %shard_map.215 = (f32[512,256]{1,0:T(8,128)}, f32[512,256]{1,0:T(8,128)}, f32[512,256]{1,0:T(8,128)}, f32[512,256]{1,0:T(8,128)}, bf16[512,256]{1,0:T(8,128)(2,1...) custom-call(f32[512,256]{1,0:T(8,128)} %get-tuple-element.104.q, ...), custom_call_target="tpu_custom_call" | custom-call | flops 10000000000 | bytes 20000000 | tf_op jit(solution)/shard_map/pallas_call | solution.py:405
  200.5 1.5 collective-permute-start.22
  202.9 3.9 %collective-permute-done.22 = bf16[64,256]{1,0:T(8,128)(2,1)S(1)} collective-permute-done((bf16[64,256]{1,0:T(8,128)(2,1)S(1)}, bf16[64,256]{1,0:T(8,128)(2,1)S(1)}, u32[]{:S(2)}, u32[]{:S(2)}) %collective-permute-start.22) | collective-permute-done | bytes 32800 | tf_op jit(solution)/shard_map/ppermute | solution.py:769
  207.4 15.1 %shard_map.216 = (bf16[512,256]{1,0:T(8,128)(2,1)}, bf16[512,256]{1,0:T(8,128)(2,1)}, bf16[512,256]{1,0:T(8,128)(2,1)}, bf16[512,256]{1,0:T(8,128)(2,1)}, f32[8,256]{1,0:T(8,128)}, /*index=5*/f32[256,256]{1,0:T(8,128)}) custom-call(f32[512,256]{1,0:T(8,128)} %get-tuple-element.104.q, f32[512,256]{1,0:T(8,128)} %get-tuple-element.105.kp, ...), custom_call_target="tpu_custom_call" | custom-call | flops 10000000000 | bytes 20000000 | tf_op jit(solution)/shard_map/pallas_call | solution.py:405
  222.6 11.4 %shard_map.217 = (bf16[8,576,256]{2,1,0:T(8,128)(2,1)}, f32[16,1024]{1,0:T(8,128)}, f32[8,1024]{1,0:T(8,128)}, bf16[128,1024]{1,0:T(8,128)(2,1)}, bf16[128,1024]...) custom-call(s32[4]{0:T(128)} %pad_add_fusion.ids.here, f32[512,1024]{1,0:T(8,128)} %subtract_multiply_fusion.unit, ...), custom_call_target="tpu_custom_call" | custom-call | flops 10000000000 | bytes 20000000 | tf_op jit(solution)/shard_map/pallas_call | solution.py:707
  235.4 2.8 collective-permute-done.23.came
  239.3 3.6 %shard_map.218 = (bf16[2,288,256]{2,1,0:T(8,128)(2,1)}, bf16[2,288,256]{2,1,0:T(8,128)(2,1)}, f32[2,288,256]{2,1,0:T(8,128)}, f32[2,288,256]{2,1,0:T(8,128)}) custom-call(s32[4]{0:T(128)} %pad_add_fusion.ids.here, bf16[8,576,256]{2,1,0:T(8,128)(2,1)} %get-tuple-element.166.kept, bf16[4,576,256]{2,1,0:T(8,128)(2,1)} %copy-done.7), custom_call_target="tpu_custom_call" | custom-call | flops 10000000000 | bytes 20000000 | tf_op jit(solution)/shard_map/pallas_call | solution.py:707
  246.3 1.6 collective-permute-start.15
  247.9 4.4 %collective-permute-start.16 = (bf16[128,1024]{1,0:T(8,128)(2,1)S(1)}, bf16[128,1024]{1,0:T(8,128)(2,1)S(1)}, u32[]{:S(2)}, u32[]{:S(2)}) collective-permute-start(bf16[128,1024]{1,0:T(8,128)(2,1)S(1)} %copy-done.11), channel_id=1, source_target_pairs={{0,2},{1,3},{2,0},{3,1},{4,6},{5,7},{6,4},{7,5},{8,10},{9,11},{10,... | collective-permute-start | bytes 786440 | tf_op jit(solution)/shard_map/ppermute | solution.py:774
  253.2 5.4 %collective-permute-start.17 = (bf16[128,1024]{1,0:T(8,128)(2,1)S(1)}, bf16[128,1024]{1,0:T(8,128)(2,1)S(1)}, u32[]{:S(2)}, u32[]{:S(2)}) collective-permute-start(bf16[128,1024]{1,0:T(8,128)(2,1)S(1)} %copy-done.10), channel_id=1, source_target_pairs={{0,3},{1,0},{2,1},{3,2},{4,7},{5,4},{6,5},{7,6},{8,11},{9,8},{10,9... | collective-permute-start | bytes 786440 | tf_op jit(solution)/shard_map/ppermute | solution.py:774
  260.1 3.1 shard_map.219
  263.2 3.8 %collective-permute-start.31 = (bf16[128,1024]{1,0:T(8,128)(2,1)S(1)}, bf16[128,1024]{1,0:T(8,128)(2,1)S(1)}, u32[]{:S(2)}, u32[]{:S(2)}) collective-permute-start(bf16[128,1024]{1,0:T(8,128)(2,1)S(1)} %copy-done.12), channel_id=1, source_target_pairs={{0,3},{1,0},{2,1},{3,2},{4,7},{5,4},{6,5},{7,6},{8,11},{9,8},{10,9... | collective-permute-start | bytes 786440 | tf_op jit(solution)/shard_map/ppermute | solution.py:774
  267.0 3.5 %collective-permute-done.16 = bf16[128,1024]{1,0:T(8,128)(2,1)S(1)} collective-permute-done((bf16[128,1024]{1,0:T(8,128)(2,1)S(1)}, bf16[128,1024]{1,0:T(8,128)(2,1)S(1)}, u32[]{:S(2)}, u32[]{:S(2)}) %collective-permute-start.16) | collective-permute-done | bytes 262176 | tf_op jit(solution)/shard_map/ppermute | solution.py:774
  270.5 2.6 collective-permute-start.26
  275.6 1.6 collective-permute-done.26.came_y
  279.3 2.6 shard_map.220
  283.3 8.8 %collective-permute-done.30 = bf16[128,1024]{1,0:T(8,128)(2,1)S(1)} collective-permute-done((bf16[128,1024]{1,0:T(8,128)(2,1)}, bf16[128,1024]{1,0:T(8,128)(2,1)S(1)}, u32[]{:S(2)}, u32[]{:S(2)}) %collective-permute-start.30) | collective-permute-done | bytes 262176 | tf_op jit(solution)/shard_map/ppermute | solution.py:774
  292.1 7.0 %collective-permute-start.32 = (bf16[160,256]{1,0:T(8,128)(2,1)}, bf16[160,256]{1,0:T(8,128)(2,1)S(1)}, u32[]{:S(2)}, u32[]{:S(2)}) collective-permute-start(bf16[160,256]{1,0:T(8,128)(2,1)} %get-tuple-element.190.refs_0_), channel_id=1, source_target_pairs={{0,1},{1,2},{2,3},{3,0},{4,5},{5,6},{6,7},{7,4},{8,9},{9,10},{10,1... | collective-permute-start | bytes 245768 | tf_op jit(solution)/shard_map/ppermute | solution.py:774
  299.6 2.0 slice_convert_fusion
  301.7 2.4 collective-permute-start.36
  304.1 2.8 collective-permute-start.37
  308.4 1.6 collective-permute-done.36
  311.1 1.8 collective-permute-done.34.refs_3_
  313.5 2.4 shard_map.222
  321.1 2.0 fusion.1
  (209 shorter events, 62.1 us)
Async XLA Ops:
  7.2 19.5 %copy-start.3 = (bf16[1024,128]{1,0:T(8,128)(2,1)S(1)}, bf16[1024,128]{1,0:T(8,128)(2,1)}, u32[]{:S(2)}) copy-start(bf16[1024,128]{1,0:T(8,128)(2,1)} %param.20) | copy-start | bytes 786436
  7.2 38.9 %all-gather.8.cloned.1.call-start = ((), (), s32[]{:S(2)}) async-start(), calls=%async_computation.3 | async-start | bytes 2654208 | tf_op jit(solution)/shard_map/all_gather | solution.py:869
  8.0 19.6 %copy-start = (f32[1,512,1024]{2,1,0:T(8,128)S(1)}, f32[1,512,1024]{2,1,0:T(8,128)}, u32[]{:S(2)}) copy-start(f32[1,512,1024]{2,1,0:T(8,128)} %param.12) | copy-start | bytes 6291460
  13.8 92.6 %all-gather.10.cloned.1.call-start = ((), (), s32[]{:S(2)}) async-start(), calls=%async_computation.4 | async-start | bytes 4718592 | tf_op jit(solution)/shard_map/all_gather | solution.py:886
  13.9 7.9 %collective-permute-start.1 = (bf16[256,128]{1,0:T(8,128)(2,1)}, bf16[256,128]{1,0:T(8,128)(2,1)S(1)}, u32[]{:S(2)}, u32[]{:S(2)}) collective-permute-start(bf16[256,128]{1,0:T(8,128)(2,1)} %param.14), channel_id=1, source_target_pairs={{0,3},{1,0},{2,1},{3,2},{4,7},{5,4},{6,5},{7,6},{8,11},{9,8},{10,9... | collective-permute-start | bytes 196616 | tf_op jit(solution)/shard_map/ppermute | solution.py:774
  19.0 6.7 %collective-permute-start.2 = (bf16[256,128]{1,0:T(8,128)(2,1)}, bf16[256,128]{1,0:T(8,128)(2,1)S(1)}, u32[]{:S(2)}, u32[]{:S(2)}) collective-permute-start(bf16[256,128]{1,0:T(8,128)(2,1)} %param.14), channel_id=1, source_target_pairs={{0,2},{1,3},{2,0},{3,1},{4,6},{5,7},{6,4},{7,5},{8,10},{9,11},{10,... | collective-permute-start | bytes 196616 | tf_op jit(solution)/shard_map/ppermute | solution.py:774
  19.0 6.7 %collective-permute-start.3 = (bf16[256,128]{1,0:T(8,128)(2,1)}, bf16[256,128]{1,0:T(8,128)(2,1)S(1)}, u32[]{:S(2)}, u32[]{:S(2)}) collective-permute-start(bf16[256,128]{1,0:T(8,128)(2,1)} %param.14), channel_id=1, source_target_pairs={{0,1},{1,2},{2,3},{3,0},{4,5},{5,6},{6,7},{7,4},{8,9},{9,10},{10,1... | collective-permute-start | bytes 196616 | tf_op jit(solution)/shard_map/ppermute | solution.py:774
  27.5 102.6 %all-gather.6.cloned.1.call-start = ((), (), s32[]{:S(2)}) async-start(), calls=%async_computation.1 | async-start | bytes 2359296 | tf_op jit(solution)/shard_map/all_gather | solution.py:890
  27.6 6.4 %collective-permute-start = (f32[16,1024]{1,0:T(8,128)S(1)}, f32[16,1024]{1,0:T(8,128)S(1)}, u32[]{:S(2)}, u32[]{:S(2)}) collective-permute-start(f32[16,1024]{1,0:T(8,128)S(1)} %slice_bitcast_fusion.3), channel_id=1, source_target_pairs={{0,4},{1,5},{2,6},{3,7},{8,12},{9,13},{10,14},{11,15},{16,20},{17,... | collective-permute-start | bytes 196616 | tf_op jit(solution)/shard_map/ppermute | solution.py:769
  31.0 261.1 %reduce-scatter.2.cloned.1.call-start = ((), (), s32[]{:S(2)}) async-start(), calls=%async_computation.2 | async-start | bytes 7077888 | tf_op jit(solution)/shard_map/reduce_scatter | solution.py:1003
  34.0 25.1 %copy-start.6 = (f32[16,1024]{1,0:T(8,128)}, f32[16,1024]{1,0:T(8,128)S(1)}, u32[]{:S(2)}) copy-start(f32[16,1024]{1,0:T(8,128)S(1)} %collective-permute-done.refs_1_) | copy-start | bytes 196612
  81.9 4.9 %collective-permute-start.4 = (bf16[64,256]{1,0:T(8,128)(2,1)S(1)}, bf16[64,256]{1,0:T(8,128)(2,1)S(1)}, u32[]{:S(2)}, u32[]{:S(2)}) collective-permute-start(bf16[64,256]{1,0:T(8,128)(2,1)S(1)} %convert_element_type.106), channel_id=1, source_target_pairs={{0,4},{1,5},{2,6},{3,7},{8,12},{9,13},{10,14},{11,15},{16,20},{17,... | collective-permute-start | bytes 98312 | tf_op jit(solution)/shard_map/ppermute | solution.py:769
  94.8 35.3 %collective-permute-start.5 = (bf16[512,256]{1,0:T(8,128)(2,1)}, bf16[512,256]{1,0:T(8,128)(2,1)S(1)}, u32[]{:S(2)}, u32[]{:S(2)}) collective-permute-start(bf16[512,256]{1,0:T(8,128)(2,1)} %get-tuple-element.117.refs_8_.refs_5_), channel_id=1, source_target_pairs={{0,1},{1,2},{2,3},{3,0},{4,5},{5,6},{6,7},{7,4},{8,9},{9,10},{10,1... | collective-permute-start | bytes 786440 | tf_op jit(solution)/shard_map/ppermute | solution.py:774
  96.3 33.8 %collective-permute-start.6 = (bf16[512,256]{1,0:T(8,128)(2,1)}, bf16[512,256]{1,0:T(8,128)(2,1)S(1)}, u32[]{:S(2)}, u32[]{:S(2)}) collective-permute-start(bf16[512,256]{1,0:T(8,128)(2,1)} %get-tuple-element.117.refs_8_.refs_5_), channel_id=1, source_target_pairs={{0,2},{1,3},{2,0},{3,1},{4,6},{5,7},{6,4},{7,5},{8,10},{9,11},{10,... | collective-permute-start | bytes 786440 | tf_op jit(solution)/shard_map/ppermute | solution.py:774
  98.7 31.4 %collective-permute-start.7 = (bf16[512,256]{1,0:T(8,128)(2,1)}, bf16[512,256]{1,0:T(8,128)(2,1)S(1)}, u32[]{:S(2)}, u32[]{:S(2)}) collective-permute-start(bf16[512,256]{1,0:T(8,128)(2,1)} %get-tuple-element.117.refs_8_.refs_5_), channel_id=1, source_target_pairs={{0,3},{1,0},{2,1},{3,2},{4,7},{5,4},{6,5},{7,6},{8,11},{9,8},{10,9... | collective-permute-start | bytes 786440 | tf_op jit(solution)/shard_map/ppermute | solution.py:774
  100.9 12.3 %collective-permute-start.10 = (bf16[16,256]{1,0:T(8,128)(2,1)S(1)}, bf16[16,256]{1,0:T(8,128)(2,1)S(1)}, u32[]{:S(2)}, u32[]{:S(2)}) collective-permute-start(bf16[16,256]{1,0:T(8,128)(2,1)S(1)} %slice.94), channel_id=1, source_target_pairs={{0,6},{1,7},{2,4},{3,5},{8,14},{9,15},{10,12},{11,13},{16,22},{17,... | collective-permute-start | bytes 24584 | tf_op jit(solution)/shard_map/ppermute | solution.py:785
  105.1 20.1 %collective-permute-start.11 = (bf16[16,256]{1,0:T(8,128)(2,1)S(1)}, bf16[16,256]{1,0:T(8,128)(2,1)S(1)}, u32[]{:S(2)}, u32[]{:S(2)}) collective-permute-start(bf16[16,256]{1,0:T(8,128)(2,1)S(1)} %slice.94), channel_id=1, source_target_pairs={{0,7},{1,4},{2,5},{3,6},{8,15},{9,12},{10,13},{11,14},{16,23},{17,... | collective-permute-start | bytes 24584 | tf_op jit(solution)/shard_map/ppermute | solution.py:785
  113.2 16.9 %collective-permute-start.8 = (bf16[16,256]{1,0:T(8,128)(2,1)S(1)}, bf16[16,256]{1,0:T(8,128)(2,1)S(1)}, u32[]{:S(2)}, u32[]{:S(2)}) collective-permute-start(bf16[16,256]{1,0:T(8,128)(2,1)S(1)} %slice.94), channel_id=1, source_target_pairs={{0,4},{1,5},{2,6},{3,7},{8,12},{9,13},{10,14},{11,15},{16,20},{17,... | collective-permute-start | bytes 24584 | tf_op jit(solution)/shard_map/ppermute | solution.py:785
  125.2 4.9 %collective-permute-start.9 = (bf16[16,256]{1,0:T(8,128)(2,1)S(1)}, bf16[16,256]{1,0:T(8,128)(2,1)S(1)}, u32[]{:S(2)}, u32[]{:S(2)}) collective-permute-start(bf16[16,256]{1,0:T(8,128)(2,1)S(1)} %slice.94), channel_id=1, source_target_pairs={{0,5},{1,6},{2,7},{3,4},{8,13},{9,14},{10,15},{11,12},{16,21},{17,... | collective-permute-start | bytes 24584 | tf_op jit(solution)/shard_map/ppermute | solution.py:785
  163.6 21.6 %copy-start.29 = (bf16[16,256]{1,0:T(8,128)(2,1)S(1)}, bf16[16,256]{1,0:T(8,128)(2,1)}, u32[]{:S(2)}) copy-start(bf16[16,256]{1,0:T(8,128)(2,1)} %get-tuple-element.141) | copy-start | bytes 24580
  164.5 11.1 %collective-permute-start.12 = (bf16[512,256]{1,0:T(8,128)(2,1)S(1)}, bf16[512,256]{1,0:T(8,128)(2,1)S(1)}, u32[]{:S(2)}, u32[]{:S(2)}) collective-permute-start(bf16[512,256]{1,0:T(8,128)(2,1)S(1)} %copy-done.20), channel_id=1, source_target_pairs={{0,1},{1,2},{2,3},{3,0},{4,5},{5,6},{6,7},{7,4},{8,9},{9,10},{10,1... | collective-permute-start | bytes 786440 | tf_op jit(solution)/shard_map/ppermute | solution.py:774
  164.6 20.7 %collective-permute-start.13 = (bf16[512,256]{1,0:T(8,128)(2,1)S(1)}, bf16[512,256]{1,0:T(8,128)(2,1)S(1)}, u32[]{:S(2)}, u32[]{:S(2)}) collective-permute-start(bf16[512,256]{1,0:T(8,128)(2,1)S(1)} %copy-done.17), channel_id=1, source_target_pairs={{0,2},{1,3},{2,0},{3,1},{4,6},{5,7},{6,4},{7,5},{8,10},{9,11},{10,... | collective-permute-start | bytes 786440 | tf_op jit(solution)/shard_map/ppermute | solution.py:774
  168.4 18.2 %collective-permute-start.14 = (bf16[512,256]{1,0:T(8,128)(2,1)S(1)}, bf16[512,256]{1,0:T(8,128)(2,1)S(1)}, u32[]{:S(2)}, u32[]{:S(2)}) collective-permute-start(bf16[512,256]{1,0:T(8,128)(2,1)S(1)} %copy-done.16), channel_id=1, source_target_pairs={{0,3},{1,0},{2,1},{3,2},{4,7},{5,4},{6,5},{7,6},{8,11},{9,8},{10,9... | collective-permute-start | bytes 786440 | tf_op jit(solution)/shard_map/ppermute | solution.py:774
  169.0 17.6 %collective-permute-start.18 = (bf16[16,256]{1,0:T(8,128)(2,1)S(1)}, bf16[16,256]{1,0:T(8,128)(2,1)S(1)}, u32[]{:S(2)}, u32[]{:S(2)}) collective-permute-start(bf16[16,256]{1,0:T(8,128)(2,1)S(1)} %copy-done.33), channel_id=1, source_target_pairs={{4,0},{5,1},{6,2},{7,3},{12,8},{13,9},{14,10},{15,11},{20,16},{21,... | collective-permute-start | bytes 24584 | tf_op jit(solution)/shard_map/ppermute | solution.py:785
  170.3 16.6 %collective-permute-start.19 = (bf16[16,256]{1,0:T(8,128)(2,1)S(1)}, bf16[16,256]{1,0:T(8,128)(2,1)S(1)}, u32[]{:S(2)}, u32[]{:S(2)}) collective-permute-start(bf16[16,256]{1,0:T(8,128)(2,1)S(1)} %copy-done.32), channel_id=1, source_target_pairs={{4,1},{5,2},{6,3},{7,0},{12,9},{13,10},{14,11},{15,8},{20,17},{21,... | collective-permute-start | bytes 24584 | tf_op jit(solution)/shard_map/ppermute | solution.py:785
  175.7 16.2 %collective-permute-start.20 = (bf16[16,256]{1,0:T(8,128)(2,1)S(1)}, bf16[16,256]{1,0:T(8,128)(2,1)S(1)}, u32[]{:S(2)}, u32[]{:S(2)}) collective-permute-start(bf16[16,256]{1,0:T(8,128)(2,1)S(1)} %copy-done.31), channel_id=1, source_target_pairs={{4,2},{5,3},{6,0},{7,1},{12,10},{13,11},{14,8},{15,9},{20,18},{21,... | collective-permute-start | bytes 24584 | tf_op jit(solution)/shard_map/ppermute | solution.py:785
  185.3 6.6 %collective-permute-start.21 = (bf16[16,256]{1,0:T(8,128)(2,1)S(1)}, bf16[16,256]{1,0:T(8,128)(2,1)S(1)}, u32[]{:S(2)}, u32[]{:S(2)}) collective-permute-start(bf16[16,256]{1,0:T(8,128)(2,1)S(1)} %copy-done.29), channel_id=1, source_target_pairs={{4,3},{5,0},{6,1},{7,2},{12,11},{13,8},{14,9},{15,10},{20,19},{21,... | collective-permute-start | bytes 24584 | tf_op jit(solution)/shard_map/ppermute | solution.py:785
  200.5 6.3 %collective-permute-start.22 = (bf16[64,256]{1,0:T(8,128)(2,1)S(1)}, bf16[64,256]{1,0:T(8,128)(2,1)S(1)}, u32[]{:S(2)}, u32[]{:S(2)}) collective-permute-start(bf16[64,256]{1,0:T(8,128)(2,1)S(1)} %convert_element_type.112), channel_id=1, source_target_pairs={{4,0},{5,1},{6,2},{7,3},{12,8},{13,9},{14,10},{15,11},{20,16},{21,... | collective-permute-start | bytes 98312 | tf_op jit(solution)/shard_map/ppermute | solution.py:769
  235.3 17.9 %copy-start.10 = (bf16[128,1024]{1,0:T(8,128)(2,1)S(1)}, bf16[128,1024]{1,0:T(8,128)(2,1)}, u32[]{:S(2)}) copy-start(bf16[128,1024]{1,0:T(8,128)(2,1)} %get-tuple-element.130) | copy-start | bytes 786436
  235.4 2.9 collective-permute-start.23
  242.9 16.4 %collective-permute-start.24 = (bf16[2,288,256]{2,1,0:T(8,128)(2,1)}, bf16[2,288,256]{2,1,0:T(8,128)(2,1)S(1)}, u32[]{:S(2)}, u32[]{:S(2)}) collective-permute-start(bf16[2,288,256]{2,1,0:T(8,128)(2,1)} %get-tuple-element.169), channel_id=1, source_target_pairs={{0,16},{8,24},{16,0},{24,8},{1,17},{9,25},{17,1},{25,9},{2,18},{10... | collective-permute-start | bytes 884744 | tf_op jit(solution)/shard_map/ppermute | solution.py:1074
  244.2 15.1 %collective-permute-start.25 = (bf16[2,288,256]{2,1,0:T(8,128)(2,1)}, bf16[2,288,256]{2,1,0:T(8,128)(2,1)S(1)}, u32[]{:S(2)}, u32[]{:S(2)}) collective-permute-start(bf16[2,288,256]{2,1,0:T(8,128)(2,1)} %get-tuple-element.170), channel_id=1, source_target_pairs={{0,4},{4,0},{1,5},{5,1},{2,6},{6,2},{3,7},{7,3},{8,12},{12,8},{9,1... | collective-permute-start | bytes 884744 | tf_op jit(solution)/shard_map/ppermute | solution.py:1075
  244.9 8.3 %collective-permute-start.28 = (bf16[1,1024]{1,0:T(2,128)(2,1)S(1)}, bf16[1,1024]{1,0:T(2,128)(2,1)S(1)}, u32[]{:S(2)}, u32[]{:S(2)}) collective-permute-start(bf16[1,1024]{1,0:T(2,128)(2,1)S(1)} %slice.133), channel_id=1, source_target_pairs={{4,0},{5,1},{6,2},{7,3},{12,8},{13,9},{14,10},{15,11},{20,16},{21,... | collective-permute-start | bytes 6152 | tf_op jit(solution)/shard_map/ppermute | solution.py:769
  246.3 16.9 %collective-permute-start.15 = (bf16[128,1024]{1,0:T(8,128)(2,1)}, bf16[128,1024]{1,0:T(8,128)(2,1)S(1)}, u32[]{:S(2)}, u32[]{:S(2)}) collective-permute-start(bf16[128,1024]{1,0:T(8,128)(2,1)} %get-tuple-element.128), channel_id=1, source_target_pairs={{0,1},{1,2},{2,3},{3,0},{4,5},{5,6},{6,7},{7,4},{8,9},{9,10},{10,1... | collective-permute-start | bytes 786440 | tf_op jit(solution)/shard_map/ppermute | solution.py:774
  247.9 22.6 %collective-permute-start.16 = (bf16[128,1024]{1,0:T(8,128)(2,1)S(1)}, bf16[128,1024]{1,0:T(8,128)(2,1)S(1)}, u32[]{:S(2)}, u32[]{:S(2)}) collective-permute-start(bf16[128,1024]{1,0:T(8,128)(2,1)S(1)} %copy-done.11), channel_id=1, source_target_pairs={{0,2},{1,3},{2,0},{3,1},{4,6},{5,7},{6,4},{7,5},{8,10},{9,11},{10,... | collective-permute-start | bytes 786440 | tf_op jit(solution)/shard_map/ppermute | solution.py:774
  253.2 19.9 %collective-permute-start.17 = (bf16[128,1024]{1,0:T(8,128)(2,1)S(1)}, bf16[128,1024]{1,0:T(8,128)(2,1)S(1)}, u32[]{:S(2)}, u32[]{:S(2)}) collective-permute-start(bf16[128,1024]{1,0:T(8,128)(2,1)S(1)} %copy-done.10), channel_id=1, source_target_pairs={{0,3},{1,0},{2,1},{3,2},{4,7},{5,4},{6,5},{7,6},{8,11},{9,8},{10,9... | collective-permute-start | bytes 786440 | tf_op jit(solution)/shard_map/ppermute | solution.py:774
  259.2 24.1 %collective-permute-start.29 = (bf16[128,1024]{1,0:T(8,128)(2,1)}, bf16[128,1024]{1,0:T(8,128)(2,1)S(1)}, u32[]{:S(2)}, u32[]{:S(2)}) collective-permute-start(bf16[128,1024]{1,0:T(8,128)(2,1)} %get-tuple-element.183), channel_id=1, source_target_pairs={{0,1},{1,2},{2,3},{3,0},{4,5},{5,6},{6,7},{7,4},{8,9},{9,10},{10,1... | collective-permute-start | bytes 786440 | tf_op jit(solution)/shard_map/ppermute | solution.py:774
  259.3 32.8 %collective-permute-start.30 = (bf16[128,1024]{1,0:T(8,128)(2,1)}, bf16[128,1024]{1,0:T(8,128)(2,1)S(1)}, u32[]{:S(2)}, u32[]{:S(2)}) collective-permute-start(bf16[128,1024]{1,0:T(8,128)(2,1)} %get-tuple-element.184), channel_id=1, source_target_pairs={{0,2},{1,3},{2,0},{3,1},{4,6},{5,7},{6,4},{7,5},{8,10},{9,11},{10,... | collective-permute-start | bytes 786440 | tf_op jit(solution)/shard_map/ppermute | solution.py:774
  263.2 28.9 %collective-permute-start.31 = (bf16[128,1024]{1,0:T(8,128)(2,1)S(1)}, bf16[128,1024]{1,0:T(8,128)(2,1)S(1)}, u32[]{:S(2)}, u32[]{:S(2)}) collective-permute-start(bf16[128,1024]{1,0:T(8,128)(2,1)S(1)} %copy-done.12), channel_id=1, source_target_pairs={{0,3},{1,0},{2,1},{3,2},{4,7},{5,4},{6,5},{7,6},{8,11},{9,8},{10,9... | collective-permute-start | bytes 786440 | tf_op jit(solution)/shard_map/ppermute | solution.py:774
  270.5 6.7 %collective-permute-start.26 = (bf16[288,256]{1,0:T(8,128)(2,1)}, bf16[288,256]{1,0:T(8,128)(2,1)S(1)}, u32[]{:S(2)}, u32[]{:S(2)}) collective-permute-start(bf16[288,256]{1,0:T(8,128)(2,1)} %get-tuple-element.173), channel_id=1, source_target_pairs={{0,4},{4,0},{1,5},{5,1},{2,6},{6,2},{3,7},{7,3},{8,12},{12,8},{9,1... | collective-permute-start | bytes 442376 | tf_op jit(solution)/shard_map/ppermute | solution.py:1075
  273.1 5.5 %collective-permute-start.27 = (bf16[288,256]{1,0:T(8,128)(2,1)}, bf16[288,256]{1,0:T(8,128)(2,1)S(1)}, u32[]{:S(2)}, u32[]{:S(2)}) collective-permute-start(bf16[288,256]{1,0:T(8,128)(2,1)} %get-tuple-element.174), channel_id=1, source_target_pairs={{0,16},{8,24},{16,0},{24,8},{1,17},{9,25},{17,1},{25,9},{2,18},{10... | collective-permute-start | bytes 442376 | tf_op jit(solution)/shard_map/ppermute | solution.py:1074
  281.9 26.5 %copy-start.24 = (bf16[160,256]{1,0:T(8,128)(2,1)S(1)}, bf16[160,256]{1,0:T(8,128)(2,1)}, u32[]{:S(2)}) copy-start(bf16[160,256]{1,0:T(8,128)(2,1)} %get-tuple-element.190.refs_0_) | copy-start | bytes 245764
  292.1 19.0 %collective-permute-start.32 = (bf16[160,256]{1,0:T(8,128)(2,1)}, bf16[160,256]{1,0:T(8,128)(2,1)S(1)}, u32[]{:S(2)}, u32[]{:S(2)}) collective-permute-start(bf16[160,256]{1,0:T(8,128)(2,1)} %get-tuple-element.190.refs_0_), channel_id=1, source_target_pairs={{0,1},{1,2},{2,3},{3,0},{4,5},{5,6},{6,7},{7,4},{8,9},{9,10},{10,1... | collective-permute-start | bytes 245768 | tf_op jit(solution)/shard_map/ppermute | solution.py:774
  299.1 12.0 %collective-permute-start.33 = (bf16[160,256]{1,0:T(8,128)(2,1)}, bf16[160,256]{1,0:T(8,128)(2,1)S(1)}, u32[]{:S(2)}, u32[]{:S(2)}) collective-permute-start(bf16[160,256]{1,0:T(8,128)(2,1)} %get-tuple-element.190.refs_0_), channel_id=1, source_target_pairs={{0,2},{1,3},{2,0},{3,1},{4,6},{5,7},{6,4},{7,5},{8,10},{9,11},{10,... | collective-permute-start | bytes 245768 | tf_op jit(solution)/shard_map/ppermute | solution.py:774
  301.6 6.9 %collective-permute-start.35 = (bf16[256,128]{1,0:T(8,128)(2,1)S(1)}, bf16[256,128]{1,0:T(8,128)(2,1)S(1)}, u32[]{:S(2)}, u32[]{:S(2)}) collective-permute-start(bf16[256,128]{1,0:T(8,128)(2,1)S(1)} %get-tuple-element.227), channel_id=1, source_target_pairs={{0,1},{1,2},{2,3},{3,0},{4,5},{5,6},{6,7},{7,4},{8,9},{9,10},{10,1... | collective-permute-start | bytes 196616 | tf_op jit(solution)/shard_map/ppermute | solution.py:774
  301.7 8.4 %collective-permute-start.36 = (bf16[256,128]{1,0:T(8,128)(2,1)S(1)}, bf16[256,128]{1,0:T(8,128)(2,1)S(1)}, u32[]{:S(2)}, u32[]{:S(2)}) collective-permute-start(bf16[256,128]{1,0:T(8,128)(2,1)S(1)} %get-tuple-element.229), channel_id=1, source_target_pairs={{0,2},{1,3},{2,0},{3,1},{4,6},{5,7},{6,4},{7,5},{8,10},{9,11},{10,... | collective-permute-start | bytes 196616 | tf_op jit(solution)/shard_map/ppermute | solution.py:774
  304.1 6.3 %collective-permute-start.37 = (bf16[256,128]{1,0:T(8,128)(2,1)S(1)}, bf16[256,128]{1,0:T(8,128)(2,1)S(1)}, u32[]{:S(2)}, u32[]{:S(2)}) collective-permute-start(bf16[256,128]{1,0:T(8,128)(2,1)S(1)} %get-tuple-element.228), channel_id=1, source_target_pairs={{0,3},{1,0},{2,1},{3,2},{4,7},{5,4},{6,5},{7,6},{8,11},{9,8},{10,9... | collective-permute-start | bytes 196616 | tf_op jit(solution)/shard_map/ppermute | solution.py:774
  308.4 4.4 %collective-permute-start.34 = (bf16[160,256]{1,0:T(8,128)(2,1)S(1)}, bf16[160,256]{1,0:T(8,128)(2,1)S(1)}, u32[]{:S(2)}, u32[]{:S(2)}) collective-permute-start(bf16[160,256]{1,0:T(8,128)(2,1)S(1)} %copy-done.24), channel_id=1, source_target_pairs={{0,3},{1,0},{2,1},{3,2},{4,7},{5,4},{6,5},{7,6},{8,11},{9,8},{10,9... | collective-permute-start | bytes 245768 | tf_op jit(solution)/shard_map/ppermute | solution.py:774
  (34 other events, 160.7 us)
Sparse Core Ops, SparseCore 0:
  13.9 32.0 all-gather.7
  48.5 36.5 all-gather.9
  87.0 27.8 all-gather.5
  163.8 61.2 reduce-scatter.1

commit v5 on v4

--- a/solution.py
+++ b/solution.py
@@ -753,14 +753,27 @@
     shared[low + EDGE :, :] = fix[...]
 
 
-def share_sum_kernel(devices, ids, *refs):
-    pieces, out, ordered = refs[:devices], refs[devices], refs[devices + 1]
+def share_sum_kernel(devices, part, ids, *refs):
+    pieces, stream, refs = refs[:devices], refs[devices], refs[devices + 1 :]
+    down, gate_down, feature, input_grad, ordered = refs
     for by in range(devices):
         ordered[lax.rem(ids[0] - by + devices, devices)] = pieces[by][...].astype(f32)
     total = ordered[0]
     for i in range(1, devices):
         total = total + ordered[i]
-    out[...] = total
+    rank, gate_at = low_parts(total.shape[1])
+    turned = total[:part, :gate_at].T
+    down[0] = turned[:rank]
+    down[1] = turned[rank:]
+    gate_down[...] = total[:part, gate_at:]
+    feature[...] = total[part : part + EDGE, :part]
+    share, features = stream.shape
+    lanes = total.shape[1]
+    input_grad[...] = stream[...]
+    ends = (ids[0] == devices - 1).astype(f32)
+    for k in range(features // lanes):
+        at = part + EDGE + k
+        input_grad[share - 1 :, k * lanes : (k + 1) * lanes] += total[at : at + 1] * ends
 
 
 def to_next(x, axis, by):
@@ -968,7 +981,9 @@
     ffn_pieces = channel[8 : 8 + mp]
     grad_pieces = channel[8 + mp : 8 + 2 * mp]
     fix_pieces = channel[8 + 2 * mp :]
-    fixes = [slanted(fix_pieces[by], -1, by) for by in range(mp)]
+    fixes = []
+    for by in range(mp):
+        fixes.append(slanted(fix_pieces[by], -1, by))
     d_gated = [grad_pieces[0]]
     for by in range(1, mp):
         d_gated.append(around(grad_pieces[by], by))
@@ -1067,9 +1082,20 @@
     packed, feature_grad, edge_fix = unprojected[:3]
     stream_pieces = unprojected[3:]
     fix = to_next(edge_fix[7:].astype(bf16), "seq", -1)
-    stream_came = [stream_pieces[0]] + [around(stream_pieces[by], by) for by in range(1, mp)]
+    stream_came = [stream_pieces[0]]
+    for by in range(1, mp):
+        stream_came.append(around(stream_pieces[by], by))
     fix_rows = features // lanes
     fix = jnp.pad(fix.reshape(fix_rows, lanes), ((0, EDGE - fix_rows), (0, 0)))
+
+    def settle(large):
+        key_grad = large[hidden_here : hidden_here + lots * part].reshape(lots, part, part)
+        return (
+            large[:hidden_here].astype(f32),
+            key_grad.transpose(1, 0, 2).reshape(part, lots * part).astype(f32),
+            scatter_shares(large[hidden_here + lots * part :].reshape(mp, width, part)),
+        )
+
     if quick:
         swap = lambda x, bit: lax.ppermute(x, "dp", [(i, i ^ bit) for i in range(4)])
         turn = lambda x: lax.ppermute(x, "seq", [(0, 1), (1, 0)])
@@ -1081,6 +1107,8 @@
             core_sum_kernel, ids, [(packed, quarter), (came, None)],
             [(sides, bf16, None)] * 2 + [(sides, f32, None)] * 2, [], 1,
         )
+        keep_x, large = lax.optimization_barrier((keep_x, large))
+        settled = settle(large)
         left_x, left_y, send_y, send_x = run_slabs(
             side_sum_kernel,
             ids,
@@ -1089,6 +1117,7 @@
             [],
             1,
         )
+        left_x, settled = lax.optimization_barrier((left_x, settled))
         own_rkv, own_up, own_gate_up, own_head, shared = run_slabs(
             last_sum_kernel,
             ids,
@@ -1126,41 +1155,38 @@
         shared = jnp.concatenate(
             [summed[edges[1] : edges[2]], summed[edges[4] : edges[5]], fix], axis=0
         )
-    shared, large, stream_came = lax.optimization_barrier((shared, large, stream_came))
-    shares = [shared] + [around(shared, by) for by in range(1, mp)]
-    out_rows = large[hidden_here + lots * part :].reshape(mp, width, part)
-    value_grad = large[:hidden_here].astype(f32)
-    key_grad = large[hidden_here : hidden_here + lots * part].reshape(lots, part, part)
-    key_grad = key_grad.transpose(1, 0, 2).reshape(part, lots * part).astype(f32)
-    out_grad = scatter_shares(out_rows)
+        settled = settle(large)
+    value_grad, key_grad, out_grad = settled
     input_grad = lax.dynamic_slice_in_dim(cot, share_at, share, 0) + sum(
         x.astype(f32) for x in stream_came
     )
-    everywhere = run_slabs(
-        functools.partial(share_sum_kernel, mp),
+    down_grad, gate_down_grad, feature_out, input_grad = run_slabs(
+        functools.partial(share_sum_kernel, mp, part),
         ids,
-        [(x, None) for x in shares],
-        [(shared.shape, f32, None)],
+        [(x, None) for x in [shared] + [around(shared, by) for by in range(1, mp)]]
+        + [(input_grad, None)],
+        [
+            ((2, rank, part), f32, None),
+            ((part, gate_rank), f32, None),
+            ((EDGE, part), f32, None),
+            ((share, features), f32, None),
+        ],
         [(mp,) + shared.shape],
         1,
-    )[0]
-    down_sum = everywhere[:part]
-    fix = everywhere[part + EDGE : part + EDGE + fix_rows].reshape(1, features)
-    last = lax.broadcasted_iota(jnp.int32, (share, 1), 0) == share - 1
-    input_grad = input_grad + jnp.where(last & (mp_here == mp - 1), fix, 0.0)
+    )
     return (
         block_out[None],
         input_grad[None],
         own_rkv.reshape(3, part, width),
         out_grad,
-        jnp.stack([down_sum[:, :rank], down_sum[:, rank : 2 * rank]]),
+        down_grad.transpose(0, 2, 1),
         own_up.reshape(2, up_rows, width),
-        down_sum[:, 2 * rank : low_width],
+        gate_down_grad,
         own_gate_up,
         key_grad,
         value_grad,
         own_head[:7, : heads * head_part].reshape(7, heads, head_part),
-        everywhere[part : part + 11, :part],
+        feature_out[:11],
     )
 
 

time: 332 us -> 329 us (level)
  starting transfers between devices: 83.6 us -> 98 us
  waiting for transfers between devices: 61.8 us -> 49.8 us
  local copies, waits for them, and re-layouts: 34.1 us -> 28.1 us
    ppermute x21, starting transfers between devices: 44.4 us -> 63.1 us  [around(): lax.ppermute(x, 'mp', [(i, (i + by) % devices) for i in range(devices)])]
    ppermute x21, waiting for transfers between devices: 33.8 us -> 20.5 us  [around(): lax.ppermute(x, 'mp', [(i, (i + by) % devices) for i in range(devices)])]
    ppermute x3, waiting for transfers between devices: 4.3 us -> 0.08 us  [body(): lax.ppermute(x, 'dp', [(i, i ^ bit) for i in range(4)])]
    unnamed x98 -> x89, local copies, waits for them, and re-layouts: 14.4 us -> 12.3 us
  transfers between devices with their start and end apart: 42 -> 42, of which waited for: 20 -> 15; matrix products, arithmetic and copies ran while one was open for 10% -> 11% of each run, Pallas kernels for 25% -> 25%
where the time goes in v5:
time: 329 us; the launch traced here: 327 us
  Pallas kernels  116 us (35%)
  starting transfers between devices  98 us (30%)
  waiting for transfers between devices  49.8 us (15%)
  local copies, waits for them, and re-layouts  28.1 us (9%)
  other arithmetic  18.5 us (6%)
  between operations  15.8 us (5%)
    pallas_call x8, Pallas kernels, run_slabs(): pl.pallas_call(kernel, grid_spec=pltpu.PrefetchScalarGridSpec(num_scalar_...  64.7 us
    ppermute x21, starting transfers between devices, around(): lax.ppermute(x, 'mp', [(i, (i + by) % devices) for i in range(devices)])  63.1 us
    pallas_call x4, Pallas kernels, run_blocks(): pl.pallas_call(functools.partial(kernel, per), grid=(steps,), in_specs=[s...  51.6 us
    ppermute x8, starting transfers between devices, slanted(): return lax.ppermute(x, ('seq', 'mp'), pairs_here)  24 us
    ppermute x21, waiting for transfers between devices, around(): lax.ppermute(x, 'mp', [(i, (i + by) % devices) for i in range(devices)])  20.5 us
    unnamed x89, local copies, waits for them, and re-layouts  12.3 us
    ppermute x4, starting transfers between devices, to_next(): return lax.ppermute(x, axis, pairs_here)  9.49 us
    ppermute x4, waiting for transfers between devices, to_next(): return lax.ppermute(x, axis, pairs_here)  9.48 us
  transfers between devices with their start and end apart: 42, of which 15 were waited for; matrix products, arithmetic and copies ran while one was open for 11% of the time, Pallas kernels for 25%

profile of v5, /device:TPU:0, one launch (start us, length us, event | category | flops | bytes accessed | tf_op | source)
XLA Modules:
  0.0 326.7 jit_solution(6897440328186344514)
XLA Ops:
  13.9 5.1 %collective-permute-start.1 = (bf16[256,128]{1,0:T(8,128)(2,1)}, bf16[256,128]{1,0:T(8,128)(2,1)S(1)}, u32[]{:S(2)}, u32[]{:S(2)}) collective-permute-start(bf16[256,128]{1,0:T(8,128)(2,1)} %param.14), channel_id=1, source_target_pairs={{0,3},{1,0},{2,1},{3,2},{4,7},{5,4},{6,5},{7,6},{8,11},{9,8},{10,9... | collective-permute-start | bytes 196616 | tf_op jit(solution)/shard_map/ppermute | solution.py:787
  21.8 3.9 %collective-permute-done.2 = bf16[256,128]{1,0:T(8,128)(2,1)S(1)} collective-permute-done((bf16[256,128]{1,0:T(8,128)(2,1)}, bf16[256,128]{1,0:T(8,128)(2,1)S(1)}, u32[]{:S(2)}, u32[]{:S(2)}) %collective-permute-start.2) | collective-permute-done | bytes 65568 | tf_op jit(solution)/shard_map/ppermute | solution.py:787
  27.6 3.4 %collective-permute-start = (f32[16,1024]{1,0:T(8,128)S(1)}, f32[16,1024]{1,0:T(8,128)S(1)}, u32[]{:S(2)}, u32[]{:S(2)}) collective-permute-start(f32[16,1024]{1,0:T(8,128)S(1)} %slice_bitcast_fusion.1), channel_id=1, source_target_pairs={{0,4},{1,5},{2,6},{3,7},{8,12},{9,13},{10,14},{11,15},{16,20},{17,... | collective-permute-start | bytes 196616 | tf_op jit(solution)/shard_map/ppermute | solution.py:782
  31.8 1.6 subtract_multiply_fusion.unit
  37.3 8.7 %all-gather.8.cloned.1.call-done = bf16[4608,256]{1,0:T(8,128)(2,1)} async-done(((bf16[576,256]{1,0:T(8,128)(2,1)}), bf16[4608,256]{1,0:T(8,128)(2,1)}) %all-gather.8.cloned.1.call-update) | async-done | bytes 2359312 | tf_op jit(solution)/shard_map/all_gather | solution.py:882
  50.6 8.6 %shard_map.211 = (f32[512,256]{1,0:T(8,128)}, f32[512,256]{1,0:T(8,128)}, f32[512,256]{1,0:T(8,128)}, f32[512,256]{1,0:T(8,128)}, f32[512,256]{1,0:T(8,128)}, /*index=5*/f32[512,256]{1,0:T(8,128)}, f32[512,256]{1,0:T(8,128)}) custom-call(s32[4]{0:T(128)} %pad_add_fusion.ids.here, f32[512,1024]{1,0:T(8,128)} %subtract_multiply_fusion.unit, ...), custom_call_target="tpu_custom_call" | custom-call | flops 10000000000 | bytes 20000000 | tf_op jit(solution)/shard_map/pallas_call | solution.py:707
  59.1 22.0 %shard_map.212 = (f32[512,256]{1,0:T(8,128)}, f32[512,256]{1,0:T(8,128)}, f32[512,256]{1,0:T(8,128)}, f32[512,256]{1,0:T(8,128)}, bf16[512,256]{1,0:T(8,128)(2,1...) custom-call(f32[512,256]{1,0:T(8,128)} %get-tuple-element.108.q, ...), custom_call_target="tpu_custom_call" | custom-call | flops 10000000000 | bytes 20000000 | tf_op jit(solution)/shard_map/pallas_call | solution.py:405
  82.0 3.3 %collective-permute-start.4 = (bf16[64,256]{1,0:T(8,128)(2,1)S(1)}, bf16[64,256]{1,0:T(8,128)(2,1)S(1)}, u32[]{:S(2)}, u32[]{:S(2)}) collective-permute-start(bf16[64,256]{1,0:T(8,128)(2,1)S(1)} %convert_element_type.106), channel_id=1, source_target_pairs={{0,4},{1,5},{2,6},{3,7},{8,12},{9,13},{10,14},{11,15},{16,20},{17,... | collective-permute-start | bytes 98312 | tf_op jit(solution)/shard_map/ppermute | solution.py:782
  85.2 1.6 collective-permute-done.4
  87.4 7.4 %shard_map.213 = (bf16[512,256]{1,0:T(8,128)(2,1)}, f32[512,256]{1,0:T(8,128)}, f32[512,256]{1,0:T(8,128)}, f32[512,256]{1,0:T(8,128)}, f32[512,256]{1,0:T(8,128)}) custom-call(f32[512,256]{1,0:T(8,128)} %get-tuple-element.108.q, f32[512,256]{1,0:T(8,128)} %get-tuple-element.109.kp, f32[512,256]{1,0:T(8,128)} %get-tuple-element.110.v, ...), custom_call_target="tpu_custom_call" | custom-call | flops 10000000000 | bytes 20000000 | tf_op jit(solution)/shard_map/pallas_call | solution.py:405
  94.8 1.5 collective-permute-start.5
  96.3 2.4 collective-permute-start.6
  98.8 1.4 collective-permute-start.7
  100.9 4.2 %collective-permute-start.10 = (bf16[16,256]{1,0:T(8,128)(2,1)S(1)}, bf16[16,256]{1,0:T(8,128)(2,1)S(1)}, u32[]{:S(2)}, u32[]{:S(2)}) collective-permute-start(bf16[16,256]{1,0:T(8,128)(2,1)S(1)} %slice.78), channel_id=1, source_target_pairs={{0,6},{1,7},{2,4},{3,5},{8,14},{9,15},{10,12},{11,13},{16,22},{17,... | collective-permute-start | bytes 24584 | tf_op jit(solution)/shard_map/ppermute | solution.py:798
  106.4 2.5 fusion.2
  111.7 1.5 collective-permute-done.10.refs_14_.refs_11_
  113.2 12.0 %collective-permute-start.8 = (bf16[16,256]{1,0:T(8,128)(2,1)S(1)}, bf16[16,256]{1,0:T(8,128)(2,1)S(1)}, u32[]{:S(2)}, u32[]{:S(2)}) collective-permute-start(bf16[16,256]{1,0:T(8,128)(2,1)S(1)} %slice.78), channel_id=1, source_target_pairs={{0,4},{1,5},{2,6},{3,7},{8,12},{9,13},{10,14},{11,15},{16,20},{17,... | collective-permute-start | bytes 24584 | tf_op jit(solution)/shard_map/ppermute | solution.py:798
  125.2 1.5 collective-permute-start.9
  126.7 3.2 copy_bitcast_fusion
  130.9 19.9 %shard_map.214 = (bf16[512,1024]{1,0:T(8,128)(2,1)}, bf16[512,1024]{1,0:T(8,128)(2,1)}, bf16[512,1024]{1,0:T(8,128)(2,1)}, bf16[512,1024]{1,0:T(8,128)(2,1)}, bf...) custom-call(s32[4]{0:T(128)} %pad_add_fusion.ids.here, ...), custom_call_target="tpu_custom_call" | custom-call | flops 10000000000 | bytes 20000000 | tf_op jit(solution)/shard_map/pallas_call | solution.py:707
  150.8 12.6 %shard_map.219 = bf16[8,3072,128]{2,1,0:T(8,128)(2,1)} custom-call(s32[4]{0:T(128)} %pad_add_fusion.ids.here, bf16[512,1024]{1,0:T(8,128)(2,1)} %get-tuple-element.172.refs_0_, bf16[512,1024]{1,0:T(8,128)(2,1)} %get-tuple-element.173.refs_1_, bf16[512,1024]{1,0:T(8,128)(2,1)} %get-tuple-element.174.refs_2_, bf16[512,1024]{1,0:T(8,128)(2,1)} %get-tuple-element.175.refs_3_, ...), custom_call_target="tpu_custom_call" | custom-call | flops 10000000000 | bytes 20000000 | tf_op jit(solution)/shard_map/pallas_call | solution.py:707
  164.4 3.8 %collective-permute-start.13 = (bf16[512,256]{1,0:T(8,128)(2,1)S(1)}, bf16[512,256]{1,0:T(8,128)(2,1)S(1)}, u32[]{:S(2)}, u32[]{:S(2)}) collective-permute-start(bf16[512,256]{1,0:T(8,128)(2,1)S(1)} %copy-done.15), channel_id=1, source_target_pairs={{0,2},{1,3},{2,0},{3,1},{4,6},{5,7},{6,4},{7,5},{8,10},{9,11},{10,... | collective-permute-start | bytes 786440 | tf_op jit(solution)/shard_map/ppermute | solution.py:787
  171.4 4.0 %collective-permute-done.12.refs_1_ = bf16[512,256]{1,0:T(8,128)(2,1)S(1)} collective-permute-done((bf16[512,256]{1,0:T(8,128)(2,1)S(1)}, bf16[512,256]{1,0:T(8,128)(2,1)S(1)}, u32[]{:S(2)}, u32[]{:S(2)}) %collective-permute-start.12) | collective-permute-done | bytes 262176 | tf_op jit(solution)/shard_map/ppermute | solution.py:787
  176.7 8.3 %collective-permute-done.13.refs_2_ = bf16[512,256]{1,0:T(8,128)(2,1)S(1)} collective-permute-done((bf16[512,256]{1,0:T(8,128)(2,1)S(1)}, bf16[512,256]{1,0:T(8,128)(2,1)S(1)}, u32[]{:S(2)}, u32[]{:S(2)}) %collective-permute-start.13) | collective-permute-done | bytes 262176 | tf_op jit(solution)/shard_map/ppermute | solution.py:787
  186.8 5.0 %collective-permute-done.20.refs_6_ = bf16[16,256]{1,0:T(8,128)(2,1)S(1)} collective-permute-done((bf16[16,256]{1,0:T(8,128)(2,1)S(1)}, bf16[16,256]{1,0:T(8,128)(2,1)S(1)}, u32[]{:S(2)}, u32[]{:S(2)}) %collective-permute-start.20) | collective-permute-done | bytes 8224 | tf_op jit(solution)/shard_map/ppermute | solution.py:798
  192.4 7.2 %shard_map.215 = (f32[512,256]{1,0:T(8,128)}, f32[512,256]{1,0:T(8,128)}, f32[512,256]{1,0:T(8,128)}, f32[512,256]{1,0:T(8,128)}, bf16[512,256]{1,0:T(8,128)(2,1...) custom-call(f32[512,256]{1,0:T(8,128)} %get-tuple-element.108.q, ...), custom_call_target="tpu_custom_call" | custom-call | flops 10000000000 | bytes 20000000 | tf_op jit(solution)/shard_map/pallas_call | solution.py:405
  200.4 1.5 collective-permute-start.22
  202.8 3.7 %collective-permute-done.22 = bf16[64,256]{1,0:T(8,128)(2,1)S(1)} collective-permute-done((bf16[64,256]{1,0:T(8,128)(2,1)S(1)}, bf16[64,256]{1,0:T(8,128)(2,1)S(1)}, u32[]{:S(2)}, u32[]{:S(2)}) %collective-permute-start.22) | collective-permute-done | bytes 32800 | tf_op jit(solution)/shard_map/ppermute | solution.py:782
  207.2 15.1 %shard_map.216 = (bf16[512,256]{1,0:T(8,128)(2,1)}, bf16[512,256]{1,0:T(8,128)(2,1)}, bf16[512,256]{1,0:T(8,128)(2,1)}, bf16[512,256]{1,0:T(8,128)(2,1)}, f32[8,256]{1,0:T(8,128)}, /*index=5*/f32[256,256]{1,0:T(8,128)}) custom-call(f32[512,256]{1,0:T(8,128)} %get-tuple-element.108.q, f32[512,256]{1,0:T(8,128)} %get-tuple-element.109.kp, ...), custom_call_target="tpu_custom_call" | custom-call | flops 10000000000 | bytes 20000000 | tf_op jit(solution)/shard_map/pallas_call | solution.py:405
  222.4 11.4 %shard_map.217 = (bf16[8,576,256]{2,1,0:T(8,128)(2,1)}, f32[16,1024]{1,0:T(8,128)}, f32[8,1024]{1,0:T(8,128)}, bf16[128,1024]{1,0:T(8,128)(2,1)}, bf16[128,1024]...) custom-call(s32[4]{0:T(128)} %pad_add_fusion.ids.here, f32[512,1024]{1,0:T(8,128)} %subtract_multiply_fusion.unit, ...), custom_call_target="tpu_custom_call" | custom-call | flops 10000000000 | bytes 20000000 | tf_op jit(solution)/shard_map/pallas_call | solution.py:707
  233.8 1.4 slice.79
  235.3 1.6 collective-permute-start.15
  236.9 5.2 %collective-permute-start.16 = (bf16[128,1024]{1,0:T(8,128)(2,1)}, bf16[128,1024]{1,0:T(8,128)(2,1)S(1)}, u32[]{:S(2)}, u32[]{:S(2)}) collective-permute-start(bf16[128,1024]{1,0:T(8,128)(2,1)} %get-tuple-element.133), channel_id=1, source_target_pairs={{0,2},{1,3},{2,0},{3,1},{4,6},{5,7},{6,4},{7,5},{8,10},{9,11},{10,... | collective-permute-start | bytes 786440 | tf_op jit(solution)/shard_map/ppermute | solution.py:787
  244.2 4.2 %collective-permute-done.31 = bf16[1,1024]{1,0:T(2,128)(2,1)S(1)} collective-permute-done((bf16[1,1024]{1,0:T(2,128)(2,1)S(1)}, bf16[1,1024]{1,0:T(2,128)(2,1)S(1)}, u32[]{:S(2)}, u32[]{:S(2)}) %collective-permute-start.31) | collective-permute-done | bytes 2080 | tf_op jit(solution)/shard_map/ppermute | solution.py:782
  248.4 2.0 collective-permute-start.35
  251.0 7.0 %collective-permute-start.36 = (bf16[128,1024]{1,0:T(8,128)(2,1)}, bf16[128,1024]{1,0:T(8,128)(2,1)S(1)}, u32[]{:S(2)}, u32[]{:S(2)}) collective-permute-start(bf16[128,1024]{1,0:T(8,128)(2,1)} %get-tuple-element.191), channel_id=1, source_target_pairs={{0,2},{1,3},{2,0},{3,1},{4,6},{5,7},{6,4},{7,5},{8,10},{9,11},{10,... | collective-permute-start | bytes 786440 | tf_op jit(solution)/shard_map/ppermute | solution.py:787
  258.1 2.2 collective-permute-done.16
  261.2 3.6 %shard_map.218 = (bf16[2,288,256]{2,1,0:T(8,128)(2,1)}, bf16[2,288,256]{2,1,0:T(8,128)(2,1)}, f32[2,288,256]{2,1,0:T(8,128)}, f32[2,288,256]{2,1,0:T(8,128)}) custom-call(s32[4]{0:T(128)} %pad_add_fusion.ids.here, bf16[8,576,256]{2,1,0:T(8,128)(2,1)} %get-tuple-element.170.kept, bf16[4,576,256]{2,1,0:T(8,128)(2,1)} %collective-permute-done.23.came), custom_call_target="tpu_custom_call" | custom-call | flops 10000000000 | bytes 20000000 | tf_op jit(solution)/shard_map/pallas_call | solution.py:707
  265.3 2.0 fusion.3
  267.3 17.9 %collective-permute-start.26 = (bf16[256,128]{1,0:T(8,128)(2,1)S(1)}, bf16[256,128]{1,0:T(8,128)(2,1)S(1)}, u32[]{:S(2)}, u32[]{:S(2)}) collective-permute-start(bf16[256,128]{1,0:T(8,128)(2,1)S(1)} %get-tuple-element.211), channel_id=1, source_target_pairs={{0,1},{1,2},{2,3},{3,0},{4,5},{5,6},{6,7},{7,4},{8,9},{9,10},{10,1... | collective-permute-start | bytes 196616 | tf_op jit(solution)/shard_map/ppermute | solution.py:787
  285.2 5.6 %collective-permute-start.27 = (bf16[256,128]{1,0:T(8,128)(2,1)S(1)}, bf16[256,128]{1,0:T(8,128)(2,1)S(1)}, u32[]{:S(2)}, u32[]{:S(2)}) collective-permute-start(bf16[256,128]{1,0:T(8,128)(2,1)S(1)} %get-tuple-element.213), channel_id=1, source_target_pairs={{0,2},{1,3},{2,0},{3,1},{4,6},{5,7},{6,4},{7,5},{8,10},{9,11},{10,... | collective-permute-start | bytes 196616 | tf_op jit(solution)/shard_map/ppermute | solution.py:787
  290.8 3.4 %collective-permute-start.28 = (bf16[256,128]{1,0:T(8,128)(2,1)S(1)}, bf16[256,128]{1,0:T(8,128)(2,1)S(1)}, u32[]{:S(2)}, u32[]{:S(2)}) collective-permute-start(bf16[256,128]{1,0:T(8,128)(2,1)S(1)} %get-tuple-element.212), channel_id=1, source_target_pairs={{0,3},{1,0},{2,1},{3,2},{4,7},{5,4},{6,5},{7,6},{8,11},{9,8},{10,9... | collective-permute-start | bytes 196616 | tf_op jit(solution)/shard_map/ppermute | solution.py:787
  294.2 3.1 shard_map.220
  300.1 4.1 %collective-permute-done.29.came_y = bf16[288,256]{1,0:T(8,128)(2,1)S(1)} collective-permute-done((bf16[288,256]{1,0:T(8,128)(2,1)}, bf16[288,256]{1,0:T(8,128)(2,1)S(1)}, u32[]{:S(2)}, u32[]{:S(2)}) %collective-permute-start.29) | collective-permute-done | bytes 147488 | tf_op jit(solution)/shard_map/ppermute | solution.py:1101
  304.9 2.8 shard_map.221
  309.6 2.0 collective-permute-start.34
  311.5 2.0 bitcast_add_fusion.refs_4_
  317.3 2.8 shard_map.222
  (195 shorter events, 49.7 us)
Async XLA Ops:
  7.2 19.5 %copy-start.4 = (bf16[1024,128]{1,0:T(8,128)(2,1)S(1)}, bf16[1024,128]{1,0:T(8,128)(2,1)}, u32[]{:S(2)}) copy-start(bf16[1024,128]{1,0:T(8,128)(2,1)} %param.20) | copy-start | bytes 786436
  7.2 38.9 %all-gather.8.cloned.1.call-start = ((), (), s32[]{:S(2)}) async-start(), calls=%async_computation.3 | async-start | bytes 2654208 | tf_op jit(solution)/shard_map/all_gather | solution.py:882
  8.0 19.6 %copy-start = (f32[1,512,1024]{2,1,0:T(8,128)S(1)}, f32[1,512,1024]{2,1,0:T(8,128)}, u32[]{:S(2)}) copy-start(f32[1,512,1024]{2,1,0:T(8,128)} %param.12) | copy-start | bytes 6291460
  13.8 92.6 %all-gather.10.cloned.1.call-start = ((), (), s32[]{:S(2)}) async-start(), calls=%async_computation.4 | async-start | bytes 4718592 | tf_op jit(solution)/shard_map/all_gather | solution.py:899
  13.9 7.9 %collective-permute-start.1 = (bf16[256,128]{1,0:T(8,128)(2,1)}, bf16[256,128]{1,0:T(8,128)(2,1)S(1)}, u32[]{:S(2)}, u32[]{:S(2)}) collective-permute-start(bf16[256,128]{1,0:T(8,128)(2,1)} %param.14), channel_id=1, source_target_pairs={{0,3},{1,0},{2,1},{3,2},{4,7},{5,4},{6,5},{7,6},{8,11},{9,8},{10,9... | collective-permute-start | bytes 196616 | tf_op jit(solution)/shard_map/ppermute | solution.py:787
  19.0 6.7 %collective-permute-start.2 = (bf16[256,128]{1,0:T(8,128)(2,1)}, bf16[256,128]{1,0:T(8,128)(2,1)S(1)}, u32[]{:S(2)}, u32[]{:S(2)}) collective-permute-start(bf16[256,128]{1,0:T(8,128)(2,1)} %param.14), channel_id=1, source_target_pairs={{0,2},{1,3},{2,0},{3,1},{4,6},{5,7},{6,4},{7,5},{8,10},{9,11},{10,... | collective-permute-start | bytes 196616 | tf_op jit(solution)/shard_map/ppermute | solution.py:787
  19.0 6.7 %collective-permute-start.3 = (bf16[256,128]{1,0:T(8,128)(2,1)}, bf16[256,128]{1,0:T(8,128)(2,1)S(1)}, u32[]{:S(2)}, u32[]{:S(2)}) collective-permute-start(bf16[256,128]{1,0:T(8,128)(2,1)} %param.14), channel_id=1, source_target_pairs={{0,1},{1,2},{2,3},{3,0},{4,5},{5,6},{6,7},{7,4},{8,9},{9,10},{10,1... | collective-permute-start | bytes 196616 | tf_op jit(solution)/shard_map/ppermute | solution.py:787
  27.5 102.4 %all-gather.6.cloned.1.call-start = ((), (), s32[]{:S(2)}) async-start(), calls=%async_computation.1 | async-start | bytes 2359296 | tf_op jit(solution)/shard_map/all_gather | solution.py:903
  27.6 6.5 %collective-permute-start = (f32[16,1024]{1,0:T(8,128)S(1)}, f32[16,1024]{1,0:T(8,128)S(1)}, u32[]{:S(2)}, u32[]{:S(2)}) collective-permute-start(f32[16,1024]{1,0:T(8,128)S(1)} %slice_bitcast_fusion.1), channel_id=1, source_target_pairs={{0,4},{1,5},{2,6},{3,7},{8,12},{9,13},{10,14},{11,15},{16,20},{17,... | collective-permute-start | bytes 196616 | tf_op jit(solution)/shard_map/ppermute | solution.py:782
  31.0 234.2 %reduce-scatter.2.cloned.1.call-start = ((), (), s32[]{:S(2)}) async-start(), calls=%async_computation.2 | async-start | bytes 7077888 | tf_op jit(solution)/shard_map/reduce_scatter | solution.py:1018
  34.1 25.1 %copy-start.6 = (f32[16,1024]{1,0:T(8,128)}, f32[16,1024]{1,0:T(8,128)S(1)}, u32[]{:S(2)}) copy-start(f32[16,1024]{1,0:T(8,128)S(1)} %collective-permute-done.refs_1_) | copy-start | bytes 196612
  82.0 4.9 %collective-permute-start.4 = (bf16[64,256]{1,0:T(8,128)(2,1)S(1)}, bf16[64,256]{1,0:T(8,128)(2,1)S(1)}, u32[]{:S(2)}, u32[]{:S(2)}) collective-permute-start(bf16[64,256]{1,0:T(8,128)(2,1)S(1)} %convert_element_type.106), channel_id=1, source_target_pairs={{0,4},{1,5},{2,6},{3,7},{8,12},{9,13},{10,14},{11,15},{16,20},{17,... | collective-permute-start | bytes 98312 | tf_op jit(solution)/shard_map/ppermute | solution.py:782
  94.8 35.2 %collective-permute-start.5 = (bf16[512,256]{1,0:T(8,128)(2,1)}, bf16[512,256]{1,0:T(8,128)(2,1)S(1)}, u32[]{:S(2)}, u32[]{:S(2)}) collective-permute-start(bf16[512,256]{1,0:T(8,128)(2,1)} %get-tuple-element.121.refs_8_.refs_5_), channel_id=1, source_target_pairs={{0,1},{1,2},{2,3},{3,0},{4,5},{5,6},{6,7},{7,4},{8,9},{9,10},{10,1... | collective-permute-start | bytes 786440 | tf_op jit(solution)/shard_map/ppermute | solution.py:787
  96.3 33.7 %collective-permute-start.6 = (bf16[512,256]{1,0:T(8,128)(2,1)}, bf16[512,256]{1,0:T(8,128)(2,1)S(1)}, u32[]{:S(2)}, u32[]{:S(2)}) collective-permute-start(bf16[512,256]{1,0:T(8,128)(2,1)} %get-tuple-element.121.refs_8_.refs_5_), channel_id=1, source_target_pairs={{0,2},{1,3},{2,0},{3,1},{4,6},{5,7},{6,4},{7,5},{8,10},{9,11},{10,... | collective-permute-start | bytes 786440 | tf_op jit(solution)/shard_map/ppermute | solution.py:787
  98.8 31.3 %collective-permute-start.7 = (bf16[512,256]{1,0:T(8,128)(2,1)}, bf16[512,256]{1,0:T(8,128)(2,1)S(1)}, u32[]{:S(2)}, u32[]{:S(2)}) collective-permute-start(bf16[512,256]{1,0:T(8,128)(2,1)} %get-tuple-element.121.refs_8_.refs_5_), channel_id=1, source_target_pairs={{0,3},{1,0},{2,1},{3,2},{4,7},{5,4},{6,5},{7,6},{8,11},{9,8},{10,9... | collective-permute-start | bytes 786440 | tf_op jit(solution)/shard_map/ppermute | solution.py:787
  100.9 12.3 %collective-permute-start.10 = (bf16[16,256]{1,0:T(8,128)(2,1)S(1)}, bf16[16,256]{1,0:T(8,128)(2,1)S(1)}, u32[]{:S(2)}, u32[]{:S(2)}) collective-permute-start(bf16[16,256]{1,0:T(8,128)(2,1)S(1)} %slice.78), channel_id=1, source_target_pairs={{0,6},{1,7},{2,4},{3,5},{8,14},{9,15},{10,12},{11,13},{16,22},{17,... | collective-permute-start | bytes 24584 | tf_op jit(solution)/shard_map/ppermute | solution.py:798
  105.1 20.1 %collective-permute-start.11 = (bf16[16,256]{1,0:T(8,128)(2,1)S(1)}, bf16[16,256]{1,0:T(8,128)(2,1)S(1)}, u32[]{:S(2)}, u32[]{:S(2)}) collective-permute-start(bf16[16,256]{1,0:T(8,128)(2,1)S(1)} %slice.78), channel_id=1, source_target_pairs={{0,7},{1,4},{2,5},{3,6},{8,15},{9,12},{10,13},{11,14},{16,23},{17,... | collective-permute-start | bytes 24584 | tf_op jit(solution)/shard_map/ppermute | solution.py:798
  113.2 16.7 %collective-permute-start.8 = (bf16[16,256]{1,0:T(8,128)(2,1)S(1)}, bf16[16,256]{1,0:T(8,128)(2,1)S(1)}, u32[]{:S(2)}, u32[]{:S(2)}) collective-permute-start(bf16[16,256]{1,0:T(8,128)(2,1)S(1)} %slice.78), channel_id=1, source_target_pairs={{0,4},{1,5},{2,6},{3,7},{8,12},{9,13},{10,14},{11,15},{16,20},{17,... | collective-permute-start | bytes 24584 | tf_op jit(solution)/shard_map/ppermute | solution.py:798
  125.2 4.8 %collective-permute-start.9 = (bf16[16,256]{1,0:T(8,128)(2,1)S(1)}, bf16[16,256]{1,0:T(8,128)(2,1)S(1)}, u32[]{:S(2)}, u32[]{:S(2)}) collective-permute-start(bf16[16,256]{1,0:T(8,128)(2,1)S(1)} %slice.78), channel_id=1, source_target_pairs={{0,5},{1,6},{2,7},{3,4},{8,13},{9,14},{10,15},{11,12},{16,21},{17,... | collective-permute-start | bytes 24584 | tf_op jit(solution)/shard_map/ppermute | solution.py:798
  163.4 21.6 %copy-start.26 = (bf16[16,256]{1,0:T(8,128)(2,1)S(1)}, bf16[16,256]{1,0:T(8,128)(2,1)}, u32[]{:S(2)}) copy-start(bf16[16,256]{1,0:T(8,128)(2,1)} %get-tuple-element.145) | copy-start | bytes 24580
  164.3 11.1 %collective-permute-start.12 = (bf16[512,256]{1,0:T(8,128)(2,1)S(1)}, bf16[512,256]{1,0:T(8,128)(2,1)S(1)}, u32[]{:S(2)}, u32[]{:S(2)}) collective-permute-start(bf16[512,256]{1,0:T(8,128)(2,1)S(1)} %copy-done.18), channel_id=1, source_target_pairs={{0,1},{1,2},{2,3},{3,0},{4,5},{5,6},{6,7},{7,4},{8,9},{9,10},{10,1... | collective-permute-start | bytes 786440 | tf_op jit(solution)/shard_map/ppermute | solution.py:787
  164.4 20.7 %collective-permute-start.13 = (bf16[512,256]{1,0:T(8,128)(2,1)S(1)}, bf16[512,256]{1,0:T(8,128)(2,1)S(1)}, u32[]{:S(2)}, u32[]{:S(2)}) collective-permute-start(bf16[512,256]{1,0:T(8,128)(2,1)S(1)} %copy-done.15), channel_id=1, source_target_pairs={{0,2},{1,3},{2,0},{3,1},{4,6},{5,7},{6,4},{7,5},{8,10},{9,11},{10,... | collective-permute-start | bytes 786440 | tf_op jit(solution)/shard_map/ppermute | solution.py:787
  168.2 18.2 %collective-permute-start.14 = (bf16[512,256]{1,0:T(8,128)(2,1)S(1)}, bf16[512,256]{1,0:T(8,128)(2,1)S(1)}, u32[]{:S(2)}, u32[]{:S(2)}) collective-permute-start(bf16[512,256]{1,0:T(8,128)(2,1)S(1)} %copy-done.14), channel_id=1, source_target_pairs={{0,3},{1,0},{2,1},{3,2},{4,7},{5,4},{6,5},{7,6},{8,11},{9,8},{10,9... | collective-permute-start | bytes 786440 | tf_op jit(solution)/shard_map/ppermute | solution.py:787
  168.8 17.6 %collective-permute-start.18 = (bf16[16,256]{1,0:T(8,128)(2,1)S(1)}, bf16[16,256]{1,0:T(8,128)(2,1)S(1)}, u32[]{:S(2)}, u32[]{:S(2)}) collective-permute-start(bf16[16,256]{1,0:T(8,128)(2,1)S(1)} %copy-done.30), channel_id=1, source_target_pairs={{4,0},{5,1},{6,2},{7,3},{12,8},{13,9},{14,10},{15,11},{20,16},{21,... | collective-permute-start | bytes 24584 | tf_op jit(solution)/shard_map/ppermute | solution.py:798
  170.1 16.7 %collective-permute-start.19 = (bf16[16,256]{1,0:T(8,128)(2,1)S(1)}, bf16[16,256]{1,0:T(8,128)(2,1)S(1)}, u32[]{:S(2)}, u32[]{:S(2)}) collective-permute-start(bf16[16,256]{1,0:T(8,128)(2,1)S(1)} %copy-done.29), channel_id=1, source_target_pairs={{4,1},{5,2},{6,3},{7,0},{12,9},{13,10},{14,11},{15,8},{20,17},{21,... | collective-permute-start | bytes 24584 | tf_op jit(solution)/shard_map/ppermute | solution.py:798
  175.4 16.4 %collective-permute-start.20 = (bf16[16,256]{1,0:T(8,128)(2,1)S(1)}, bf16[16,256]{1,0:T(8,128)(2,1)S(1)}, u32[]{:S(2)}, u32[]{:S(2)}) collective-permute-start(bf16[16,256]{1,0:T(8,128)(2,1)S(1)} %copy-done.28), channel_id=1, source_target_pairs={{4,2},{5,3},{6,0},{7,1},{12,10},{13,11},{14,8},{15,9},{20,18},{21,... | collective-permute-start | bytes 24584 | tf_op jit(solution)/shard_map/ppermute | solution.py:798
  185.1 6.7 %collective-permute-start.21 = (bf16[16,256]{1,0:T(8,128)(2,1)S(1)}, bf16[16,256]{1,0:T(8,128)(2,1)S(1)}, u32[]{:S(2)}, u32[]{:S(2)}) collective-permute-start(bf16[16,256]{1,0:T(8,128)(2,1)S(1)} %copy-done.26), channel_id=1, source_target_pairs={{4,3},{5,0},{6,1},{7,2},{12,11},{13,8},{14,9},{15,10},{20,19},{21,... | collective-permute-start | bytes 24584 | tf_op jit(solution)/shard_map/ppermute | solution.py:798
  200.4 6.1 %collective-permute-start.22 = (bf16[64,256]{1,0:T(8,128)(2,1)S(1)}, bf16[64,256]{1,0:T(8,128)(2,1)S(1)}, u32[]{:S(2)}, u32[]{:S(2)}) collective-permute-start(bf16[64,256]{1,0:T(8,128)(2,1)S(1)} %convert_element_type.112), channel_id=1, source_target_pairs={{4,0},{5,1},{6,2},{7,3},{12,8},{13,9},{14,10},{15,11},{20,16},{21,... | collective-permute-start | bytes 98312 | tf_op jit(solution)/shard_map/ppermute | solution.py:782
  233.8 26.4 %copy-start.2 = (f32[128,1024]{1,0:T(8,128)S(1)}, f32[128,1024]{1,0:T(8,128)}, u32[]{:S(2)}) copy-start(f32[128,1024]{1,0:T(8,128)} %get-tuple-element.122) | copy-start | bytes 1572868
  233.8 26.4 %copy-start.5 = (bf16[128,1024]{1,0:T(8,128)(2,1)S(1)}, bf16[128,1024]{1,0:T(8,128)(2,1)}, u32[]{:S(2)}) copy-start(bf16[128,1024]{1,0:T(8,128)(2,1)} %get-tuple-element.131) | copy-start | bytes 786436
  235.3 26.0 %collective-permute-start.23 = (bf16[4,576,256]{2,1,0:T(8,128)(2,1)S(1)}, bf16[4,576,256]{2,1,0:T(8,128)(2,1)}, u32[]{:S(2)}, u32[]{:S(2)}) collective-permute-start(bf16[4,576,256]{2,1,0:T(8,128)(2,1)S(1)} %slice.79), channel_id=1, source_target_pairs={{0,8},{8,0},{16,24},{24,16},{1,9},{9,1},{17,25},{25,17},{2,10},{10... | collective-permute-start | bytes 3538952 | tf_op jit(solution)/shard_map/ppermute | solution.py:1100
  235.3 15.7 %collective-permute-start.15 = (bf16[128,1024]{1,0:T(8,128)(2,1)}, bf16[128,1024]{1,0:T(8,128)(2,1)S(1)}, u32[]{:S(2)}, u32[]{:S(2)}) collective-permute-start(bf16[128,1024]{1,0:T(8,128)(2,1)} %get-tuple-element.132), channel_id=1, source_target_pairs={{0,1},{1,2},{2,3},{3,0},{4,5},{5,6},{6,7},{7,4},{8,9},{9,10},{10,1... | collective-permute-start | bytes 786440 | tf_op jit(solution)/shard_map/ppermute | solution.py:787
  236.9 23.3 %collective-permute-start.16 = (bf16[128,1024]{1,0:T(8,128)(2,1)}, bf16[128,1024]{1,0:T(8,128)(2,1)S(1)}, u32[]{:S(2)}, u32[]{:S(2)}) collective-permute-start(bf16[128,1024]{1,0:T(8,128)(2,1)} %get-tuple-element.133), channel_id=1, source_target_pairs={{0,2},{1,3},{2,0},{3,1},{4,6},{5,7},{6,4},{7,5},{8,10},{9,11},{10,... | collective-permute-start | bytes 786440 | tf_op jit(solution)/shard_map/ppermute | solution.py:787
  242.1 18.1 %collective-permute-start.17 = (bf16[128,1024]{1,0:T(8,128)(2,1)S(1)}, bf16[128,1024]{1,0:T(8,128)(2,1)S(1)}, u32[]{:S(2)}, u32[]{:S(2)}) collective-permute-start(bf16[128,1024]{1,0:T(8,128)(2,1)S(1)} %copy-done.9), channel_id=1, source_target_pairs={{0,3},{1,0},{2,1},{3,2},{4,7},{5,4},{6,5},{7,6},{8,11},{9,8},{10,9... | collective-permute-start | bytes 786440 | tf_op jit(solution)/shard_map/ppermute | solution.py:787
  242.9 5.5 %collective-permute-start.31 = (bf16[1,1024]{1,0:T(2,128)(2,1)S(1)}, bf16[1,1024]{1,0:T(2,128)(2,1)S(1)}, u32[]{:S(2)}, u32[]{:S(2)}) collective-permute-start(bf16[1,1024]{1,0:T(2,128)(2,1)S(1)} %slice.105), channel_id=1, source_target_pairs={{4,0},{5,1},{6,2},{7,3},{12,8},{13,9},{14,10},{15,11},{20,16},{21,... | collective-permute-start | bytes 6152 | tf_op jit(solution)/shard_map/ppermute | solution.py:782
  248.4 61.2 %collective-permute-start.35 = (bf16[128,1024]{1,0:T(8,128)(2,1)}, bf16[128,1024]{1,0:T(8,128)(2,1)S(1)}, u32[]{:S(2)}, u32[]{:S(2)}) collective-permute-start(bf16[128,1024]{1,0:T(8,128)(2,1)} %get-tuple-element.190), channel_id=1, source_target_pairs={{0,1},{1,2},{2,3},{3,0},{4,5},{5,6},{6,7},{7,4},{8,9},{9,10},{10,1... | collective-permute-start | bytes 786440 | tf_op jit(solution)/shard_map/ppermute | solution.py:787
  251.0 60.5 %collective-permute-start.36 = (bf16[128,1024]{1,0:T(8,128)(2,1)}, bf16[128,1024]{1,0:T(8,128)(2,1)S(1)}, u32[]{:S(2)}, u32[]{:S(2)}) collective-permute-start(bf16[128,1024]{1,0:T(8,128)(2,1)} %get-tuple-element.191), channel_id=1, source_target_pairs={{0,2},{1,3},{2,0},{3,1},{4,6},{5,7},{6,4},{7,5},{8,10},{9,11},{10,... | collective-permute-start | bytes 786440 | tf_op jit(solution)/shard_map/ppermute | solution.py:787
  264.8 20.4 %collective-permute-start.24 = (bf16[2,288,256]{2,1,0:T(8,128)(2,1)}, bf16[2,288,256]{2,1,0:T(8,128)(2,1)S(1)}, u32[]{:S(2)}, u32[]{:S(2)}) collective-permute-start(bf16[2,288,256]{2,1,0:T(8,128)(2,1)} %get-tuple-element.179), channel_id=1, source_target_pairs={{0,16},{8,24},{16,0},{24,8},{1,17},{9,25},{17,1},{25,9},{2,18},{10... | collective-permute-start | bytes 884744 | tf_op jit(solution)/shard_map/ppermute | solution.py:1100
  265.3 25.5 %collective-permute-start.25 = (bf16[2,288,256]{2,1,0:T(8,128)(2,1)}, bf16[2,288,256]{2,1,0:T(8,128)(2,1)S(1)}, u32[]{:S(2)}, u32[]{:S(2)}) collective-permute-start(bf16[2,288,256]{2,1,0:T(8,128)(2,1)} %get-tuple-element.180), channel_id=1, source_target_pairs={{0,4},{4,0},{1,5},{5,1},{2,6},{6,2},{3,7},{7,3},{8,12},{12,8},{9,1... | collective-permute-start | bytes 884744 | tf_op jit(solution)/shard_map/ppermute | solution.py:1101
  267.3 30.9 %collective-permute-start.26 = (bf16[256,128]{1,0:T(8,128)(2,1)S(1)}, bf16[256,128]{1,0:T(8,128)(2,1)S(1)}, u32[]{:S(2)}, u32[]{:S(2)}) collective-permute-start(bf16[256,128]{1,0:T(8,128)(2,1)S(1)} %get-tuple-element.211), channel_id=1, source_target_pairs={{0,1},{1,2},{2,3},{3,0},{4,5},{5,6},{6,7},{7,4},{8,9},{9,10},{10,1... | collective-permute-start | bytes 196616 | tf_op jit(solution)/shard_map/ppermute | solution.py:787
  285.2 13.7 %collective-permute-start.27 = (bf16[256,128]{1,0:T(8,128)(2,1)S(1)}, bf16[256,128]{1,0:T(8,128)(2,1)S(1)}, u32[]{:S(2)}, u32[]{:S(2)}) collective-permute-start(bf16[256,128]{1,0:T(8,128)(2,1)S(1)} %get-tuple-element.213), channel_id=1, source_target_pairs={{0,2},{1,3},{2,0},{3,1},{4,6},{5,7},{6,4},{7,5},{8,10},{9,11},{10,... | collective-permute-start | bytes 196616 | tf_op jit(solution)/shard_map/ppermute | solution.py:787
  290.8 8.1 %collective-permute-start.28 = (bf16[256,128]{1,0:T(8,128)(2,1)S(1)}, bf16[256,128]{1,0:T(8,128)(2,1)S(1)}, u32[]{:S(2)}, u32[]{:S(2)}) collective-permute-start(bf16[256,128]{1,0:T(8,128)(2,1)S(1)} %get-tuple-element.212), channel_id=1, source_target_pairs={{0,3},{1,0},{2,1},{3,2},{4,7},{5,4},{6,5},{7,6},{8,11},{9,8},{10,9... | collective-permute-start | bytes 196616 | tf_op jit(solution)/shard_map/ppermute | solution.py:787
  298.1 13.4 %collective-permute-start.37 = (bf16[128,1024]{1,0:T(8,128)(2,1)S(1)}, bf16[128,1024]{1,0:T(8,128)(2,1)S(1)}, u32[]{:S(2)}, u32[]{:S(2)}) collective-permute-start(bf16[128,1024]{1,0:T(8,128)(2,1)S(1)} %copy-done.10), channel_id=1, source_target_pairs={{0,3},{1,0},{2,1},{3,2},{4,7},{5,4},{6,5},{7,6},{8,11},{9,8},{10,9... | collective-permute-start | bytes 786440 | tf_op jit(solution)/shard_map/ppermute | solution.py:787
  298.8 5.4 %collective-permute-start.29 = (bf16[288,256]{1,0:T(8,128)(2,1)}, bf16[288,256]{1,0:T(8,128)(2,1)S(1)}, u32[]{:S(2)}, u32[]{:S(2)}) collective-permute-start(bf16[288,256]{1,0:T(8,128)(2,1)} %get-tuple-element.185), channel_id=1, source_target_pairs={{0,4},{4,0},{1,5},{5,1},{2,6},{6,2},{3,7},{7,3},{8,12},{12,8},{9,1... | collective-permute-start | bytes 442376 | tf_op jit(solution)/shard_map/ppermute | solution.py:1101
  298.9 5.4 %collective-permute-start.30 = (bf16[288,256]{1,0:T(8,128)(2,1)}, bf16[288,256]{1,0:T(8,128)(2,1)S(1)}, u32[]{:S(2)}, u32[]{:S(2)}) collective-permute-start(bf16[288,256]{1,0:T(8,128)(2,1)} %get-tuple-element.186), channel_id=1, source_target_pairs={{0,16},{8,24},{16,0},{24,8},{1,17},{9,25},{17,1},{25,9},{2,18},{10... | collective-permute-start | bytes 442376 | tf_op jit(solution)/shard_map/ppermute | solution.py:1100
  307.7 7.2 %collective-permute-start.32 = (bf16[160,256]{1,0:T(8,128)(2,1)}, bf16[160,256]{1,0:T(8,128)(2,1)S(1)}, u32[]{:S(2)}, u32[]{:S(2)}) collective-permute-start(bf16[160,256]{1,0:T(8,128)(2,1)} %get-tuple-element.188.refs_0_), channel_id=1, source_target_pairs={{0,1},{1,2},{2,3},{3,0},{4,5},{5,6},{6,7},{7,4},{8,9},{9,10},{10,1... | collective-permute-start | bytes 245768 | tf_op jit(solution)/shard_map/ppermute | solution.py:787
  309.0 7.0 %collective-permute-start.33 = (bf16[160,256]{1,0:T(8,128)(2,1)}, bf16[160,256]{1,0:T(8,128)(2,1)S(1)}, u32[]{:S(2)}, u32[]{:S(2)}) collective-permute-start(bf16[160,256]{1,0:T(8,128)(2,1)} %get-tuple-element.188.refs_0_), channel_id=1, source_target_pairs={{0,2},{1,3},{2,0},{3,1},{4,6},{5,7},{6,4},{7,5},{8,10},{9,11},{10,... | collective-permute-start | bytes 245768 | tf_op jit(solution)/shard_map/ppermute | solution.py:787
  309.6 6.5 %collective-permute-start.34 = (bf16[160,256]{1,0:T(8,128)(2,1)}, bf16[160,256]{1,0:T(8,128)(2,1)S(1)}, u32[]{:S(2)}, u32[]{:S(2)}) collective-permute-start(bf16[160,256]{1,0:T(8,128)(2,1)} %get-tuple-element.188.refs_0_), channel_id=1, source_target_pairs={{0,3},{1,0},{2,1},{3,2},{4,7},{5,4},{6,5},{7,6},{8,11},{9,8},{10,9... | collective-permute-start | bytes 245768 | tf_op jit(solution)/shard_map/ppermute | solution.py:787
  (31 other events, 132.0 us)
Sparse Core Ops, SparseCore 0:
  13.9 32.0 all-gather.7
  48.5 36.5 all-gather.9
  87.0 27.9 all-gather.5
  163.6 61.3 reduce-scatter.1
